TPU v7x, 512 devices: a whole 4x8x8 slice. The times are simulated.
512 devices in a mesh: dp: 32 (over x, y), seq: 16 (over z, core).
Axes of the slice: x: 4, y: 8, z: 8, core: 2. Of those that a mesh axis runs over, the one named last changes fastest.
Arguments:
- mixer_input: bfloat16 [32, 2048, 2048], P('dp', 'seq'), may hold values from -5 to 5
- state_input: bfloat16 [32, 2048, 256], P('dp', 'seq'), may hold values from -1 to 1
- step_raw: float32 [32, 32, 2048], P('dp', None, 'seq'), may hold values from -5 to 6
- conv_weight: float32 [4, 2304], replicated, may hold values from -3 to 3
- conv_bias: float32 [2304], replicated, may hold values from -0.3 to 0.3
- step_bias: float32 [32], replicated, may hold values from -0.5 to 0.5
- log_rate: float32 [32], replicated, may hold values from -10 to -1
- skip_gain: float32 [32], replicated, may hold values from 0.25 to 1.75
- grad_out: bfloat16 [32, 2048, 2048], P('dp', 'seq'), may hold values from -6 to 6
Outputs:
- grad_mixer: bfloat16 [32, 2048, 2048], P('dp', 'seq')
- grad_state: bfloat16 [32, 2048, 256], P('dp', 'seq')
- grad_step: float32 [32, 32, 2048], P('dp', None, 'seq')
- grad_conv_weight: float32 [4, 2304], replicated
- grad_conv_bias: float32 [2304], replicated
- grad_step_bias: float32 [32], replicated
- grad_log_rate: float32 [32], replicated
- grad_skip_gain: float32 [32], replicated
All inputs are finite; a program needn't handle non-finite values.
Results may differ from a plain program's by a relative error of at most 0.013.
Values may be sent and summed in bfloat16 or wider, within the bound.
No kernel may reach another device: no remote copies, remote signals or barrier semaphores. Data moves between devices by JAX's collectives and lax.ppermute only.
A program may use at most 128 MiB of HBM per device.

v0:
```python
import jax
import jax.numpy as jnp
from jax import lax
from jax.sharding import PartitionSpec as P

highest = lax.Precision.HIGHEST


def from_behind(shard, axis, by):
    count = lax.axis_size(axis)
    pairs = [(i, i + by) for i in range(count) if 0 <= i + by < count]
    return lax.ppermute(shard, axis, pairs)


def entering(shard, axis, combine, identity, reverse):
    count, index = (lax.axis_size(axis), lax.axis_index(axis))
    everything = jax.tree.map(lambda part: lax.all_gather(part, axis), shard)
    start = jax.tree.map(
        lambda part, zero: jnp.broadcast_to(jnp.asarray(zero, part.dtype), part.shape),
        shard,
        identity,
    )

    def turn(k, before):
        at = count - 1 - k if reverse else k
        reached = at > index if reverse else at < index
        new = combine(before, jax.tree.map(lambda part: part[at], everything))
        return jax.tree.map(lambda a, b: jnp.where(reached, a, b), new, before)

    return lax.fori_loop(0, count, turn, start)


def convolve(padded, weight, offset):
    kernel_taps = weight.shape[0]
    row_count = padded.shape[0] - kernel_taps + 1
    wide = padded.astype(jnp.float32)
    summed = offset[None, :] + weight[0][None, :] * wide[0:row_count]
    for tap_index in range(1, kernel_taps):
        summed = summed + weight[tap_index][None, :] * wide[tap_index : tap_index + row_count]
    return jax.nn.silu(summed).astype(jnp.bfloat16)


def prepare(padded_x, padded_bc, step_block, conv_weight, conv_bias, step_bias, log_rate):
    inner_width = padded_x.shape[1]
    state_width = padded_bc.shape[1] // 2
    x_active = convolve(padded_x, conv_weight[:, :inner_width], conv_bias[:inner_width])
    bc_active = convolve(padded_bc, conv_weight[:, inner_width:], conv_bias[inner_width:])
    b_active = bc_active[:, :state_width]
    c_active = bc_active[:, state_width:]
    stride_durations = jax.nn.softplus(step_block + step_bias[:, None])
    log_decay = -jnp.exp(log_rate)[:, None] * stride_durations
    cumul = jnp.cumsum(log_decay, axis=1)
    return (x_active, b_active, c_active, stride_durations, cumul)


def end_state(x_active, b_active, stride_durations, cumul, head_count):
    row_count = x_active.shape[0]
    weights = jnp.exp(cumul[:, -1:] - cumul) * stride_durations
    scaled = (
        x_active.astype(jnp.float32).reshape(row_count, head_count, -1) * weights.T[:, :, None]
    ).astype(jnp.bfloat16)
    return jnp.einsum("shp,sn->hpn", scaled, b_active, preferred_element_type=jnp.float32)


def block_forward(
    padded_x,
    padded_bc,
    step_block,
    conv_weight,
    conv_bias,
    step_bias,
    log_rate,
    skip_gain,
    entry_state,
):
    head_count = step_block.shape[0]
    x_active, b_active, c_active, stride_durations, cumul = prepare(
        padded_x, padded_bc, step_block, conv_weight, conv_bias, step_bias, log_rate
    )
    row_count = x_active.shape[0]
    scores = jnp.dot(c_active, b_active.T, preferred_element_type=jnp.float32)
    causal = jnp.arange(row_count)[:, None] >= jnp.arange(row_count)[None, :]
    log_gap = jnp.where(causal[None], cumul[:, :, None] - cumul[:, None, :], -jnp.inf)
    mixing = (scores[None] * jnp.exp(log_gap) * stride_durations[:, None, :]).astype(jnp.bfloat16)
    x_heads = x_active.reshape(row_count, head_count, -1)
    inner_out = jnp.einsum("hts,shp->thp", mixing, x_heads, preferred_element_type=jnp.float32)
    carried = (
        jnp.einsum("tn,hpn->thp", c_active.astype(jnp.float32), entry_state, precision=highest)
        * jnp.exp(cumul).T[:, :, None]
    )
    output = inner_out + carried + skip_gain[None, :, None] * x_heads.astype(jnp.float32)
    finish = jnp.exp(cumul[:, -1])[:, None, None] * entry_state + end_state(
        x_active, b_active, stride_durations, cumul, head_count
    )
    return (output.reshape(row_count, -1), finish)


def combine_carries(earlier, later):
    return (earlier[0] + later[0], jnp.exp(later[0])[..., None, None] * earlier[1] + later[1])


def on_device(
    mixer_input,
    state_input,
    step_raw,
    conv_weight,
    conv_bias,
    step_bias,
    log_rate,
    skip_gain,
    grad_out,
):
    x_rows = mixer_input[0]
    bc_rows = state_input[0]
    step_rows = step_raw[0]
    kernel_taps = conv_weight.shape[0]
    rim_count = kernel_taps - 1
    head_count = step_rows.shape[0]
    row_count = x_rows.shape[0]
    rim_x, rim_bc = from_behind(
        (x_rows[row_count - rim_count :], bc_rows[row_count - rim_count :]), "seq", 1
    )
    padded_x = jnp.concatenate([rim_x, x_rows], 0)
    padded_bc = jnp.concatenate([rim_bc, bc_rows], 0)
    x_active, b_active, c_active, stride_durations, cumul = prepare(
        padded_x, padded_bc, step_rows, conv_weight, conv_bias, step_bias, log_rate
    )
    local_end = end_state(x_active, b_active, stride_durations, cumul, head_count)
    decay_total = cumul[:, -1]
    cotangent = grad_out[0].astype(jnp.float32)
    weighted = cotangent.reshape(row_count, head_count, -1) * jnp.exp(cumul).T[:, :, None]
    back_term = jnp.einsum("thp,tn->hpn", weighted, c_active.astype(jnp.float32), precision=highest)
    identity = (jnp.zeros_like(decay_total), jnp.zeros_like(local_end))
    entry_state = entering((decay_total, local_end), "seq", combine_carries, identity, False)[1]
    later_grads = entering((decay_total, back_term), "seq", combine_carries, identity, True)[1]

    def local_block(
        x_pad, bc_pad, step_block, weight_taps, bias_taps, bias_step, rate_log, gain_skip
    ):
        return block_forward(
            x_pad,
            bc_pad,
            step_block,
            weight_taps,
            bias_taps,
            bias_step,
            rate_log,
            gain_skip,
            entry_state,
        )

    outputs, pull_back = jax.vjp(
        local_block,
        padded_x,
        padded_bc,
        step_rows,
        conv_weight,
        conv_bias,
        step_bias,
        log_rate,
        skip_gain,
    )
    grad_px, grad_pbc, grad_steps, grad_cw, grad_cb, grad_sb, grad_lr, grad_sk = pull_back(
        (cotangent, later_grads)
    )
    back_x, back_bc = from_behind((grad_px[:rim_count], grad_pbc[:rim_count]), "seq", -1)
    grad_x_rows = grad_px[rim_count:].at[row_count - rim_count :].add(back_x)
    grad_bc_rows = grad_pbc[rim_count:].at[row_count - rim_count :].add(back_bc)
    packed = (grad_cw, grad_cb, grad_sb, grad_lr, grad_sk)
    summed_grads = lax.psum((packed[0], packed[1], packed[2], packed[3], packed[4]), ("dp", "seq"))
    records = lax.axis_size("dp")
    return (
        grad_x_rows[None],
        grad_bc_rows[None],
        grad_steps[None],
        summed_grads[0] / records,
        summed_grads[1] / records,
        summed_grads[2] / records,
        summed_grads[3] / records,
        summed_grads[4] / records,
    )


def solution(mesh):
    return jax.shard_map(
        on_device,
        mesh=mesh,
        in_specs=(
            P("dp", "seq", None),
            P("dp", "seq", None),
            P("dp", None, "seq"),
            P(),
            P(),
            P(),
            P(),
            P(),
            P("dp", "seq", None),
        ),
        out_specs=(
            P("dp", "seq", None),
            P("dp", "seq", None),
            P("dp", None, "seq"),
            P(),
            P(),
            P(),
            P(),
            P(),
        ),
        check_vma=False,
    )
```

profile of v0, /device:TPU:1, one launch (start us, length us, event | category | flops | bytes accessed | tf_op | source)
XLA Modules:
  0.0 410.6 jit_solution(3421446078782662908)
XLA Ops:
  7.9 5.4 %collective-permute-start = (bf16[3,256]{1,0:T(4,128)(2,1)S(1)}, bf16[3,256]{1,0:T(4,128)(2,1)S(1)}, u32[]{:S(2)}, u32[]{:S(2)}) collective-permute-start(bf16[3,256]{1,0:T(4,128)(2,1)S(1)} %slice_bitcast_fusion.3), channel_id=1, source_target_pairs={{0,1},{1,2},{2,3},{3,4},{4,5},{5,6},{6,7},{7,8},{8,9},{9,10},{10,1... | collective-permute-start | bytes 4616 | tf_op jit(solution)/shard_map/ppermute | solution.py:12
  21.2 1.6 fusion.12
  23.5 1.9 collective-permute-start.1
  28.0 28.8 %all-reduce.24 = f32[512]{0:T(512)S(1)} all-reduce(f32[512]{0:T(512)S(1)} %fusion.64), channel_id=2, replica_groups=mesh['dp'=32,'seq'=16] {'seq'}, use_global_device_ids=true, to_apply=%add.24 | all-reduce | flops 512 | bytes 4096
  58.6 4.1 fusion.27
  62.7 62.9 %all-gather.6.cloned.1.call-done = f32[512,64,128]{2,1,0:T(8,128)} async-done(((f32[32,64,128]{2,1,0:T(8,128)}), f32[512,64,128]{2,1,0:T(8,128)}) %all-gather.6.cloned.1.call-update) | async-done | bytes 16777232 | tf_op jit(solution)/shard_map/all_gather | solution.py:17
  125.7 24.2 %while.32 = (s32[]{:T(128)}, f32[32,64,128]{2,1,0:T(8,128)S(1)}, s32[]{:T(128)}, f32[16,32]{1,0:T(8,128)S(1)}, f32[16,32,64,128]{3,2,1,0:T(8,128)}, /*index=5*/s32[]{:T(128)}, s32[]{:T(128)}, s32[]{:T(128)}, s32[]{:T(128)}) while((s32[]{:T(128)}, f32[32,64,128]{2,1,0:T(8,128)S(1)}, s32[]{:T(128)}, f32[16,32]{1,0:T(8,128)S(1)}, ...), condition=%wide.region_2.3_spmd.clone, body=%wide.region_1.2_spmd.clone.sunk | while | flops 1048584 | bytes 3146287 | solution.py:30
  125.7 1.5 fusion.82
  127.2 1.5 fusion.82
  128.7 1.5 fusion.82
  130.2 1.5 fusion.82
  131.7 1.5 fusion.82
  133.2 1.5 fusion.82
  134.8 1.5 fusion.82
  136.3 1.5 fusion.82
  137.8 1.5 fusion.82
  139.3 1.5 fusion.82
  140.8 1.5 fusion.82
  142.3 1.5 fusion.82
  143.9 1.5 fusion.82
  145.4 1.5 fusion.82
  146.9 1.5 fusion.82
  148.4 1.5 fusion.82
  149.9 1.7 fusion.23
  152.4 1.9 fusion.62
  154.3 1.5 copy.69
  155.8 2.0 fusion.37
  162.0 1.5 copy.70
  163.5 2.3 fusion.16
  165.9 3.0 multiply_reduce_fusion.3
  170.2 1.7 add_convert_fusion
  172.8 2.4 collective-permute-start.2
  175.5 2.6 fusion.10
  184.9 10.3 %collective-permute-done.2 = bf16[3,2048]{0,1:T(8,128)(2,1)} collective-permute-done((bf16[3,2048]{0,1:T(8,128)(2,1)}, bf16[3,2048]{0,1:T(8,128)(2,1)}, u32[]{:S(2)}, u32[]{:S(2)}) %collective-permute-start.2) | collective-permute-done | bytes 12320 | tf_op jit(solution)/shard_map/ppermute | solution.py:12
  196.5 5.8 %scatter-add.6 = bf16[1,128,2048]{1,2,0:T(8,128)(2,1)} dynamic-update-slice(bf16[1,128,2048]{1,2,0:T(8,128)(2,1)} %slice_bitcast_fusion, bf16[1,3,2048]{1,2,0:T(8,128)(2,1)S(1)} %fusion.34, s32[]{:T(128)} %constant.154.clone.1, s32[]{:T(128)} %constant.158.clone.1, s32[]{:T(128)} %constant.154.clone.1) | dynamic-update-slice | bytes 24580 | tf_op jit(solution)/shard_map/scatter-add | solution.py:167
  202.3 2.0 copy.82
  204.3 53.5 %all-gather.8.cloned.1.call-done = f32[512,64,128]{2,1,0:T(8,128)} async-done(((f32[32,64,128]{2,1,0:T(8,128)}), f32[512,64,128]{2,1,0:T(8,128)}) %all-gather.8.cloned.1.call-update) | async-done | bytes 16777232 | tf_op jit(solution)/shard_map/all_gather | solution.py:17
  257.8 34.8 %while.33 = (s32[]{:T(128)}, f32[32,64,128]{2,1,0:T(8,128)S(1)}, s32[]{:T(128)}, f32[16,32]{1,0:T(8,128)}, f32[16,32,64,128]{3,2,1,0:T(8,128)}, /*index=5*/s32[]{:T(128)}, s32[]{:T(128)}) while((s32[]{:T(128)}, f32[32,64,128]{2,1,0:T(8,128)S(1)}, s32[]{:T(128)}, f32[16,32]{1,0:T(8,128)}, f32[16,32,64,128]{3,2,1,0:T(8,128)}, ...), condition=%wide.region_4.5_spmd.clone, body=%wide.region_3.4_spmd.clone.sunk | while | flops 1048580 | bytes 3146225 | solution.py:30
  260.6 1.5 fusion.83
  262.8 1.5 fusion.83
  269.3 1.5 fusion.83
  271.5 1.5 fusion.83
  273.7 1.5 fusion.83
  275.9 1.5 fusion.83
  278.0 1.5 fusion.83
  293.7 1.8 fusion.19
  297.9 98.7 %all-reduce.25 = (f32[4,2304]{1,0:T(4,128)S(1)}, f32[2304]{0:T(1024)S(1)}, f32[32]{0:T(128)S(1)}, f32[32]{0:T(128)S(1)}, f32[32]{0:T(128)S(1)}) all-reduce(f32[4,2304]{1,0:T(4,128)S(1)} %pad_add_fusion, f32[2304]{0:T(1024)S(1)} %pad_add_fusion.2, f32[32]{0:T(128)S(1)} %get-tuple-element.378, ...), channel_id=1, replica_groups=mesh['dp'=32,'seq'=16] {'dp','seq'}, use_global_device_ids=true, to_apply=%region_22.23 | all-reduce | flops 11616 | bytes 92928 | tf_op jit(solution)/shard_map/psum | solution.py:170
  397.9 2.6 collective-permute-start.3
  (213 shorter events, 60.3 us)
Async XLA Ops:
  7.2 118.5 %all-gather.6.cloned.1.call-start = ((), (), s32[]{:S(2)}) async-start(), calls=%async_computation | async-start | bytes 17825792 | tf_op jit(solution)/shard_map/all_gather | solution.py:17
  7.9 11.7 %collective-permute-start = (bf16[3,256]{1,0:T(4,128)(2,1)S(1)}, bf16[3,256]{1,0:T(4,128)(2,1)S(1)}, u32[]{:S(2)}, u32[]{:S(2)}) collective-permute-start(bf16[3,256]{1,0:T(4,128)(2,1)S(1)} %slice_bitcast_fusion.3), channel_id=1, source_target_pairs={{0,1},{1,2},{2,3},{3,4},{4,5},{5,6},{6,7},{7,8},{8,9},{9,10},{10,1... | collective-permute-start | bytes 4616 | tf_op jit(solution)/shard_map/ppermute | solution.py:12
  17.4 5.4 %copy-start.32 = (f32[1,256]{1,0:T(1,128)}, f32[1,256]{1,0:T(1,128)S(1)}, u32[]{:S(2)}) copy-start(f32[1,256]{1,0:T(1,128)S(1)} %get-tuple-element.398) | copy-start | bytes 3076
  17.4 5.4 %copy-start.34 = (f32[1,256]{1,0:T(1,128)}, f32[1,256]{1,0:T(1,128)S(1)}, u32[]{:S(2)}) copy-start(f32[1,256]{1,0:T(1,128)S(1)} %get-tuple-element.399) | copy-start | bytes 3076
  17.4 5.4 %copy-start.36 = (f32[1,256]{1,0:T(1,128)}, f32[1,256]{1,0:T(1,128)S(1)}, u32[]{:S(2)}) copy-start(f32[1,256]{1,0:T(1,128)S(1)} %get-tuple-element.400) | copy-start | bytes 3076
  17.4 5.4 %copy-start.38 = (f32[1,256]{1,0:T(1,128)}, f32[1,256]{1,0:T(1,128)S(1)}, u32[]{:S(2)}) copy-start(f32[1,256]{1,0:T(1,128)S(1)} %get-tuple-element.401) | copy-start | bytes 3076
  18.2 4.7 %copy-start.11 = (f32[128,32]{0,1:T(8,128)}, f32[128,32]{0,1:T(8,128)S(1)}, u32[]{:S(2)}) copy-start(f32[128,32]{0,1:T(8,128)S(1)} %copy.67) | copy-start | bytes 49156
  18.2 4.8 %copy-start.6 = (bf16[1,128,2048]{2,1,0:T(8,128)(2,1)S(1)}, bf16[1,128,2048]{2,1,0:T(8,128)(2,1)}, u32[]{:S(2)}) copy-start(bf16[1,128,2048]{2,1,0:T(8,128)(2,1)} %param.17) | copy-start | bytes 1572868
  21.2 6.6 %copy-start.28 = (f32[4,2304]{1,0:T(4,128)S(1)}, f32[4,2304]{1,0:T(4,128)}, u32[]{:S(2)}) copy-start(f32[4,2304]{1,0:T(4,128)} %param.20) | copy-start | bytes 110596
  21.2 6.8 %copy-start.42 = (f32[2304]{0:T(1024)S(1)}, f32[2304]{0:T(1024)}, u32[]{:S(2)}) copy-start(f32[2304]{0:T(1024)} %param.21) | copy-start | bytes 27652
  22.9 234.9 %all-gather.8.cloned.1.call-start = ((), (), s32[]{:S(2)}) async-start(), calls=%async_computation.1 | async-start | bytes 17825792 | tf_op jit(solution)/shard_map/all_gather | solution.py:17
  23.5 33.4 %collective-permute-start.1 = (bf16[3,2048]{0,1:T(8,128)(2,1)S(1)}, bf16[3,2048]{0,1:T(8,128)(2,1)S(1)}, u32[]{:S(2)}, u32[]{:S(2)}) collective-permute-start(bf16[3,2048]{0,1:T(8,128)(2,1)S(1)} %slice_bitcast_fusion.1), channel_id=1, source_target_pairs={{0,1},{1,2},{2,3},{3,4},{4,5},{5,6},{6,7},{7,8},{8,9},{9,10},{10,1... | collective-permute-start | bytes 36872 | tf_op jit(solution)/shard_map/ppermute | solution.py:12
  27.9 34.9 %copy-start.18 = (f32[1,2048]{1,0:T(1,128)}, f32[1,2048]{1,0:T(1,128)S(1)}, u32[]{:S(2)}) copy-start(f32[1,2048]{1,0:T(1,128)S(1)} %get-tuple-element.403) | copy-start | bytes 24580
  27.9 34.9 %copy-start.20 = (f32[1,2048]{1,0:T(1,128)}, f32[1,2048]{1,0:T(1,128)S(1)}, u32[]{:S(2)}) copy-start(f32[1,2048]{1,0:T(1,128)S(1)} %get-tuple-element.404) | copy-start | bytes 24580
  27.9 34.9 %copy-start.22 = (f32[1,2048]{1,0:T(1,128)}, f32[1,2048]{1,0:T(1,128)S(1)}, u32[]{:S(2)}) copy-start(f32[1,2048]{1,0:T(1,128)S(1)} %get-tuple-element.405) | copy-start | bytes 24580
  151.6 6.2 %copy-start.2 = (f32[128,2048]{0,1:T(8,128)}, f32[128,2048]{0,1:T(8,128)S(1)}, u32[]{:S(2)}) copy-start(f32[128,2048]{0,1:T(8,128)S(1)} %get-tuple-element.383) | copy-start | bytes 3145732
  163.5 2.4 copy-start.1
  163.5 2.4 copy-start.5
  165.9 3.0 copy-start.19
  165.9 3.0 copy-start.21
  165.9 3.0 copy-start.23
  170.2 5.0 %copy-start.3 = (f32[128,2048]{0,1:T(8,128)S(1)}, f32[128,2048]{0,1:T(8,128)}, u32[]{:S(2)}) copy-start(f32[128,2048]{0,1:T(8,128)} %copy-done.2) | copy-start | bytes 3145732
  170.2 5.0 %copy-start.13 = (f32[128,32]{0,1:T(8,128)S(1)}, f32[128,32]{0,1:T(8,128)}, u32[]{:S(2)}) copy-start(f32[128,32]{0,1:T(8,128)} %copy.69) | copy-start | bytes 49156
  171.9 7.1 %copy-start.4 = (bf16[131,2048]{0,1:T(8,128)(2,1)}, bf16[131,2048]{0,1:T(8,128)(2,1)S(1)}, u32[]{:S(2)}) copy-start(bf16[131,2048]{0,1:T(8,128)(2,1)S(1)} %add_convert_fusion) | copy-start | bytes 1609732
  171.9 3.6 copy-start.25
  171.9 3.6 copy-start.26
  171.9 3.6 copy-start.30
  171.9 3.6 copy-start.31
  172.8 22.5 %collective-permute-start.2 = (bf16[3,2048]{0,1:T(8,128)(2,1)}, bf16[3,2048]{0,1:T(8,128)(2,1)}, u32[]{:S(2)}, u32[]{:S(2)}) collective-permute-start(bf16[3,2048]{0,1:T(8,128)(2,1)} %slice.207), channel_id=1, source_target_pairs={{1,0},{2,1},{3,2},{4,3},{5,4},{6,5},{7,6},{8,7},{9,8},{10,9},{11,1... | collective-permute-start | bytes 36872 | tf_op jit(solution)/shard_map/ppermute | solution.py:12
  292.9 2.6 copy-start.16
  292.9 2.8 copy-start.7
  292.9 2.8 copy-start.17
  292.9 3.0 copy-start.33
  292.9 3.0 copy-start.35
  292.9 3.0 copy-start.37
  292.9 3.0 copy-start.39
  293.6 2.5 copy-start.8
  293.6 2.5 copy-start.9
  293.6 2.5 copy-start.40
  293.6 2.5 copy-start.43
  293.6 2.5 copy-start.46
  295.5 2.2 copy-start.10
  295.5 2.2 copy-start.45
  295.5 2.3 copy-start.48
  295.5 2.3 copy-start.14
  295.5 2.4 copy-start.29
  295.6 2.4 copy-start.47
  397.9 5.1 %collective-permute-start.3 = (bf16[3,256]{1,0:T(4,128)(2,1)S(1)}, bf16[3,256]{1,0:T(4,128)(2,1)S(1)}, u32[]{:S(2)}, u32[]{:S(2)}) collective-permute-start(bf16[3,256]{1,0:T(4,128)(2,1)S(1)} %add_convert_fusion.2), channel_id=1, source_target_pairs={{1,0},{2,1},{3,2},{4,3},{5,4},{6,5},{7,6},{8,7},{9,8},{10,9},{11,1... | collective-permute-start | bytes 4616 | tf_op jit(solution)/shard_map/ppermute | solution.py:12
  (7 other events, 8.7 us)
Sparse Core Ops, SparseCore 0:
  23.0 102.6 all-gather.5
  158.0 99.7 all-gather.7
where the time goes:
time: 413 us; the launch traced here: 411 us
  waiting for transfers between devices  127 us (31%)
  blocking collectives  127 us (31%)
  other arithmetic  70.6 us (17%)
  local copies, waits for them, and re-layouts  41.4 us (10%)
  between operations  15.5 us (4%)
  matrix products  14.8 us (4%)
  starting transfers between devices  12.3 us (3%)
    all_gather x2, waiting for transfers between devices, entering(): everything = jax.tree.map(lambda part: lax.all_gather(part, axis), shard)  116 us
    psum x1, blocking collectives, on_device(): lax.psum((packed[0], packed[1], packed[2], packed[3], packed[4]), ('dp',...  98.7 us
    select_n x32, other arithmetic, turn(): return jax.tree.map(lambda a, b: jnp.where(reached, a, b), new, before)  46.9 us
    unnamed x1, blocking collectives  28.8 us
    ppermute x4, starting transfers between devices, from_behind(): return lax.ppermute(shard, axis, pairs)  12.2 us
    exp x32, local copies, waits for them, and re-layouts, combine_carries(): jnp.exp(later[0])[..., None, None] * earlier[1] + later[1]  11.1 us
    ppermute x4, waiting for transfers between devices, from_behind(): return lax.ppermute(shard, axis, pairs)  11.1 us
    unnamed x107, local copies, waits for them, and re-layouts  9.88 us
  transfers between devices with their start and end apart: 6, of which 4 were waited for; matrix products, arithmetic and copies ran while one was open for 12% of the time, Pallas kernels for 0%

commit v1 on v0

v1 whole, which is shorter than its diff:
```python
import jax
import jax.numpy as jnp
from jax import lax
from jax.experimental import pallas as pl
from jax.experimental.pallas import tpu as pltpu
from jax.sharding import PartitionSpec as P

HIGH = lax.Precision.HIGHEST
F32 = jnp.float32
BF16 = jnp.bfloat16
ROWS = 128
LANES = 128
HALO = 8
VMEM = pl.BlockSpec(memory_space=pltpu.VMEM)
SMEM = pl.BlockSpec(memory_space=pltpu.SMEM)
INTERPRET = False


def call(body, outs, ins, scratch=()):
    return pl.pallas_call(
        body,
        out_shape=outs,
        in_specs=ins,
        out_specs=[VMEM] * len(outs),
        scratch_shapes=list(scratch),
        interpret=INTERPRET,
    )


def shape(*dims, dtype=F32):
    return jax.ShapeDtypeStruct(dims, dtype)


def dot(a, b, dims=((1,), (0,)), precision=None):
    return lax.dot_general(
        a, b, (dims, ((), ())), precision=precision, preferred_element_type=F32
    )


NT = ((1,), (1,))
TN = ((0,), (0,))


def iota(dims, axis):
    return lax.broadcasted_iota(jnp.int32, dims, axis)


def column_of(ref, count):
    rows = iota((count, LANES), 0)
    col = jnp.zeros((count, LANES), F32)
    for h in range(count):
        col = jnp.where(rows == h, ref[h], col)
    return col


def steps_body(step_ref, bias_ref, rate_ref, rows_ref, cols_ref):
    heads = step_ref.shape[0]
    raw = step_ref[...] + column_of(bias_ref, heads)
    step = jnp.maximum(raw, 0.0) + jnp.log1p(jnp.exp(-jnp.abs(raw)))
    rate = -jnp.exp(column_of(rate_ref, heads))
    upto = (iota((ROWS, ROWS), 0) <= iota((ROWS, ROWS), 1)).astype(F32)
    cumul = dot(rate * step, upto, precision=HIGH)
    weight = jnp.exp(cumul[:, ROWS - 1 :] - cumul) * step
    fade = jnp.exp(cumul)
    stack = jnp.concatenate([cumul, step, weight, fade], 0)
    rows_ref[: 4 * heads, :] = stack
    rows_ref[4 * heads : 5 * heads, :] = jax.nn.sigmoid(raw)
    rows_ref[5 * heads :, :] = rate
    cols_ref[...] = stack.T


def preact(ext_ref, taps_ref, at, lanes):
    acc = taps_ref[4:5, pl.ds(at, lanes)]
    for k in range(4):
        acc = acc + taps_ref[k : k + 1, pl.ds(at, lanes)] * ext_ref[pl.ds(HALO - 3 + k, ROWS), :]
    return acc


def pair_column(cols_ref, first, second, left):
    a = jnp.broadcast_to(cols_ref[:, first : first + 1], (ROWS, LANES))
    b = jnp.broadcast_to(cols_ref[:, second : second + 1], (ROWS, LANES))
    return jnp.where(left, a, b)


def first_body(x_ref, bc_ref, halo_ref, taps_ref, g_ref, cols_ref, xact_ref, bcact_ref, send_ref, ext_ref, ext2_ref):
    inner = x_ref.shape[1]
    heads = inner // 64
    ext2_ref[:HALO, :] = halo_ref[:, inner:].astype(F32)
    ext2_ref[HALO:, :] = bc_ref[...].astype(F32)
    pre = preact(ext2_ref, taps_ref, inner, 2 * LANES)
    bc = (pre * jax.nn.sigmoid(pre)).astype(BF16)
    bcact_ref[...] = bc
    b_t = bc[:, :LANES].astype(F32).T.astype(BF16)
    c_t = bc[:, LANES:].astype(F32).T.astype(BF16)
    left = iota((ROWS, LANES), 1) < 64
    for i in range(inner // LANES):
        at = i * LANES
        lanes = pl.ds(at, LANES)
        ext = ext_ref.at[i % 2]
        ext[:HALO, :] = halo_ref[:, lanes].astype(F32)
        ext[HALO:, :] = x_ref[:, lanes].astype(F32)
        pre = preact(ext, taps_ref, at, LANES)
        act = (pre * jax.nn.sigmoid(pre)).astype(BF16)
        xact_ref[:, lanes] = act
        weight = pair_column(cols_ref, 2 * heads + 2 * i, 2 * heads + 2 * i + 1, left)
        fade = pair_column(cols_ref, 3 * heads + 2 * i, 3 * heads + 2 * i + 1, left)
        xw = (act.astype(F32) * weight).astype(BF16)
        gw = (g_ref[:, lanes].astype(F32) * fade).astype(BF16)
        send_ref[i, :ROWS, :] = dot(b_t, xw).astype(BF16)
        send_ref[i, ROWS : 2 * ROWS, :] = dot(c_t, gw).astype(BF16)
        total = fade[ROWS - 1 :, :]
        high = total.astype(BF16)
        low = (total - high.astype(F32)).astype(BF16)
        row = iota((16, LANES), 0)
        send_ref[i, 2 * ROWS :, :] = jnp.where(row == 0, high.astype(F32), jnp.where(row == 1, low.astype(F32), 0.0)).astype(BF16)


def scan_body(got_ref, out_ref):
    count = got_ref.shape[0]

    def decay(j):
        tail = got_ref[j, 2 * ROWS :, :].astype(F32)
        return tail[0:1, :] + tail[1:2, :]

    state = jnp.zeros((ROWS, LANES), F32)
    for j in range(count):
        out_ref[j, :ROWS, :] = state.astype(BF16)
        state = decay(j) * state + got_ref[j, :ROWS, :].astype(F32)
    state = jnp.zeros((ROWS, LANES), F32)
    for j in range(count - 1, -1, -1):
        out_ref[j, ROWS:, :] = state.astype(BF16)
        state = decay(j) * state + got_ref[j, ROWS : 2 * ROWS, :].astype(F32)


def inner_body(
    x_ref, bc_ref, halo_ref, taps_ref, g_ref, rows_ref, cols_ref, xact_ref, bcact_ref, skip_ref,
    dx_ref, slope_ref, xw_ref, gw_ref, dbc_ref, slope2_ref, row_ref, ext_ref, ext2_ref,
):
    inner = x_ref.shape[1]
    heads = inner // 64
    ext2_ref[:HALO, :] = halo_ref[:, inner:].astype(F32)
    ext2_ref[HALO:, :] = bc_ref[...].astype(F32)
    pre = preact(ext2_ref, taps_ref, inner, 2 * LANES)
    gate = jax.nn.sigmoid(pre)
    slope2_ref[...] = gate * (1.0 + pre * (1.0 - gate))
    b = bcact_ref[:, :LANES]
    c = bcact_ref[:, LANES:]
    scores = dot(b, c, NT)
    causal = iota((ROWS, ROWS), 0) <= iota((ROWS, ROWS), 1)
    left = iota((ROWS, LANES), 1) < 64
    ones = jnp.ones((8, ROWS), BF16)
    dscores = jnp.zeros((ROWS, ROWS), F32)
    for i in range(inner // LANES):
        at = i * LANES
        lanes = pl.ds(at, LANES)
        ext = ext_ref.at[i % 2]
        ext[:HALO, :] = halo_ref[:, lanes].astype(F32)
        ext[HALO:, :] = x_ref[:, lanes].astype(F32)
        pre = preact(ext, taps_ref, at, LANES)
        gate = jax.nn.sigmoid(pre)
        slope_ref[:, lanes] = gate * (1.0 + pre * (1.0 - gate))
        act = xact_ref[:, lanes]
        g = g_ref[:, lanes]
        wide = g.astype(F32)
        weight = pair_column(cols_ref, 2 * heads + 2 * i, 2 * heads + 2 * i + 1, left)
        fade = pair_column(cols_ref, 3 * heads + 2 * i, 3 * heads + 2 * i + 1, left)
        xw_ref[:, lanes] = (act.astype(F32) * weight).astype(BF16)
        gw_ref[:, lanes] = (wide * fade).astype(BF16)
        skip = jnp.where(left, skip_ref[2 * i], skip_ref[2 * i + 1])
        dx = skip * wide
        both = jnp.sum(act.astype(F32) * wide, 0, keepdims=True)
        row_ref[2 * heads + 2 * i : 2 * heads + 2 * i + 1, :] = jnp.where(left[:1], both, 0.0)
        row_ref[2 * heads + 2 * i + 1 : 2 * heads + 2 * i + 2, :] = jnp.where(left[:1], 0.0, both)
        for k in range(2):
            h = 2 * i + k
            mine = left if k == 0 else ~left
            own = jnp.where(mine, wide, 0.0).astype(BF16)
            gap = rows_ref[h : h + 1, :] - cols_ref[:, h : h + 1]
            fall = jnp.exp(jnp.where(causal, gap, -1e30)) * cols_ref[:, heads + h : heads + h + 1]
            mixing = scores * fall
            dmix = dot(act, own, NT).astype(BF16).astype(F32)
            dscores = dscores + dmix * fall
            both = (dmix * mixing).astype(BF16)
            row_ref[h : h + 1, :] = dot(ones, both)[:1]
            row_ref[heads + h : heads + h + 1, :] = dot(ones, both, NT)[:1]
            dx = dx + dot(mixing.astype(BF16), own)
        dx_ref[:, lanes] = dx
    ds = dscores.astype(BF16)
    dbc_ref[:, :LANES] = dot(ds, c)
    dbc_ref[:, LANES:] = dot(ds, b, TN)


def back_through(dact, slope, pad_ref, ext_ref, taps_ref, at, lanes, out_ref, out_at, rim_ref):
    dpre = dact.astype(BF16).astype(F32) * slope
    pad_ref[:HALO, :] = jnp.zeros((HALO, lanes), F32)
    pad_ref[HALO : HALO + ROWS, :] = dpre
    pad_ref[HALO + ROWS :, :] = jnp.zeros((HALO, lanes), F32)
    own = jnp.zeros((ROWS, lanes), F32)
    rim = jnp.zeros((HALO, lanes), F32)
    sums = []
    for k in range(4):
        tap = taps_ref[k : k + 1, pl.ds(at, lanes)]
        own = own + tap * pad_ref[pl.ds(HALO + 3 - k, ROWS), :]
        rim = rim + tap * pad_ref[pl.ds(HALO - k, HALO), :]
        sums.append(jnp.sum(dpre * ext_ref[pl.ds(HALO - 3 + k, ROWS), :], 0, keepdims=True))
    sums.append(jnp.sum(dpre, 0, keepdims=True))
    out_ref[:, pl.ds(out_at, lanes)] = own.astype(BF16)
    rim_ref[:, pl.ds(at, lanes)] = rim.astype(BF16)
    return sums


def last_body(
    x_ref, bc_ref, halo_ref, taps_ref, rows_ref, cols_ref, bcact_ref, states_ref,
    dx_ref, slope_ref, xw_ref, gw_ref, dbc_ref, slope2_ref, row_ref,
    gx_ref, gbc_ref, gstep_ref, rim_ref, part_ref, ext_ref, pad_ref, ext2_ref, pad2_ref, acc_ref,
):
    inner = x_ref.shape[1]
    heads = inner // 64
    b = bcact_ref[:, :LANES]
    c = bcact_ref[:, LANES:]
    left = iota((ROWS, LANES), 1) < 64
    half = jnp.where((iota((8, LANES), 1) < 64) == (iota((8, LANES), 0) == 0), 1.0, 0.0).astype(BF16)
    db = dbc_ref[:, :LANES]
    dc = dbc_ref[:, LANES:]
    part_ref[...] = jnp.zeros(part_ref.shape, F32)
    for i in range(inner // LANES):
        at = i * LANES
        lanes = pl.ds(at, LANES)
        state = states_ref[i, :ROWS, :]
        later = states_ref[i, ROWS:, :]
        xw = xw_ref[:, lanes]
        gw = gw_ref[:, lanes]
        carried = dot(c, state) * gw.astype(F32)
        dxw = dot(b, later).astype(BF16).astype(F32)
        dc = dc + dot(gw, state, NT)
        db = db + dot(xw, later, NT)
        acc_ref[2 * i : 2 * i + 2, :] = dot(half, carried.astype(BF16), NT)[:2]
        acc_ref[heads + 2 * i : heads + 2 * i + 2, :] = dot(half, (dxw * xw.astype(F32)).astype(BF16), NT)[:2]
        both = jnp.sum(state.astype(F32) * later.astype(F32), 0, keepdims=True)
        acc_ref[2 * heads + 2 * i : 2 * heads + 2 * i + 1, :] = jnp.where(left[:1], both, 0.0)
        acc_ref[2 * heads + 2 * i + 1 : 2 * heads + 2 * i + 2, :] = jnp.where(left[:1], 0.0, both)
        weight = pair_column(cols_ref, 2 * heads + 2 * i, 2 * heads + 2 * i + 1, left)
        ext = ext_ref.at[i % 2]
        ext[:HALO, :] = halo_ref[:, lanes].astype(F32)
        ext[HALO:, :] = x_ref[:, lanes].astype(F32)
        sums = back_through(
            dx_ref[:, lanes] + weight * dxw, slope_ref[:, lanes], pad_ref.at[i % 2], ext, taps_ref, at, LANES, gx_ref, at, rim_ref
        )
        for k in range(5):
            part_ref[i, k : k + 1, :] = sums[k]
    ext2_ref[:HALO, :] = halo_ref[:, inner:].astype(F32)
    ext2_ref[HALO:, :] = bc_ref[...].astype(F32)
    dbc = jnp.concatenate([db, dc], 1)
    sums = back_through(dbc, slope2_ref[...], pad2_ref, ext2_ref, taps_ref, inner, 2 * LANES, gbc_ref, 0, rim_ref)
    for k in range(5):
        part_ref[k, 5:6, :] = sums[k][:, :LANES]
        part_ref[k, 6:7, :] = sums[k][:, LANES:]
    step = rows_ref[heads : 2 * heads, :]
    gate = rows_ref[4 * heads : 5 * heads, :]
    rate = rows_ref[5 * heads : 6 * heads, :]
    total = rows_ref[3 * heads : 4 * heads, ROWS - 1 :]
    at_t = row_ref[:heads, :]
    at_s = row_ref[heads : 2 * heads, :]
    ended = acc_ref[heads : 2 * heads, :]
    at_end = jnp.sum(ended, 1, keepdims=True) + total * jnp.sum(acc_ref[2 * heads : 3 * heads, :], 1, keepdims=True)
    final = iota((heads, ROWS), 1) == ROWS - 1
    dcumul = at_t - at_s + acc_ref[:heads, :] - ended + jnp.where(final, at_end, 0.0)
    onward = (iota((ROWS, ROWS), 0) >= iota((ROWS, ROWS), 1)).astype(F32)
    ddecay = dot(dcumul, onward, precision=HIGH)
    dstep = (at_s + ended) / step + ddecay * rate
    dstep = dstep * gate
    gstep_ref[...] = dstep
    dbias = jnp.sum(dstep, 1, keepdims=True)
    drate = jnp.sum(ddecay * rate * step, 1, keepdims=True)
    dskip = jnp.sum(row_ref[2 * heads : 3 * heads, :], 1, keepdims=True)
    r, l = iota((heads, LANES), 0), iota((heads, LANES), 1)
    placed = jnp.where(l == r, dbias, jnp.where(l == r + heads, drate, jnp.where(l == r + 2 * heads, dskip, 0.0)))
    part_ref[0, 7:8, :] = jnp.sum(placed, 0, keepdims=True)


def on_device(
    mixer_input, state_input, step_raw, conv_weight, conv_bias, step_bias, log_rate, skip_gain, grad_out
):
    x, bc, step, g = mixer_input[0], state_input[0], step_raw[0], grad_out[0]
    rows, inner = x.shape
    heads = step.shape[0]
    pairs = inner // LANES
    n_seq, n_dp = lax.axis_size("seq"), lax.axis_size("dp")
    assert rows == ROWS and n_seq == pairs and bc.shape[1] == 2 * LANES and heads * 64 == inner
    tail = jnp.concatenate([x[rows - HALO :], bc[rows - HALO :]], 1)
    halo = lax.ppermute(tail, "seq", [(i, i + 1) for i in range(n_seq - 1)])
    taps = jnp.concatenate([conv_weight, conv_bias[None]], 0)
    by_row, by_col = call(
        steps_body, [shape(6 * heads, ROWS), shape(ROWS, 4 * heads)], [VMEM, SMEM, SMEM]
    )(step, step_bias, log_rate)
    ext = [pltpu.VMEM((2, ROWS + HALO, LANES), F32)]
    ext2 = [pltpu.VMEM((ROWS + HALO, 2 * LANES), F32)]
    x_act, bc_act, send = call(
        first_body,
        [shape(rows, inner, dtype=BF16), shape(rows, 2 * LANES, dtype=BF16), shape(pairs, 2 * ROWS + 16, LANES, dtype=BF16)],
        [VMEM] * 6,
        ext + ext2,
    )(x, bc, halo, taps, g, by_col)
    got = lax.all_to_all(send, "seq", 0, 0)
    dx, slope, xw, gw, dbc, slope2, row = call(
        inner_body,
        [
            shape(rows, inner),
            shape(rows, inner),
            shape(rows, inner, dtype=BF16),
            shape(rows, inner, dtype=BF16),
            shape(rows, 2 * LANES),
            shape(rows, 2 * LANES),
            shape(3 * heads, ROWS),
        ],
        [VMEM] * 9 + [SMEM],
        ext + ext2,
    )(x, bc, halo, taps, g, by_row, by_col, x_act, bc_act, skip_gain)
    scanned = call(scan_body, [shape(n_seq, 2 * ROWS, LANES, dtype=BF16)], [VMEM])(got)[0]
    states = lax.all_to_all(scanned, "seq", 0, 0)
    gx, gbc, gstep, rim, part = call(
        last_body,
        [
            shape(rows, inner, dtype=BF16),
            shape(rows, 2 * LANES, dtype=BF16),
            shape(heads, ROWS),
            shape(HALO, inner + 2 * LANES, dtype=BF16),
            shape(pairs, 8, LANES),
        ],
        [VMEM] * 15,
        ext
        + [pltpu.VMEM((2, ROWS + 2 * HALO, LANES), F32)]
        + ext2
        + [pltpu.VMEM((ROWS + 2 * HALO, 2 * LANES), F32), pltpu.VMEM((3 * heads, ROWS), F32)],
    )(x, bc, halo, taps, by_row, by_col, bc_act, states, dx, slope, xw, gw, dbc, slope2, row)
    back = lax.ppermute(rim, "seq", [(i, i - 1) for i in range(1, n_seq)])
    mine = jnp.sum(lax.all_to_all(part, "seq", 0, 0), 0)
    shared = lax.all_to_all(jnp.broadcast_to(mine[None], (n_dp, 8, LANES)), "dp", 0, 0)
    mean = jnp.sum(shared, 0) / n_dp
    whole = lax.all_to_all(jnp.broadcast_to(mean[None], (pairs, 8, LANES)), "seq", 0, 0)
    gx = gx.at[rows - 3 :].add(back[:3, :inner])
    gbc = gbc.at[rows - 3 :].add(back[:3, inner:])
    conv = jnp.concatenate([whole[:, k, :].reshape(1, inner) for k in range(5)], 0)
    conv = jnp.concatenate([conv, whole[:5, 5, :], whole[:5, 6, :]], 1)
    small = whole[0, 7]
    return (
        gx[None],
        gbc[None],
        gstep[None],
        conv[:4],
        conv[4],
        small[:heads],
        small[heads : 2 * heads],
        small[2 * heads : 3 * heads],
    )


def solution(mesh):
    return jax.shard_map(
        on_device,
        mesh=mesh,
        in_specs=(
            P("dp", "seq", None),
            P("dp", "seq", None),
            P("dp", None, "seq"),
            P(),
            P(),
            P(),
            P(),
            P(),
            P("dp", "seq", None),
        ),
        out_specs=(
            P("dp", "seq", None),
            P("dp", "seq", None),
            P("dp", None, "seq"),
            P(),
            P(),
            P(),
            P(),
            P(),
        ),
        check_vma=False,
    )
```

time: 413 us -> 145 us (0.35)
  blocking collectives: 127 us -> 39.8 us
  waiting for transfers between devices: 127 us -> 40.1 us
  other arithmetic: 70.6 us -> 3.59 us
  local copies, waits for them, and re-layouts: 41.4 us -> 9.07 us
  Pallas kernels: 0 us -> 21.8 us
  starting transfers between devices: 12.3 us -> 29.4 us
  matrix products: 14.8 us -> 0 us
  between operations: 15.5 us -> 0.7 us
    all_gather x2 -> x0, waiting for transfers between devices: 116 us -> none  [entering(): everything = jax.tree.map(lambda part: lax.all_gather(part, axis), shard)]
    psum x1 -> x0, blocking collectives: 98.7 us -> none  [on_device(): lax.psum((packed[0], packed[1], packed[2], packed[3], packed[4]), ('dp',...]
    select_n x32 -> x0, other arithmetic: 46.9 us -> none  [turn(): return jax.tree.map(lambda a, b: jnp.where(reached, a, b), new, before)]
    all_to_all x0 -> x4, waiting for transfers between devices: none -> 40.1 us  [the longest x1 21.6 us: on_device(): states = lax.all_to_all(scanned, 'seq', 0, 0)]
    all_to_all x0 -> x1, blocking collectives: none -> 39.8 us  [on_device(): got = lax.all_to_all(send, 'seq', 0, 0)]
    unnamed x1 -> x0, blocking collectives: 28.8 us -> none
    all_to_all x0 -> x4, starting transfers between devices: none -> 22 us  [the longest x1 9.67 us: on_device(): lax.all_to_all(jnp.broadcast_to(mine[None], (n_dp, 8, LANES)), 'dp', 0, 0)]
    pallas_call x0 -> x5, Pallas kernels: none -> 21.8 us  [the longest x1 6.97 us: on_device(): call(last_body, [shape(rows, inner, dtype=BF16), shape(rows, 2 * LANES, d...]
  transfers between devices with their start and end apart: 6 -> 6, of which waited for: 4 -> 4; matrix products, arithmetic and copies ran while one was open for 12% -> 5% of each run, Pallas kernels for 0% -> 6%
where the time goes in v1:
time: 145 us; the launch traced here: 144 us
  waiting for transfers between devices  40.1 us (28%)
  blocking collectives  39.8 us (27%)
  starting transfers between devices  29.4 us (20%)
  Pallas kernels  21.8 us (15%)
  local copies, waits for them, and re-layouts  9.07 us (6%)
  other arithmetic  3.59 us (2%)
    all_to_all x1, blocking collectives, on_device(): got = lax.all_to_all(send, 'seq', 0, 0)  39.8 us
    all_to_all x1, waiting for transfers between devices, on_device(): states = lax.all_to_all(scanned, 'seq', 0, 0)  21.6 us
    all_to_all x1, starting transfers between devices, on_device(): lax.all_to_all(jnp.broadcast_to(mine[None], (n_dp, 8, LANES)), 'dp', 0, 0)  9.67 us
    pallas_call x1, Pallas kernels, on_device(): call(last_body, [shape(rows, inner, dtype=BF16), shape(rows, 2 * LANES, d...  6.97 us
    all_to_all x1, waiting for transfers between devices, on_device(): lax.all_to_all(jnp.broadcast_to(mine[None], (n_dp, 8, LANES)), 'dp', 0, 0)  6.94 us
    pallas_call x1, Pallas kernels, on_device(): call(inner_body, [shape(rows, inner), shape(rows, inner), shape(rows, inn...  6.48 us
    all_to_all x1, waiting for transfers between devices, on_device(): lax.all_to_all(jnp.broadcast_to(mean[None], (pairs, 8, LANES)), 'seq', 0, 0)  5.84 us
    all_to_all x1, waiting for transfers between devices, on_device(): mine = jnp.sum(lax.all_to_all(part, 'seq', 0, 0), 0)  5.76 us
  transfers between devices with their start and end apart: 6, of which 4 were waited for; matrix products, arithmetic and copies ran while one was open for 5% of the time, Pallas kernels for 6%

profile of v1, /device:TPU:1, one launch (start us, length us, event | category | flops | bytes accessed | tf_op | source)
XLA Modules:
  0.0 144.4 jit_solution(1317696242659803624)
XLA Ops:
  0.6 0.7 slice_bitcast_fusion.6
  1.3 0.8 slice_bitcast_fusion
  2.1 5.4 %collective-permute-start = (bf16[8,2304]{1,0:T(8,128)(2,1)S(1)}, bf16[8,2304]{1,0:T(8,128)(2,1)S(1)}, u32[]{:S(2)}, u32[]{:S(2)}) collective-permute-start(bf16[8,2304]{1,0:T(8,128)(2,1)S(1)} %pad_maximum_fusion.2), channel_id=1, source_target_pairs={{0,1},{1,2},{2,3},{3,4},{4,5},{5,6},{6,7},{7,8},{8,9},{9,10},{10,1... | collective-permute-start | bytes 110600 | tf_op jit(solution)/shard_map/ppermute | solution.py:291
  7.5 0.7 broadcast_in_dim.28
  8.2 1.4 pad_maximum_fusion.taps_ref
  9.6 1.8 %shard_map.152 = (f32[192,128]{1,0:T(8,128)}, f32[128,128]{1,0:T(8,128)}) custom-call(f32[32,128]{1,0:T(8,128)} %bitcast.43, f32[32]{0:T(128)} %bias_ref.1, f32[32]{0:T(128)} %rate_ref.1), custom_call_target="tpu_custom_call" | custom-call | tf_op jit(solution)/shard_map/pallas_call | solution.py:293
  11.4 0.0 collective-permute-done.halo_ref
  11.4 0.0 copy-start.1
  11.4 0.6 copy-done.1
  12.0 4.1 %shard_map.153 = (bf16[128,2048]{1,0:T(8,128)(2,1)}, bf16[128,256]{1,0:T(8,128)(2,1)}, bf16[16,272,128]{2,1,0:T(8,128)(2,1)}) custom-call(bf16[128,2048]{1,0:T(8,128)(2,1)} %bitcast.35, bf16[128,256]{1,0:T(8,128)(2,1)} %bitcast.40, bf16[8,2304]{1,0:T(8,128)(2,1)} %copy-done.1, f32[5,2304]{1,0:T(8,128)} %pad_maximum_fusion.taps_ref, ...), custom_call_target="tpu_custom_call" | custom-call | tf_op jit(solution)/shard_map/pallas_call | solution.py:298
  16.1 39.8 %all_to_all.25.got_ref = bf16[16,272,128]{2,1,0:T(8,128)(2,1)} all-to-all(bf16[16,272,128]{2,1,0:T(8,128)(2,1)} %get-tuple-element.52), channel_id=1, replica_groups=mesh['dp'=32,'seq'=16] {'seq'}, dimensions={0} | all-to-all | bytes 2228224 | tf_op jit(solution)/shard_map/all_to_all | solution.py:304
  55.9 2.5 %shard_map.154 = bf16[16,256,128]{2,1,0:T(8,128)(2,1)} custom-call(bf16[16,272,128]{2,1,0:T(8,128)(2,1)} %all_to_all.25.got_ref), custom_call_target="tpu_custom_call" | custom-call | tf_op jit(solution)/shard_map/pallas_call | solution.py:319
  58.3 3.6 %all-to-all-start.1 = ((bf16[16,256,128]{2,1,0:T(8,128)(2,1)}), bf16[16,256,128]{2,1,0:T(8,128)(2,1)S(1)}, u32[]{:S(2)}, u32[]{:S(2)}) async-start(bf16[16,256,128]{2,1,0:T(8,128)(2,1)} %shard_map.154), calls=%async_computation.1 | async-start | bytes 2097152 | tf_op jit(solution)/shard_map/all_to_all | solution.py:320
  61.9 6.5 %shard_map.155 = (f32[128,2048]{1,0:T(8,128)}, f32[128,2048]{1,0:T(8,128)}, bf16[128,2048]{1,0:T(8,128)(2,1)}, bf16[128,2048]{1,0:T(8,128)(2,1)}, f32[128,256]{1...) custom-call(bf16[128,2048]{1,0:T(8,128)(2,1)} %bitcast.36, bf16[128,256]{1,0:T(8,128)(2,1)} %bitcast.41, ...), custom_call_target="tpu_custom_call" | custom-call | tf_op jit(solution)/shard_map/pallas_call | solution.py:305
  68.3 21.6 %all-to-all-done.1.states_ref = bf16[16,256,128]{2,1,0:T(8,128)(2,1)S(1)} async-done(((bf16[16,256,128]{2,1,0:T(8,128)(2,1)}), bf16[16,256,128]{2,1,0:T(8,128)(2,1)S(1)}, u32[]{:S(2)}, u32[]{:S(2)}) %all-to-all-start.1) | async-done | bytes 1048608 | tf_op jit(solution)/shard_map/all_to_all | solution.py:320
  89.9 0.0 copy-start
  89.9 1.0 copy-done
  90.9 7.0 %shard_map.156 = (bf16[128,2048]{1,0:T(8,128)(2,1)}, bf16[128,256]{1,0:T(8,128)(2,1)}, f32[32,128]{1,0:T(8,128)}, bf16[8,2304]{1,0:T(8,128)(2,1)}, f32[16,8,128]{2,1,0:T(8,128)}) custom-call(bf16[128,2048]{1,0:T(8,128)(2,1)} %bitcast.37, bf16[128,256]{1,0:T(8,128)(2,1)} %bitcast.42, bf16[8,2304]{1,0:T(8,128)(2,1)} %copy-done.1, ...), custom_call_target="tpu_custom_call" | custom-call | tf_op jit(solution)/shard_map/pallas_call | solution.py:321
  97.8 3.4 %all-to-all-start.2 = ((f32[16,8,128]{2,1,0:T(8,128)}), f32[16,8,128]{2,1,0:T(8,128)S(1)}, u32[]{:S(2)}, u32[]{:S(2)}) async-start(f32[16,8,128]{2,1,0:T(8,128)} %get-tuple-element.65), calls=%async_computation.2 | async-start | bytes 131072 | tf_op jit(solution)/shard_map/all_to_all | solution.py:337
  101.3 2.0 %collective-permute-start.1 = (bf16[8,2304]{1,0:T(8,128)(2,1)}, bf16[8,2304]{1,0:T(8,128)(2,1)S(1)}, u32[]{:S(2)}, u32[]{:S(2)}) collective-permute-start(bf16[8,2304]{1,0:T(8,128)(2,1)} %get-tuple-element.62), channel_id=1, source_target_pairs={{1,0},{2,1},{3,2},{4,3},{5,4},{6,5},{7,6},{8,7},{9,8},{10,9},{11,1... | collective-permute-start | bytes 110600 | tf_op jit(solution)/shard_map/ppermute | solution.py:336
  103.3 5.8 %all-to-all-done.2 = f32[16,8,128]{2,1,0:T(8,128)S(1)} async-done(((f32[16,8,128]{2,1,0:T(8,128)}), f32[16,8,128]{2,1,0:T(8,128)S(1)}, u32[]{:S(2)}, u32[]{:S(2)}) %all-to-all-start.2) | async-done | bytes 65568 | tf_op jit(solution)/shard_map/all_to_all | solution.py:337
  109.1 0.6 broadcast_in_dim.34
  109.7 9.7 %all-to-all-start.3 = ((f32[32,8,128]{2,1,0:T(8,128)}), f32[32,8,128]{2,1,0:T(8,128)S(1)}, u32[]{:S(2)}, u32[]{:S(2)}) async-start(f32[32,8,128]{2,1,0:T(8,128)} %broadcast_in_dim.34), calls=%async_computation.3 | async-start | bytes 262144 | tf_op jit(solution)/shard_map/all_to_all | solution.py:338
  119.4 0.0 collective-permute-done.1
  119.4 0.8 fusion
  120.2 1.4 scatter-add.6
  121.6 6.9 %all-to-all-done.3 = f32[32,8,128]{2,1,0:T(8,128)S(1)} async-done(((f32[32,8,128]{2,1,0:T(8,128)}), f32[32,8,128]{2,1,0:T(8,128)S(1)}, u32[]{:S(2)}, u32[]{:S(2)}) %all-to-all-start.3) | async-done | bytes 131104 | tf_op jit(solution)/shard_map/all_to_all | solution.py:338
  128.6 0.6 broadcast_in_dim.35
  129.2 5.4 %all-to-all-start.4 = ((f32[16,8,128]{2,1,0:T(8,128)}), f32[16,8,128]{2,1,0:T(8,128)S(1)}, u32[]{:S(2)}, u32[]{:S(2)}) async-start(f32[16,8,128]{2,1,0:T(8,128)} %broadcast_in_dim.35), calls=%async_computation.4 | async-start | bytes 131072 | tf_op jit(solution)/shard_map/all_to_all | solution.py:340
  134.6 0.7 fusion.1
  135.3 1.3 scatter-add.9
  136.6 5.8 %all-to-all-done.4 = f32[16,8,128]{2,1,0:T(8,128)S(1)} async-done(((f32[16,8,128]{2,1,0:T(8,128)}), f32[16,8,128]{2,1,0:T(8,128)S(1)}, u32[]{:S(2)}, u32[]{:S(2)}) %all-to-all-start.4) | async-done | bytes 65568 | tf_op jit(solution)/shard_map/all_to_all | solution.py:340
  142.5 0.1 concatenate.18
  142.6 0.6 maximum_reduce_fusion
  143.2 0.6 slice.137
  143.8 0.6 slice_bitcast_fusion.7
  (8 shorter events, 0.1 us)
Async XLA Ops:
  2.1 9.3 %collective-permute-start = (bf16[8,2304]{1,0:T(8,128)(2,1)S(1)}, bf16[8,2304]{1,0:T(8,128)(2,1)S(1)}, u32[]{:S(2)}, u32[]{:S(2)}) collective-permute-start(bf16[8,2304]{1,0:T(8,128)(2,1)S(1)} %pad_maximum_fusion.2), channel_id=1, source_target_pairs={{0,1},{1,2},{2,3},{3,4},{4,5},{5,6},{6,7},{7,8},{8,9},{9,10},{10,1... | collective-permute-start | bytes 110600 | tf_op jit(solution)/shard_map/ppermute | solution.py:291
  11.4 0.6 copy-start.1
  58.3 31.6 %all-to-all-start.1 = ((bf16[16,256,128]{2,1,0:T(8,128)(2,1)}), bf16[16,256,128]{2,1,0:T(8,128)(2,1)S(1)}, u32[]{:S(2)}, u32[]{:S(2)}) async-start(bf16[16,256,128]{2,1,0:T(8,128)(2,1)} %shard_map.154), calls=%async_computation.1 | async-start | bytes 2097152 | tf_op jit(solution)/shard_map/all_to_all | solution.py:320
  89.9 1.0 copy-start
  97.8 11.2 %all-to-all-start.2 = ((f32[16,8,128]{2,1,0:T(8,128)}), f32[16,8,128]{2,1,0:T(8,128)S(1)}, u32[]{:S(2)}, u32[]{:S(2)}) async-start(f32[16,8,128]{2,1,0:T(8,128)} %get-tuple-element.65), calls=%async_computation.2 | async-start | bytes 131072 | tf_op jit(solution)/shard_map/all_to_all | solution.py:337
  101.3 18.1 %collective-permute-start.1 = (bf16[8,2304]{1,0:T(8,128)(2,1)}, bf16[8,2304]{1,0:T(8,128)(2,1)S(1)}, u32[]{:S(2)}, u32[]{:S(2)}) collective-permute-start(bf16[8,2304]{1,0:T(8,128)(2,1)} %get-tuple-element.62), channel_id=1, source_target_pairs={{1,0},{2,1},{3,2},{4,3},{5,4},{6,5},{7,6},{8,7},{9,8},{10,9},{11,1... | collective-permute-start | bytes 110600 | tf_op jit(solution)/shard_map/ppermute | solution.py:336
  109.7 18.8 %all-to-all-start.3 = ((f32[32,8,128]{2,1,0:T(8,128)}), f32[32,8,128]{2,1,0:T(8,128)S(1)}, u32[]{:S(2)}, u32[]{:S(2)}) async-start(f32[32,8,128]{2,1,0:T(8,128)} %broadcast_in_dim.34), calls=%async_computation.3 | async-start | bytes 262144 | tf_op jit(solution)/shard_map/all_to_all | solution.py:338
  129.2 13.2 %all-to-all-start.4 = ((f32[16,8,128]{2,1,0:T(8,128)}), f32[16,8,128]{2,1,0:T(8,128)S(1)}, u32[]{:S(2)}, u32[]{:S(2)}) async-start(f32[16,8,128]{2,1,0:T(8,128)} %broadcast_in_dim.35), calls=%async_computation.4 | async-start | bytes 131072 | tf_op jit(solution)/shard_map/all_to_all | solution.py:340

commit v2 on v1

--- a/solution.py
+++ b/solution.py
@@ -12,23 +12,37 @@
 LANES = 128
 HALO = 8
 VMEM = pl.BlockSpec(memory_space=pltpu.VMEM)
+FAR = pl.BlockSpec(memory_space=pltpu.VMEM)
 SMEM = pl.BlockSpec(memory_space=pltpu.SMEM)
 INTERPRET = False
 
 
 def call(body, outs, ins, scratch=()):
-    return pl.pallas_call(
+    kernel = pl.pallas_call(
         body,
         out_shape=outs,
         in_specs=ins,
         out_specs=[VMEM] * len(outs),
         scratch_shapes=list(scratch),
+        compiler_params=pltpu.CompilerParams(vmem_limit_bytes=16 << 20),
         interpret=INTERPRET,
     )
+    if INTERPRET:
+        return kernel
+    return lambda *given: kernel(
+        *(
+            pltpu.with_memory_space_constraint(a, pltpu.VMEM if spec is VMEM else pltpu.HBM)
+            for a, spec in zip(given, ins, strict=True)
+        )
+    )
 
 
 def shape(*dims, dtype=F32):
     return jax.ShapeDtypeStruct(dims, dtype)
+
+
+def kept(*dims, dtype=F32):
+    return shape(*dims, dtype=dtype) if INTERPRET else pltpu.VMEM(dims, dtype)
 
 
 def dot(a, b, dims=((1,), (0,)), precision=None):
@@ -53,8 +67,10 @@
     return col
 
 
-def steps_body(step_ref, bias_ref, rate_ref, rows_ref, cols_ref):
+def steps_body(step_ref, weight_ref, offset_ref, bias_ref, rate_ref, rows_ref, cols_ref, taps_ref):
     heads = step_ref.shape[0]
+    taps_ref[:4, :] = weight_ref[...]
+    taps_ref[4:5, :] = offset_ref[...].reshape(1, -1)
     raw = step_ref[...] + column_of(bias_ref, heads)
     step = jnp.maximum(raw, 0.0) + jnp.log1p(jnp.exp(-jnp.abs(raw)))
     rate = -jnp.exp(column_of(rate_ref, heads))
@@ -82,7 +98,7 @@
     return jnp.where(left, a, b)
 
 
-def first_body(x_ref, bc_ref, halo_ref, taps_ref, g_ref, cols_ref, xact_ref, bcact_ref, send_ref, ext_ref, ext2_ref):
+def first_body(x_ref, bc_ref, halo_ref, taps_ref, g_ref, cols_ref, bcact_ref, send_ref, ext_ref, ext2_ref):
     inner = x_ref.shape[1]
     heads = inner // 64
     ext2_ref[:HALO, :] = halo_ref[:, inner:].astype(F32)
@@ -101,39 +117,61 @@
         ext[HALO:, :] = x_ref[:, lanes].astype(F32)
         pre = preact(ext, taps_ref, at, LANES)
         act = (pre * jax.nn.sigmoid(pre)).astype(BF16)
-        xact_ref[:, lanes] = act
         weight = pair_column(cols_ref, 2 * heads + 2 * i, 2 * heads + 2 * i + 1, left)
         fade = pair_column(cols_ref, 3 * heads + 2 * i, 3 * heads + 2 * i + 1, left)
         xw = (act.astype(F32) * weight).astype(BF16)
         gw = (g_ref[:, lanes].astype(F32) * fade).astype(BF16)
-        send_ref[i, :ROWS, :] = dot(b_t, xw).astype(BF16)
-        send_ref[i, ROWS : 2 * ROWS, :] = dot(c_t, gw).astype(BF16)
+        send_ref[i % 2, i // 2, :ROWS, :] = dot(b_t, xw).astype(BF16)
+        send_ref[i % 2, i // 2, ROWS : 2 * ROWS, :] = dot(c_t, gw).astype(BF16)
         total = fade[ROWS - 1 :, :]
-        high = total.astype(BF16)
-        low = (total - high.astype(F32)).astype(BF16)
-        row = iota((16, LANES), 0)
-        send_ref[i, 2 * ROWS :, :] = jnp.where(row == 0, high.astype(F32), jnp.where(row == 1, low.astype(F32), 0.0)).astype(BF16)
+        send_ref[i % 2, i // 2, 2 * ROWS :, :] = decay_rows(total)
+
+
+def decay_of(tail):
+    tail = tail.astype(F32)
+    return tail[0:1, :] + tail[1:2, :]
+
+
+def decay_rows(total):
+    high = total.astype(BF16).astype(F32)
+    row = iota((16, LANES), 0)
+    return jnp.where(row == 0, high, jnp.where(row == 1, total - high, 0.0)).astype(BF16)
+
+
+def join_body(got_ref, out_ref):
+    for i in range(got_ref.shape[1]):
+        first, second = decay_of(got_ref[0, i, 2 * ROWS :, :]), decay_of(got_ref[1, i, 2 * ROWS :, :])
+        end = second * got_ref[0, i, :ROWS, :].astype(F32) + got_ref[1, i, :ROWS, :].astype(F32)
+        by_entry = got_ref[0, i, ROWS : 2 * ROWS, :].astype(F32) + first * got_ref[1, i, ROWS : 2 * ROWS, :].astype(F32)
+        out_ref[i, :ROWS, :] = end.astype(BF16)
+        out_ref[i, ROWS : 2 * ROWS, :] = by_entry.astype(BF16)
+        out_ref[i, 2 * ROWS :, :] = decay_rows(first * second)
 
 
 def scan_body(got_ref, out_ref):
     count = got_ref.shape[0]
-
-    def decay(j):
-        tail = got_ref[j, 2 * ROWS :, :].astype(F32)
-        return tail[0:1, :] + tail[1:2, :]
-
     state = jnp.zeros((ROWS, LANES), F32)
     for j in range(count):
         out_ref[j, :ROWS, :] = state.astype(BF16)
-        state = decay(j) * state + got_ref[j, :ROWS, :].astype(F32)
+        state = decay_of(got_ref[j, 2 * ROWS :, :]) * state + got_ref[j, :ROWS, :].astype(F32)
     state = jnp.zeros((ROWS, LANES), F32)
     for j in range(count - 1, -1, -1):
         out_ref[j, ROWS:, :] = state.astype(BF16)
-        state = decay(j) * state + got_ref[j, ROWS : 2 * ROWS, :].astype(F32)
+        state = decay_of(got_ref[j, 2 * ROWS :, :]) * state + got_ref[j, ROWS : 2 * ROWS, :].astype(F32)
+
+
+def part_body(got_ref, both_ref, out_ref):
+    for i in range(both_ref.shape[0]):
+        state, later = both_ref[i, :ROWS, :], both_ref[i, ROWS:, :]
+        first, second = decay_of(got_ref[0, i, 2 * ROWS :, :]), decay_of(got_ref[1, i, 2 * ROWS :, :])
+        out_ref[0, i, :ROWS, :] = state
+        out_ref[1, i, :ROWS, :] = (first * state.astype(F32) + got_ref[0, i, :ROWS, :].astype(F32)).astype(BF16)
+        out_ref[0, i, ROWS:, :] = (second * later.astype(F32) + got_ref[1, i, ROWS : 2 * ROWS, :].astype(F32)).astype(BF16)
+        out_ref[1, i, ROWS:, :] = later
 
 
 def inner_body(
-    x_ref, bc_ref, halo_ref, taps_ref, g_ref, rows_ref, cols_ref, xact_ref, bcact_ref, skip_ref,
+    x_ref, bc_ref, halo_ref, taps_ref, g_ref, rows_ref, cols_ref, bcact_ref, skip_ref,
     dx_ref, slope_ref, xw_ref, gw_ref, dbc_ref, slope2_ref, row_ref, ext_ref, ext2_ref,
 ):
     inner = x_ref.shape[1]
@@ -159,7 +197,7 @@
         pre = preact(ext, taps_ref, at, LANES)
         gate = jax.nn.sigmoid(pre)
         slope_ref[:, lanes] = gate * (1.0 + pre * (1.0 - gate))
-        act = xact_ref[:, lanes]
+        act = (pre * gate).astype(BF16)
         g = g_ref[:, lanes]
         wide = g.astype(F32)
         weight = pair_column(cols_ref, 2 * heads + 2 * i, 2 * heads + 2 * i + 1, left)
@@ -226,8 +264,8 @@
     for i in range(inner // LANES):
         at = i * LANES
         lanes = pl.ds(at, LANES)
-        state = states_ref[i, :ROWS, :]
-        later = states_ref[i, ROWS:, :]
+        state = states_ref[i % 2, i // 2, :ROWS, :]
+        later = states_ref[i % 2, i // 2, ROWS:, :]
         xw = xw_ref[:, lanes]
         gw = gw_ref[:, lanes]
         carried = dot(c, state) * gw.astype(F32)
@@ -289,35 +327,43 @@
     assert rows == ROWS and n_seq == pairs and bc.shape[1] == 2 * LANES and heads * 64 == inner
     tail = jnp.concatenate([x[rows - HALO :], bc[rows - HALO :]], 1)
     halo = lax.ppermute(tail, "seq", [(i, i + 1) for i in range(n_seq - 1)])
-    taps = jnp.concatenate([conv_weight, conv_bias[None]], 0)
-    by_row, by_col = call(
-        steps_body, [shape(6 * heads, ROWS), shape(ROWS, 4 * heads)], [VMEM, SMEM, SMEM]
-    )(step, step_bias, log_rate)
+    by_row, by_col, taps = call(
+        steps_body,
+        [kept(6 * heads, ROWS), kept(ROWS, 4 * heads), kept(5, inner + 2 * LANES)],
+        [FAR, FAR, FAR, SMEM, SMEM],
+    )(step, conv_weight, conv_bias, step_bias, log_rate)
     ext = [pltpu.VMEM((2, ROWS + HALO, LANES), F32)]
     ext2 = [pltpu.VMEM((ROWS + HALO, 2 * LANES), F32)]
-    x_act, bc_act, send = call(
+    bc_act, send = call(
         first_body,
-        [shape(rows, inner, dtype=BF16), shape(rows, 2 * LANES, dtype=BF16), shape(pairs, 2 * ROWS + 16, LANES, dtype=BF16)],
-        [VMEM] * 6,
+        [kept(rows, 2 * LANES, dtype=BF16), shape(2, pairs // 2, 2 * ROWS + 16, LANES, dtype=BF16)],
+        [FAR, FAR, VMEM, VMEM, FAR, VMEM],
         ext + ext2,
     )(x, bc, halo, taps, g, by_col)
-    got = lax.all_to_all(send, "seq", 0, 0)
+    chips = n_seq // 2
+    cores = [[2 * c, 2 * c + 1] for c in range(chips)]
+    ring = [[2 * c + k for c in range(chips)] for k in range(2)]
+    got = lax.all_to_all(send, "seq", 0, 0, axis_index_groups=cores)
+    joined = call(join_body, [shape(pairs // 2, 2 * ROWS + 16, LANES, dtype=BF16)], [VMEM])(got)[0]
+    joined = lax.all_to_all(joined, "seq", 0, 0, axis_index_groups=ring)
     dx, slope, xw, gw, dbc, slope2, row = call(
         inner_body,
         [
-            shape(rows, inner),
-            shape(rows, inner),
-            shape(rows, inner, dtype=BF16),
-            shape(rows, inner, dtype=BF16),
-            shape(rows, 2 * LANES),
-            shape(rows, 2 * LANES),
-            shape(3 * heads, ROWS),
+            kept(rows, inner),
+            kept(rows, inner),
+            kept(rows, inner, dtype=BF16),
+            kept(rows, inner, dtype=BF16),
+            kept(rows, 2 * LANES),
+            kept(rows, 2 * LANES),
+            kept(3 * heads, ROWS),
         ],
-        [VMEM] * 9 + [SMEM],
+        [VMEM] * 8 + [SMEM],
         ext + ext2,
-    )(x, bc, halo, taps, g, by_row, by_col, x_act, bc_act, skip_gain)
-    scanned = call(scan_body, [shape(n_seq, 2 * ROWS, LANES, dtype=BF16)], [VMEM])(got)[0]
-    states = lax.all_to_all(scanned, "seq", 0, 0)
+    )(x, bc, halo, taps, g, by_row, by_col, bc_act, skip_gain)
+    scanned = call(scan_body, [shape(chips, 2 * ROWS, LANES, dtype=BF16)], [VMEM])(joined)[0]
+    scanned = lax.all_to_all(scanned, "seq", 0, 0, axis_index_groups=ring)
+    parted = call(part_body, [shape(2, chips, 2 * ROWS, LANES, dtype=BF16)], [VMEM] * 2)(got, scanned)[0]
+    states = lax.all_to_all(parted, "seq", 0, 0, axis_index_groups=cores)
     gx, gbc, gstep, rim, part = call(
         last_body,
         [

time: 145 us -> 125 us (0.86)
  waiting for transfers between devices: 40.1 us -> 27.7 us
  Pallas kernels: 21.8 us -> 14 us
  local copies, waits for them, and re-layouts: 9.07 us -> 12.3 us
  blocking collectives: 39.8 us -> 37.1 us
    all_to_all x1, waiting for transfers between devices: 21.6 us -> 6.99 us  [on_device(): scanned = lax.all_to_all(scanned, 'seq', 0, 0, axis_index_groups=ring)]
    pallas_call x5 -> x7, Pallas kernels: 21.8 us -> 14 us  [call(): kernel(*(pltpu.with_memory_space_constraint(a, pltpu.VMEM if spec is VMEM...]
    unnamed x5 -> x37, local copies, waits for them, and re-layouts: 1.59 us -> 5.54 us
    all_to_all x1 -> x3, blocking collectives: 39.8 us -> 37.1 us  [the longest x1 26.2 us: on_device(): joined = lax.all_to_all(joined, 'seq', 0, 0, axis_index_groups=ring)]
    ppermute x1, waiting for transfers between devices: 0.01 us -> 2.25 us  [on_device(): halo = lax.ppermute(tail, 'seq', [(i, i + 1) for i in range(n_seq - 1)])]
  transfers between devices with their start and end apart: 6 -> 6, of which waited for: 4 -> 5; matrix products, arithmetic and copies ran while one was open for 5% -> 4% of each run, Pallas kernels for 6% -> 4%
where the time goes in v2:
time: 125 us; the launch traced here: 124 us
  blocking collectives  37.1 us (30%)
  starting transfers between devices  29.7 us (24%)
  waiting for transfers between devices  27.7 us (22%)
  Pallas kernels  14 us (11%)
  local copies, waits for them, and re-layouts  12.3 us (10%)
  other arithmetic  2.18 us (2%)
    all_to_all x1, blocking collectives, on_device(): joined = lax.all_to_all(joined, 'seq', 0, 0, axis_index_groups=ring)  26.2 us
    pallas_call x7, Pallas kernels, call(): kernel(*(pltpu.with_memory_space_constraint(a, pltpu.VMEM if spec is VMEM...  14 us
    all_to_all x1, starting transfers between devices, on_device(): lax.all_to_all(jnp.broadcast_to(mine[None], (n_dp, 8, LANES)), 'dp', 0, 0)  9.67 us
    all_to_all x1, waiting for transfers between devices, on_device(): scanned = lax.all_to_all(scanned, 'seq', 0, 0, axis_index_groups=ring)  6.99 us
    all_to_all x1, waiting for transfers between devices, on_device(): lax.all_to_all(jnp.broadcast_to(mine[None], (n_dp, 8, LANES)), 'dp', 0, 0)  6.94 us
    all_to_all x1, blocking collectives, on_device(): states = lax.all_to_all(parted, 'seq', 0, 0, axis_index_groups=cores)  6.16 us
    all_to_all x1, waiting for transfers between devices, on_device(): lax.all_to_all(jnp.broadcast_to(mean[None], (pairs, 8, LANES)), 'seq', 0, 0)  5.84 us
    all_to_all x1, waiting for transfers between devices, on_device(): mine = jnp.sum(lax.all_to_all(part, 'seq', 0, 0), 0)  5.69 us
  transfers between devices with their start and end apart: 6, of which 5 were waited for; matrix products, arithmetic and copies ran while one was open for 4% of the time, Pallas kernels for 4%

profile of v2, /device:TPU:1, one launch (start us, length us, event | category | flops | bytes accessed | tf_op | source)
XLA Modules:
  0.0 123.9 jit_solution(11051441008293396436)
XLA Ops:
  0.6 0.7 slice_bitcast_fusion.6
  1.3 0.8 slice_bitcast_fusion
  2.1 5.4 %collective-permute-start = (bf16[8,2304]{1,0:T(8,128)(2,1)S(1)}, bf16[8,2304]{1,0:T(8,128)(2,1)S(1)}, u32[]{:S(2)}, u32[]{:S(2)}) collective-permute-start(bf16[8,2304]{1,0:T(8,128)(2,1)S(1)} %pad_maximum_fusion.1), channel_id=1, source_target_pairs={{0,1},{1,2},{2,3},{3,4},{4,5},{5,6},{6,7},{7,8},{8,9},{9,10},{10,1... | collective-permute-start | bytes 110600 | tf_op jit(solution)/shard_map/ppermute | solution.py:329
  7.5 1.2 shard_map.152
  8.6 2.3 %collective-permute-done.halo_ref = bf16[8,2304]{1,0:T(8,128)(2,1)S(1)} collective-permute-done((bf16[8,2304]{1,0:T(8,128)(2,1)S(1)}, bf16[8,2304]{1,0:T(8,128)(2,1)S(1)}, u32[]{:S(2)}, u32[]{:S(2)}) %collective-permute-start) | collective-permute-done | bytes 36896 | tf_op jit(solution)/shard_map/ppermute | solution.py:329
  10.9 3.0 %shard_map.153 = (bf16[128,256]{1,0:T(8,128)(2,1)S(1)}, bf16[2,8,272,128]{3,2,1,0:T(8,128)(2,1)S(1)}) custom-call(bf16[128,2048]{1,0:T(8,128)(2,1)} %bitcast.35, bf16[128,256]{1,0:T(8,128)(2,1)} %bitcast.40, bf16[8,2304]{1,0:T(8,128)(2,1)S(1)} %collective-permute-done.halo_ref, f32[5,2304]{1,0:T(8,128)S(1)} %get-tuple-element.49.taps_ref, ...), custom_call_target="tpu_custom_call" | custom-call | tf_op jit(solution)/shard_map/pallas_call | solution.py:32
  13.9 0.0 copy-start.9
  13.9 4.8 %all_to_all.35.got_ref = bf16[2,8,272,128]{3,2,1,0:T(8,128)(2,1)S(1)} all-to-all(bf16[2,8,272,128]{3,2,1,0:T(8,128)(2,1)S(1)} %get-tuple-element.53), channel_id=1, replica_groups={{0,1},{2,3},{4,5},{6,7},{8,9},{10,11},{12,13},{14,15},{16,17},{18,19},{..., dimensions={0} | all-to-all | bytes 2228224 | tf_op jit(solution)/shard_map/all_to_all | solution.py:346
  18.7 0.2 shard_map.154
  18.9 26.2 %all_to_all.36.got_ref = bf16[8,272,128]{2,1,0:T(8,128)(2,1)S(1)} all-to-all(bf16[8,272,128]{2,1,0:T(8,128)(2,1)S(1)} %shard_map.154), channel_id=1, replica_groups={{0,2,4,6,8,10,12,14},{1,3,5,7,9,11,13,15},{16,18,20,22,24,26,28,30},{17..., dimensions={0} | all-to-all | bytes 1114112 | tf_op jit(solution)/shard_map/all_to_all | solution.py:348
  45.0 0.9 shard_map.155
  45.9 3.5 %all-to-all-start.2 = ((bf16[8,256,128]{2,1,0:T(8,128)(2,1)}), bf16[8,256,128]{2,1,0:T(8,128)(2,1)S(1)}, u32[]{:S(2)}, u32[]{:S(2)}) async-start(bf16[8,256,128]{2,1,0:T(8,128)(2,1)} %shard_map.155), calls=%async_computation.2 | async-start | bytes 1048576 | tf_op jit(solution)/shard_map/all_to_all | solution.py:364
  49.5 0.0 copy-start.10
  49.5 0.8 copy-done.10
  50.3 4.0 %shard_map.157 = (f32[128,2048]{1,0:T(8,128)S(1)}, f32[128,2048]{1,0:T(8,128)S(1)}, bf16[128,2048]{1,0:T(8,128)(2,1)S(1)}, bf16[128,2048]{1,0:T(8,128)(2,1)S(1)}...) custom-call(bf16[128,2048]{1,0:T(8,128)(2,1)S(1)} %bitcast.36, ...), custom_call_target="tpu_custom_call" | custom-call | tf_op jit(solution)/shard_map/pallas_call | solution.py:32
  54.3 1.0 copy-done.2
  55.3 0.9 copy-done.4
  56.3 0.8 copy-done.7
  57.1 0.7 copy-done.12
  57.7 0.6 copy-done.14
  58.4 0.6 copy-done.16
  59.0 7.0 %all-to-all-done.2.both_ref = bf16[8,256,128]{2,1,0:T(8,128)(2,1)S(1)} async-done(((bf16[8,256,128]{2,1,0:T(8,128)(2,1)}), bf16[8,256,128]{2,1,0:T(8,128)(2,1)S(1)}, u32[]{:S(2)}, u32[]{:S(2)}) %all-to-all-start.2) | async-done | bytes 524320 | tf_op jit(solution)/shard_map/all_to_all | solution.py:364
  66.0 0.0 copy-start.17
  66.0 0.2 shard_map.156
  66.2 6.2 %all_to_all.37.states_ref = bf16[2,8,256,128]{3,2,1,0:T(8,128)(2,1)S(1)} all-to-all(bf16[2,8,256,128]{3,2,1,0:T(8,128)(2,1)S(1)} %shard_map.156), channel_id=1, replica_groups={{0,1},{2,3},{4,5},{6,7},{8,9},{10,11},{12,13},{14,15},{16,17},{18,19},{..., dimensions={0} | all-to-all | bytes 2097152 | tf_op jit(solution)/shard_map/all_to_all | solution.py:366
  72.4 0.0 copy-done.15
  72.4 0.0 copy-done.17
  72.4 0.0 copy-done.3
  72.4 0.0 copy-done.5
  72.4 4.6 %shard_map.158 = (bf16[128,2048]{1,0:T(8,128)(2,1)}, bf16[128,256]{1,0:T(8,128)(2,1)}, f32[32,128]{1,0:T(8,128)}, bf16[8,2304]{1,0:T(8,128)(2,1)S(1)}, f32[16,8,128]{2,1,0:T(8,128)}) custom-call(bf16[128,2048]{1,0:T(8,128)(2,1)S(1)} %bitcast.37, bf16[128,256]{1,0:T(8,128)(2,1)S(1)} %bitcast.42, bf16[8,2304]{1,0:T(8,128)(2,1)S(1)} %collective-permute-done.halo_ref, ...), custom_call_target="tpu_custom_call" | custom-call | tf_op jit(solution)/shard_map/pallas_call | solution.py:32
  77.0 3.7 %all-to-all-start.4 = ((f32[16,8,128]{2,1,0:T(8,128)}), f32[16,8,128]{2,1,0:T(8,128)S(1)}, u32[]{:S(2)}, u32[]{:S(2)}) async-start(f32[16,8,128]{2,1,0:T(8,128)} %get-tuple-element.65), calls=%async_computation.4 | async-start | bytes 131072 | tf_op jit(solution)/shard_map/all_to_all | solution.py:383
  80.7 2.1 %collective-permute-start.1 = (bf16[8,2304]{1,0:T(8,128)(2,1)S(1)}, bf16[8,2304]{1,0:T(8,128)(2,1)S(1)}, u32[]{:S(2)}, u32[]{:S(2)}) collective-permute-start(bf16[8,2304]{1,0:T(8,128)(2,1)S(1)} %get-tuple-element.62), channel_id=1, source_target_pairs={{1,0},{2,1},{3,2},{4,3},{5,4},{6,5},{7,6},{8,7},{9,8},{10,9},{11,1... | collective-permute-start | bytes 110600 | tf_op jit(solution)/shard_map/ppermute | solution.py:382
  82.8 5.7 %all-to-all-done.4 = f32[16,8,128]{2,1,0:T(8,128)S(1)} async-done(((f32[16,8,128]{2,1,0:T(8,128)}), f32[16,8,128]{2,1,0:T(8,128)S(1)}, u32[]{:S(2)}, u32[]{:S(2)}) %all-to-all-start.4) | async-done | bytes 65568 | tf_op jit(solution)/shard_map/all_to_all | solution.py:383
  88.5 0.7 broadcast_in_dim.30
  89.2 9.7 %all-to-all-start.5 = ((f32[32,8,128]{2,1,0:T(8,128)}), f32[32,8,128]{2,1,0:T(8,128)S(1)}, u32[]{:S(2)}, u32[]{:S(2)}) async-start(f32[32,8,128]{2,1,0:T(8,128)} %broadcast_in_dim.30), calls=%async_computation.5 | async-start | bytes 262144 | tf_op jit(solution)/shard_map/all_to_all | solution.py:384
  98.9 0.0 collective-permute-done.1
  98.9 0.8 fusion
  99.6 1.4 %scatter-add.6 = bf16[1,128,2048]{2,1,0:T(8,128)(2,1)} dynamic-update-slice(bf16[1,128,2048]{2,1,0:T(8,128)(2,1)} %bitcast.44, bf16[1,3,2048]{2,1,0:T(4,128)(2,1)S(1)} %fusion, s32[]{:T(128)} %constant.52.clone.1, s32[]{:T(128)} %constant.53.clone.1, s32[]{:T(128)} %constant.52.clone.1) | dynamic-update-slice | bytes 24580 | tf_op jit(solution)/shard_map/scatter-add | solution.py:387
  101.1 6.9 %all-to-all-done.5 = f32[32,8,128]{2,1,0:T(8,128)S(1)} async-done(((f32[32,8,128]{2,1,0:T(8,128)}), f32[32,8,128]{2,1,0:T(8,128)S(1)}, u32[]{:S(2)}, u32[]{:S(2)}) %all-to-all-start.5) | async-done | bytes 131104 | tf_op jit(solution)/shard_map/all_to_all | solution.py:384
  108.0 0.6 broadcast_in_dim.31
  108.7 5.4 %all-to-all-start.6 = ((f32[16,8,128]{2,1,0:T(8,128)}), f32[16,8,128]{2,1,0:T(8,128)S(1)}, u32[]{:S(2)}, u32[]{:S(2)}) async-start(f32[16,8,128]{2,1,0:T(8,128)} %broadcast_in_dim.31), calls=%async_computation.6 | async-start | bytes 131072 | tf_op jit(solution)/shard_map/all_to_all | solution.py:386
  114.1 0.7 fusion.1
  114.7 1.3 %scatter-add.9 = bf16[1,128,256]{2,1,0:T(8,128)(2,1)} dynamic-update-slice(bf16[1,128,256]{2,1,0:T(8,128)(2,1)} %bitcast.45, bf16[1,3,256]{2,1,0:T(4,128)(2,1)S(1)} %fusion.1, s32[]{:T(128)} %constant.52.clone.1, s32[]{:T(128)} %constant.53.clone.1, s32[]{:T(128)} %constant.52.clone.1) | dynamic-update-slice | bytes 3076 | tf_op jit(solution)/shard_map/scatter-add | solution.py:388
  116.0 5.8 %all-to-all-done.6 = f32[16,8,128]{2,1,0:T(8,128)S(1)} async-done(((f32[16,8,128]{2,1,0:T(8,128)}), f32[16,8,128]{2,1,0:T(8,128)S(1)}, u32[]{:S(2)}, u32[]{:S(2)}) %all-to-all-start.6) | async-done | bytes 65568 | tf_op jit(solution)/shard_map/all_to_all | solution.py:386
  121.9 0.1 concatenate.14
  122.0 0.6 maximum_reduce_fusion
  122.6 0.6 slice.137
  123.3 0.6 slice_bitcast_fusion.7
  (30 shorter events, 0.2 us)
Async XLA Ops:
  2.1 8.8 %collective-permute-start = (bf16[8,2304]{1,0:T(8,128)(2,1)S(1)}, bf16[8,2304]{1,0:T(8,128)(2,1)S(1)}, u32[]{:S(2)}, u32[]{:S(2)}) collective-permute-start(bf16[8,2304]{1,0:T(8,128)(2,1)S(1)} %pad_maximum_fusion.1), channel_id=1, source_target_pairs={{0,1},{1,2},{2,3},{3,4},{4,5},{5,6},{6,7},{7,8},{8,9},{9,10},{10,1... | collective-permute-start | bytes 110600 | tf_op jit(solution)/shard_map/ppermute | solution.py:329
  13.9 4.8 %copy-start.9 = (bf16[128,256]{1,0:T(8,128)(2,1)}, bf16[128,256]{1,0:T(8,128)(2,1)S(1)}, u32[]{:S(2)}) copy-start(bf16[128,256]{1,0:T(8,128)(2,1)S(1)} %get-tuple-element.52.bcact_ref) | copy-start | bytes 196612
  45.0 4.4 %copy-start = (bf16[1,128,2048]{2,1,0:T(8,128)(2,1)S(1)}, bf16[1,128,2048]{2,1,0:T(8,128)(2,1)}, u32[]{:S(2)}) copy-start(bf16[1,128,2048]{2,1,0:T(8,128)(2,1)} %param.13) | copy-start | bytes 1572868
  45.0 4.4 %copy-start.1 = (bf16[1,128,2048]{2,1,0:T(8,128)(2,1)S(1)}, bf16[1,128,2048]{2,1,0:T(8,128)(2,1)}, u32[]{:S(2)}) copy-start(bf16[1,128,2048]{2,1,0:T(8,128)(2,1)} %param.21) | copy-start | bytes 1572868
  45.0 4.4 %copy-start.6 = (bf16[1,128,256]{2,1,0:T(8,128)(2,1)S(1)}, bf16[1,128,256]{2,1,0:T(8,128)(2,1)}, u32[]{:S(2)}) copy-start(bf16[1,128,256]{2,1,0:T(8,128)(2,1)} %param.14) | copy-start | bytes 196612
  45.9 20.0 %all-to-all-start.2 = ((bf16[8,256,128]{2,1,0:T(8,128)(2,1)}), bf16[8,256,128]{2,1,0:T(8,128)(2,1)S(1)}, u32[]{:S(2)}, u32[]{:S(2)}) async-start(bf16[8,256,128]{2,1,0:T(8,128)(2,1)} %shard_map.155), calls=%async_computation.2 | async-start | bytes 1048576 | tf_op jit(solution)/shard_map/all_to_all | solution.py:364
  49.5 0.8 copy-start.10
  54.3 1.0 copy-start.2
  55.3 0.9 copy-start.4
  56.3 0.8 copy-start.7
  57.1 0.7 copy-start.12
  57.7 0.6 copy-start.14
  58.4 0.6 copy-start.16
  66.0 6.4 %copy-start.8 = (bf16[128,2048]{1,0:T(8,128)(2,1)S(1)}, bf16[128,2048]{1,0:T(8,128)(2,1)}, u32[]{:S(2)}) copy-start(bf16[128,2048]{1,0:T(8,128)(2,1)} %copy-done.7) | copy-start | bytes 1572868
  66.0 6.4 %copy-start.11 = (bf16[128,256]{1,0:T(8,128)(2,1)S(1)}, bf16[128,256]{1,0:T(8,128)(2,1)}, u32[]{:S(2)}) copy-start(bf16[128,256]{1,0:T(8,128)(2,1)} %copy-done.9) | copy-start | bytes 196612
  66.0 6.4 %copy-start.13 = (f32[128,256]{1,0:T(8,128)S(1)}, f32[128,256]{1,0:T(8,128)}, u32[]{:S(2)}) copy-start(f32[128,256]{1,0:T(8,128)} %copy-done.12) | copy-start | bytes 393220
  66.0 6.4 %copy-start.15 = (f32[128,256]{1,0:T(8,128)S(1)}, f32[128,256]{1,0:T(8,128)}, u32[]{:S(2)}) copy-start(f32[128,256]{1,0:T(8,128)} %copy-done.14) | copy-start | bytes 393220
  66.0 6.4 %copy-start.17 = (f32[96,128]{1,0:T(8,128)S(1)}, f32[96,128]{1,0:T(8,128)}, u32[]{:S(2)}) copy-start(f32[96,128]{1,0:T(8,128)} %copy-done.16) | copy-start | bytes 147460
  66.2 6.2 %copy-start.3 = (f32[128,2048]{1,0:T(8,128)S(1)}, f32[128,2048]{1,0:T(8,128)}, u32[]{:S(2)}) copy-start(f32[128,2048]{1,0:T(8,128)} %copy-done.2) | copy-start | bytes 3145732
  66.2 6.2 %copy-start.5 = (f32[128,2048]{1,0:T(8,128)S(1)}, f32[128,2048]{1,0:T(8,128)}, u32[]{:S(2)}) copy-start(f32[128,2048]{1,0:T(8,128)} %copy-done.4) | copy-start | bytes 3145732
  77.0 11.5 %all-to-all-start.4 = ((f32[16,8,128]{2,1,0:T(8,128)}), f32[16,8,128]{2,1,0:T(8,128)S(1)}, u32[]{:S(2)}, u32[]{:S(2)}) async-start(f32[16,8,128]{2,1,0:T(8,128)} %get-tuple-element.65), calls=%async_computation.4 | async-start | bytes 131072 | tf_op jit(solution)/shard_map/all_to_all | solution.py:383
  80.7 18.2 %collective-permute-start.1 = (bf16[8,2304]{1,0:T(8,128)(2,1)S(1)}, bf16[8,2304]{1,0:T(8,128)(2,1)S(1)}, u32[]{:S(2)}, u32[]{:S(2)}) collective-permute-start(bf16[8,2304]{1,0:T(8,128)(2,1)S(1)} %get-tuple-element.62), channel_id=1, source_target_pairs={{1,0},{2,1},{3,2},{4,3},{5,4},{6,5},{7,6},{8,7},{9,8},{10,9},{11,1... | collective-permute-start | bytes 110600 | tf_op jit(solution)/shard_map/ppermute | solution.py:382
  89.2 18.8 %all-to-all-start.5 = ((f32[32,8,128]{2,1,0:T(8,128)}), f32[32,8,128]{2,1,0:T(8,128)S(1)}, u32[]{:S(2)}, u32[]{:S(2)}) async-start(f32[32,8,128]{2,1,0:T(8,128)} %broadcast_in_dim.30), calls=%async_computation.5 | async-start | bytes 262144 | tf_op jit(solution)/shard_map/all_to_all | solution.py:384
  108.7 13.2 %all-to-all-start.6 = ((f32[16,8,128]{2,1,0:T(8,128)}), f32[16,8,128]{2,1,0:T(8,128)S(1)}, u32[]{:S(2)}, u32[]{:S(2)}) async-start(f32[16,8,128]{2,1,0:T(8,128)} %broadcast_in_dim.31), calls=%async_computation.6 | async-start | bytes 131072 | tf_op jit(solution)/shard_map/all_to_all | solution.py:386

commit v3 on v2

v3 whole, which is shorter than its diff:
```python
import jax
import jax.numpy as jnp
from jax import lax
from jax.experimental import pallas as pl
from jax.experimental.pallas import tpu as pltpu
from jax.sharding import PartitionSpec as P


HIGH = lax.Precision.HIGHEST
F32 = jnp.float32
BF16 = jnp.bfloat16
ROWS = 128
LANES = 128
HALO = 8
PAIRS = 8
HEADS = 16
HALF = PAIRS * LANES
SEG = 2 * ROWS
G_AT, B_AT, C_AT, STEP_AT = HALF, 2 * HALF, 2 * HALF + ROWS, 2 * HALF + 2 * ROWS
SIDE_AT = STEP_AT + 3 * HEADS
PACKED = SIDE_AT + 16
SENT = 2 * ROWS + 16
VMEM = pl.BlockSpec(memory_space=pltpu.VMEM)
FAR = pl.BlockSpec(memory_space=pltpu.VMEM)
SMEM = pl.BlockSpec(memory_space=pltpu.SMEM)
INTERPRET = False
NT = ((1,), (1,))
TN = ((0,), (0,))


def call(body, outs, ins, scratch=()):
    kernel = pl.pallas_call(
        body,
        out_shape=outs,
        in_specs=ins,
        out_specs=[VMEM] * len(outs),
        scratch_shapes=list(scratch),
        compiler_params=pltpu.CompilerParams(vmem_limit_bytes=16 << 20),
        interpret=INTERPRET,
    )
    if INTERPRET:
        return kernel
    return lambda *given: kernel(
        *(
            pltpu.with_memory_space_constraint(a, pltpu.VMEM if spec is VMEM else pltpu.HBM)
            for a, spec in zip(given, ins, strict=True)
        )
    )


def shape(*dims, dtype=F32):
    return jax.ShapeDtypeStruct(dims, dtype)


def far(*dims, dtype=F32):
    return shape(*dims, dtype=dtype) if INTERPRET else pltpu.HBM(dims, dtype)


def kept(*dims, dtype=F32):
    return shape(*dims, dtype=dtype) if INTERPRET else pltpu.VMEM(dims, dtype)


def dot(a, b, dims=((1,), (0,)), precision=None):
    return lax.dot_general(a, b, (dims, ((), ())), precision=precision, preferred_element_type=F32)


def iota(dims, axis):
    return lax.broadcasted_iota(jnp.int32, dims, axis)


def pack_body(x_ref, bc_ref, g_ref, step_ref, out_ref):
    bc = bc_ref[...]
    for q in range(2):
        for o in range(PAIRS):
            at = q * HALF + o * LANES
            out_ref[q, o * ROWS : (o + 1) * ROWS, :] = x_ref[:, at : at + LANES]
            out_ref[q, G_AT + o * ROWS : G_AT + (o + 1) * ROWS, :] = g_ref[:, at : at + LANES]
        out_ref[q, B_AT : B_AT + ROWS, :] = bc[:, :LANES]
        out_ref[q, C_AT : C_AT + ROWS, :] = bc[:, LANES:]
        rest = step_ref[q * HEADS : (q + 1) * HEADS, :]
        for k in range(3):
            piece = rest.astype(BF16)
            rest = rest - piece.astype(F32)
            out_ref[q, STEP_AT + k * HEADS : STEP_AT + (k + 1) * HEADS, :] = piece
        out_ref[q, SIDE_AT:, :] = jnp.full((16, LANES), float(q), F32).astype(BF16)


def tail_body(got_ref, out_ref):
    for o in range(PAIRS):
        out_ref[o, :, :] = got_ref[1, (o + 1) * ROWS - HALO : (o + 1) * ROWS, :]
    out_ref[PAIRS, :, :] = got_ref[1, B_AT + ROWS - HALO : B_AT + ROWS, :]
    out_ref[PAIRS + 1, :, :] = got_ref[1, C_AT + ROWS - HALO : C_AT + ROWS, :]


def head_rows(ref, second):
    rows = iota((2 * HEADS, LANES), 0) % HEADS
    out = jnp.zeros((2 * HEADS, LANES), F32)
    for h in range(HEADS):
        out = jnp.where(rows == h, jnp.where(second, ref[HEADS + h], ref[h]), out)
    return out


def steps_body(got_ref, weight_ref, offset_ref, bias_ref, rate_ref, skip_ref, rows_ref, cols_ref, taps_ref, side_ref):
    side = got_ref[0, SIDE_AT:, :].astype(F32)[:8]
    side_ref[...] = side
    second = side[:1] > 0.5
    offset = offset_ref[...].reshape(1, -1)
    inner = 2 * HALF
    for o in range(PAIRS):
        at = o * LANES
        lanes = slice(at, at + LANES)
        other = slice(HALF + at, HALF + at + LANES)
        taps_ref[:4, lanes] = jnp.where(second, weight_ref[:, other], weight_ref[:, lanes])
        taps_ref[4:5, lanes] = jnp.where(second, offset[:, other], offset[:, lanes])
    taps_ref[:4, HALF:] = weight_ref[:, inner:]
    taps_ref[4:5, HALF:] = offset[:, inner:]
    n = 2 * HEADS
    raw = [
        sum(got_ref[r, STEP_AT + k * HEADS : STEP_AT + (k + 1) * HEADS, :].astype(F32) for k in (2, 1, 0)) for r in range(2)
    ]
    second = jnp.broadcast_to(second, (n, LANES))
    raw = jnp.concatenate(raw, 0) + head_rows(bias_ref, second)
    step = jnp.maximum(raw, 0.0) + jnp.log1p(jnp.exp(-jnp.abs(raw)))
    rate = -jnp.exp(head_rows(rate_ref, second))
    upto = (iota((ROWS, ROWS), 0) <= iota((ROWS, ROWS), 1)).astype(F32)
    cumul = dot(rate * step, upto, precision=HIGH)
    weight = jnp.exp(cumul[:, ROWS - 1 :] - cumul) * step
    fade = jnp.exp(cumul)
    stack = jnp.concatenate([cumul, step, weight, fade], 0)
    rows_ref[: 4 * n, :] = stack
    rows_ref[4 * n : 5 * n, :] = jax.nn.sigmoid(raw)
    rows_ref[5 * n : 6 * n, :] = rate
    rows_ref[6 * n :, :] = head_rows(skip_ref, second)
    cols_ref[...] = stack.T


def head_of(r, o):
    return r * HEADS + 2 * o


def fill(ext_ref, halo, first, second):
    ext_ref[:HALO, :] = halo.astype(F32)
    ext_ref[HALO : HALO + ROWS, :] = first.astype(F32)
    ext_ref[HALO + ROWS :, :] = second.astype(F32)


def fill_pair(ext_ref, got_ref, halo_ref, o):
    rows = slice(o * ROWS, (o + 1) * ROWS)
    fill(ext_ref, halo_ref[o], got_ref[0, rows, :], got_ref[1, rows, :])


def fill_bc(ext2_ref, got_ref, halo_ref):
    for k, at in enumerate((B_AT, C_AT)):
        lanes = slice(k * LANES, (k + 1) * LANES)
        fill(ext2_ref.at[:, lanes], halo_ref[PAIRS + k], got_ref[0, at : at + ROWS, :], got_ref[1, at : at + ROWS, :])


def preact(ext_ref, taps_ref, at, lanes):
    acc = taps_ref[4:5, at : at + lanes]
    for k in range(4):
        acc = acc + taps_ref[k : k + 1, at : at + lanes] * ext_ref[pl.ds(HALO - 3 + k, SEG), :]
    return acc


def pair_column(cols_ref, which, r, o, left):
    at = which * 2 * HEADS + head_of(r, o)
    a = jnp.broadcast_to(cols_ref[:, at : at + 1], (ROWS, LANES))
    b = jnp.broadcast_to(cols_ref[:, at + 1 : at + 2], (ROWS, LANES))
    return jnp.where(left, a, b)


def decay_of(tail):
    tail = tail.astype(F32)
    return tail[0:1, :] + tail[1:2, :]


def decay_rows(total):
    high = total.astype(BF16).astype(F32)
    row = iota((16, LANES), 0)
    return jnp.where(row == 0, high, jnp.where(row == 1, total - high, 0.0)).astype(BF16)


def first_body(got_ref, halo_ref, taps_ref, cols_ref, bcact_ref, near_ref, send_ref, ext_ref, ext2_ref):
    fill_bc(ext2_ref, got_ref, halo_ref)
    pre = preact(ext2_ref, taps_ref, HALF, 2 * LANES)
    bc = pre * jax.nn.sigmoid(pre)
    bcact_ref[...] = bc.astype(BF16)
    bc = bc.astype(BF16).astype(F32)
    b_t = [bc[r * ROWS : (r + 1) * ROWS, :LANES].T.astype(BF16) for r in range(2)]
    c_t = [bc[r * ROWS : (r + 1) * ROWS, LANES:].T.astype(BF16) for r in range(2)]
    left = iota((ROWS, LANES), 1) < 64
    for o in range(PAIRS):
        ext = ext_ref.at[o % 2]
        fill_pair(ext, got_ref, halo_ref, o)
        pre = preact(ext, taps_ref, o * LANES, LANES)
        act = (pre * jax.nn.sigmoid(pre)).astype(BF16).astype(F32)
        ends, backs, totals = [], [], []
        for r in range(2):
            fade = pair_column(cols_ref, 3, r, o, left)
            xw = (act[r * ROWS : (r + 1) * ROWS] * pair_column(cols_ref, 2, r, o, left)).astype(BF16)
            gw = (got_ref[r, G_AT + o * ROWS : G_AT + (o + 1) * ROWS, :].astype(F32) * fade).astype(BF16)
            ends.append(dot(b_t[r], xw))
            backs.append(dot(c_t[r], gw))
            totals.append(fade[ROWS - 1 :, :])
        near_ref[o, :ROWS, :] = ends[0].astype(BF16)
        near_ref[o, ROWS:, :] = backs[1].astype(BF16)
        send_ref[o, :ROWS, :] = (totals[1] * ends[0] + ends[1]).astype(BF16)
        send_ref[o, ROWS : 2 * ROWS, :] = (backs[0] + totals[0] * backs[1]).astype(BF16)
        send_ref[o, 2 * ROWS :, :] = decay_rows(totals[0] * totals[1])


def scan_body(got_ref, out_ref):
    count = got_ref.shape[0]
    state = jnp.zeros((ROWS, LANES), F32)
    for j in range(count):
        out_ref[j, :ROWS, :] = state.astype(BF16)
        state = decay_of(got_ref[j, 2 * ROWS :, :]) * state + got_ref[j, :ROWS, :].astype(F32)
    state = jnp.zeros((ROWS, LANES), F32)
    for j in range(count - 1, -1, -1):
        out_ref[j, ROWS:, :] = state.astype(BF16)
        state = decay_of(got_ref[j, 2 * ROWS :, :]) * state + got_ref[j, ROWS : 2 * ROWS, :].astype(F32)


def inner_body(
    got_ref, halo_ref, taps_ref, rows_ref, cols_ref, bcact_ref,
    dx_ref, slope_ref, xw_ref, gw_ref, dbc_ref, slope2_ref, row_ref, ext_ref, ext2_ref,
):
    n = 2 * HEADS
    fill_bc(ext2_ref, got_ref, halo_ref)
    pre = preact(ext2_ref, taps_ref, HALF, 2 * LANES)
    gate = jax.nn.sigmoid(pre)
    slope2_ref[...] = gate * (1.0 + pre * (1.0 - gate))
    causal = iota((ROWS, ROWS), 0) <= iota((ROWS, ROWS), 1)
    left = iota((ROWS, LANES), 1) < 64
    ones = jnp.ones((8, ROWS), BF16)
    b = [bcact_ref[r * ROWS : (r + 1) * ROWS, :LANES] for r in range(2)]
    c = [bcact_ref[r * ROWS : (r + 1) * ROWS, LANES:] for r in range(2)]
    scores = [dot(b[r], c[r], NT) for r in range(2)]
    dscores = [jnp.zeros((ROWS, ROWS), F32) for _ in range(2)]
    for o in range(PAIRS):
        ext = ext_ref.at[o % 2]
        fill_pair(ext, got_ref, halo_ref, o)
        pre = preact(ext, taps_ref, o * LANES, LANES)
        gate = jax.nn.sigmoid(pre)
        slope_ref[o] = gate * (1.0 + pre * (1.0 - gate))
        whole = (pre * gate).astype(BF16)
        for r in range(2):
            h = head_of(r, o)
            rows = slice(r * ROWS, (r + 1) * ROWS)
            act = whole[rows]
            wide = got_ref[r, G_AT + o * ROWS : G_AT + (o + 1) * ROWS, :].astype(F32)
            xw_ref[o, rows] = (act.astype(F32) * pair_column(cols_ref, 2, r, o, left)).astype(BF16)
            gw_ref[o, rows] = (wide * pair_column(cols_ref, 3, r, o, left)).astype(BF16)
            skip = jnp.where(left[:1], rows_ref[6 * n + h : 6 * n + h + 1, :], rows_ref[6 * n + h + 1 : 6 * n + h + 2, :])
            dx = skip * wide
            both = jnp.sum(act.astype(F32) * wide, 0, keepdims=True)
            row_ref[2 * n + h : 2 * n + h + 1, :] = jnp.where(left[:1], both, 0.0)
            row_ref[2 * n + h + 1 : 2 * n + h + 2, :] = jnp.where(left[:1], 0.0, both)
            for k in range(2):
                own = jnp.where(left if k == 0 else ~left, wide, 0.0).astype(BF16)
                gap = rows_ref[h + k : h + k + 1, :] - cols_ref[:, h + k : h + k + 1]
                fall = jnp.exp(jnp.where(causal, gap, -1e30)) * cols_ref[:, n + h + k : n + h + k + 1]
                mixing = scores[r] * fall
                dmix = dot(act, own, NT).astype(BF16).astype(F32)
                dscores[r] = dscores[r] + dmix * fall
                both = (dmix * mixing).astype(BF16)
                row_ref[h + k : h + k + 1, :] = dot(ones, both)[:1]
                row_ref[n + h + k : n + h + k + 1, :] = dot(ones, both, NT)[:1]
                dx = dx + dot(mixing.astype(BF16), own)
            dx_ref[o, rows] = dx
    for r in range(2):
        ds = dscores[r].astype(BF16)
        dbc_ref[r * ROWS : (r + 1) * ROWS, :LANES] = dot(ds, c[r])
        dbc_ref[r * ROWS : (r + 1) * ROWS, LANES:] = dot(ds, b[r], TN)


def tap_sums(dpre, ext_ref):
    sums = [jnp.sum(dpre * ext_ref[pl.ds(HALO - 3 + k, SEG), :], 0, keepdims=True) for k in range(4)]
    return sums + [jnp.sum(dpre, 0, keepdims=True)]


def last_body(
    got_ref, halo_ref, rows_ref, cols_ref, bcact_ref, side_ref, states_ref,
    near_ref, dx_ref, slope_ref, xw_ref, gw_ref, dbc_ref, slope2_ref, row_ref,
    dpre_ref, gstep_ref, part_ref, ext_ref, ext2_ref, acc_ref,
):
    n = 2 * HEADS
    left = iota((ROWS, LANES), 1) < 64
    half = jnp.where((iota((8, LANES), 1) < 64) == (iota((8, LANES), 0) == 0), 1.0, 0.0).astype(BF16)
    b = [bcact_ref[r * ROWS : (r + 1) * ROWS, :LANES] for r in range(2)]
    c = [bcact_ref[r * ROWS : (r + 1) * ROWS, LANES:] for r in range(2)]
    db = [jnp.zeros((ROWS, LANES), F32) for _ in range(2)]
    dc = [jnp.zeros((ROWS, LANES), F32) for _ in range(2)]
    part_ref[...] = jnp.zeros(part_ref.shape, F32)
    pad = jnp.zeros((HALO, HALF + 2 * LANES), F32)
    dpre_ref[:HALO, :] = pad
    dpre_ref[HALO + SEG :, :] = pad
    for o in range(PAIRS):
        lanes = slice(o * LANES, (o + 1) * LANES)
        state, later = states_ref[o, :ROWS, :], states_ref[o, ROWS:, :]
        total = []
        for r in range(2):
            h = 3 * n + head_of(r, o)
            total.append(jnp.where(left[:1], cols_ref[ROWS - 1 :, h : h + 1], cols_ref[ROWS - 1 :, h + 1 : h + 2]))
        states = [state, (total[0] * state.astype(F32) + near_ref[o, :ROWS, :].astype(F32)).astype(BF16)]
        laters = [(total[1] * later.astype(F32) + near_ref[o, ROWS:, :].astype(F32)).astype(BF16), later]
        ext = ext_ref.at[o % 2]
        fill_pair(ext, got_ref, halo_ref, o)
        for r in range(2):
            rows = slice(r * ROWS, (r + 1) * ROWS)
            h = head_of(r, o)
            xw = xw_ref[o, rows]
            gw = gw_ref[o, rows]
            carried = dot(c[r], states[r]) * gw.astype(F32)
            dxw = dot(b[r], laters[r]).astype(BF16).astype(F32)
            dc[r] = dc[r] + dot(gw, states[r], NT)
            db[r] = db[r] + dot(xw, laters[r], NT)
            acc_ref[h : h + 2, :] = dot(half, carried.astype(BF16), NT)[:2]
            acc_ref[n + h : n + h + 2, :] = dot(half, (dxw * xw.astype(F32)).astype(BF16), NT)[:2]
            both = jnp.sum(states[r].astype(F32) * laters[r].astype(F32), 0, keepdims=True)
            acc_ref[2 * n + h : 2 * n + h + 1, :] = jnp.where(left[:1], both, 0.0)
            acc_ref[2 * n + h + 1 : 2 * n + h + 2, :] = jnp.where(left[:1], 0.0, both)
            dact = dx_ref[o, rows] + pair_column(cols_ref, 2, r, o, left) * dxw
            dpre_ref[HALO + r * ROWS : HALO + (r + 1) * ROWS, lanes] = dact.astype(BF16).astype(F32) * slope_ref[o, rows]
        sums = tap_sums(dpre_ref[HALO : HALO + SEG, lanes], ext)
        for k in range(5):
            part_ref[o, k : k + 1, :] = sums[k]
    fill_bc(ext2_ref, got_ref, halo_ref)
    dpre2 = jnp.concatenate([jnp.concatenate(db, 0), jnp.concatenate(dc, 0)], 1)
    dpre2 = (dbc_ref[...] + dpre2) * slope2_ref[...]
    dpre_ref[HALO : HALO + SEG, HALF:] = dpre2
    sums = tap_sums(dpre2, ext2_ref)
    for k in range(5):
        part_ref[k, 5:6, :] = sums[k][:, :LANES]
        part_ref[k, 6:7, :] = sums[k][:, LANES:]
    step = rows_ref[n : 2 * n, :]
    gate = rows_ref[4 * n : 5 * n, :]
    rate = rows_ref[5 * n : 6 * n, :]
    total = rows_ref[3 * n : 4 * n, ROWS - 1 :]
    at_t = row_ref[:n, :]
    at_s = row_ref[n : 2 * n, :]
    ended = acc_ref[n : 2 * n, :]
    at_end = jnp.sum(ended, 1, keepdims=True) + total * jnp.sum(acc_ref[2 * n :, :], 1, keepdims=True)
    final = iota((n, ROWS), 1) == ROWS - 1
    dcumul = at_t - at_s + acc_ref[:n, :] - ended + jnp.where(final, at_end, 0.0)
    onward = (iota((ROWS, ROWS), 0) >= iota((ROWS, ROWS), 1)).astype(F32)
    ddecay = dot(dcumul, onward, precision=HIGH)
    dstep = ((at_s + ended) / step + ddecay * rate) * gate
    gstep_ref[...] = dstep
    dbias = jnp.sum(dstep, 1, keepdims=True)
    drate = jnp.sum(ddecay * rate * step, 1, keepdims=True)
    dskip = jnp.sum(row_ref[2 * n :, :], 1, keepdims=True)
    second = jnp.broadcast_to(side_ref[:1] > 0.5, (n, LANES))
    at = iota((n, LANES), 1) - iota((n, LANES), 0) % HEADS - jnp.where(second, HEADS, 0)
    placed = jnp.where(at == 0, dbias, jnp.where(at == n, drate, jnp.where(at == 2 * n, dskip, 0.0)))
    part_ref[0, 7:8, :] = jnp.sum(placed, 0, keepdims=True)


def input_body(dpre_ref, taps_ref, gx_ref, gbc_ref, rim_ref):
    for o in range(PAIRS + 2):
        lanes = slice(o * LANES, (o + 1) * LANES)
        own = jnp.zeros((SEG, LANES), F32)
        rim = jnp.zeros((HALO, LANES), F32)
        for k in range(4):
            tap = taps_ref[k : k + 1, lanes]
            own = own + tap * dpre_ref[pl.ds(HALO + 3 - k, SEG), lanes]
            rim = rim + tap * dpre_ref[pl.ds(HALO - k, HALO), lanes]
        rim_ref[o, :, :] = rim.astype(BF16)
        if o < PAIRS:
            gx_ref[:, lanes] = own.astype(BF16)
        else:
            gbc_ref[:, (o - PAIRS) * LANES : (o - PAIRS + 1) * LANES] = own


def swap_body(gx_ref, gbc_ref, back_ref, gstep_ref, side_ref, keepx_ref, keepbc_ref, keepstep_ref, give_ref):
    second = side_ref[:1] > 0.5
    whole = jnp.broadcast_to(second, (ROWS, LANES))
    last = iota((HALO, LANES), 0) >= HALO - 3
    for o in range(PAIRS + 2):
        lanes = slice(o * LANES, (o + 1) * LANES)
        came = pltpu.roll(back_ref[o].astype(F32), HALO - 3, 0)
        came = jnp.where(last, came, 0.0)
        came = jnp.concatenate([jnp.zeros((ROWS - HALO, LANES), F32), came], 0)
        if o < PAIRS:
            first, then = gx_ref[:ROWS, lanes].astype(F32), gx_ref[ROWS:, lanes].astype(F32) + came
            keepx_ref[:, lanes] = jnp.where(whole, then, first).astype(BF16)
        else:
            mine = slice((o - PAIRS) * LANES, (o - PAIRS + 1) * LANES)
            first, then = gbc_ref[:ROWS, mine], gbc_ref[ROWS:, mine] + came
            keepbc_ref[:, mine] = jnp.where(whole, then, first)
        give_ref[o, :, :] = jnp.where(whole, first, then).astype(BF16)
    first, then = gstep_ref[:HEADS, :], gstep_ref[HEADS:, :]
    keepstep_ref[...] = jnp.where(whole[:HEADS], then, first)
    given = jnp.where(whole[:HEADS], first, then)
    high = given.astype(BF16)
    give_ref[PAIRS + 2, :HEADS, :] = high
    give_ref[PAIRS + 2, HEADS : 2 * HEADS, :] = (given - high.astype(F32)).astype(BF16)
    give_ref[PAIRS + 2, 2 * HEADS :, :] = jnp.zeros((ROWS - 2 * HEADS, LANES), BF16)


def merge_body(keepx_ref, keepbc_ref, keepstep_ref, came_ref, side_ref, gx_ref, gbc_ref, gstep_ref):
    second = side_ref[:1] > 0.5
    whole = jnp.broadcast_to(second, (ROWS, LANES))
    for o in range(PAIRS):
        lanes = slice(o * LANES, (o + 1) * LANES)
        mine, other = keepx_ref[:, lanes].astype(F32), came_ref[o].astype(F32)
        gx_ref[:, lanes] = jnp.where(whole, other, mine).astype(BF16)
        gx_ref[:, HALF + o * LANES : HALF + (o + 1) * LANES] = jnp.where(whole, mine, other).astype(BF16)
    for k in range(2):
        lanes = slice(k * LANES, (k + 1) * LANES)
        gbc_ref[:, lanes] = (keepbc_ref[:, lanes] + came_ref[PAIRS + k].astype(F32)).astype(BF16)
    mine = keepstep_ref[...]
    other = came_ref[PAIRS + 2, :HEADS, :].astype(F32) + came_ref[PAIRS + 2, HEADS : 2 * HEADS, :].astype(F32)
    gstep_ref[:HEADS, :] = jnp.where(whole[:HEADS], other, mine)
    gstep_ref[HEADS:, :] = jnp.where(whole[:HEADS], mine, other)


def spread_body(in_ref, out_ref, *, scale):
    total = in_ref[0]
    for j in range(1, in_ref.shape[0]):
        total = total + in_ref[j]
    total = total * scale
    for j in range(out_ref.shape[0]):
        out_ref[j] = total


def spread(x, count, scale):
    def body(in_ref, out_ref):
        spread_body(in_ref, out_ref, scale=scale)

    return call(body, [far(count, 8, LANES)], [VMEM])(x)[0]


def unpack_body(in_ref, weight_ref, offset_ref, bias_ref, rate_ref, skip_ref):
    heads = in_ref[0, 7:8, :] + in_ref[1, 7:8, :]
    for k, ref in enumerate((bias_ref, rate_ref, skip_ref)):
        ref[...] = heads[:, k * 2 * HEADS : (k + 1) * 2 * HEADS].reshape(2 * HEADS)
    for k in range(2):
        for o in range(PAIRS):
            lanes = slice(k * HALF + o * LANES, k * HALF + (o + 1) * LANES)
            weight_ref[:, lanes] = in_ref[2 * o + k, :4, :]
            offset_ref[lanes] = in_ref[2 * o + k, 4, :]
    for k in range(5):
        both = in_ref[2 * k, 5:7, :] + in_ref[2 * k + 1, 5:7, :]
        for m in range(2):
            lanes = slice(2 * HALF + m * LANES, 2 * HALF + (m + 1) * LANES)
            if k < 4:
                weight_ref[k : k + 1, lanes] = both[m : m + 1]
            else:
                offset_ref[lanes] = both[m]


def compute(
    mixer_input, state_input, step_raw, conv_weight, conv_bias, step_bias, log_rate, skip_gain, grad_out
):
    x, bc, step, g = mixer_input[0], state_input[0], step_raw[0], grad_out[0]
    n_seq, n_dp = lax.axis_size("seq"), lax.axis_size("dp")
    chips = n_seq // 2
    inner = 2 * HALF
    n = 2 * HEADS
    assert x.shape == (ROWS, inner) and bc.shape == (ROWS, 2 * LANES) and chips == PAIRS and step.shape[0] == n
    cores = [[2 * c, 2 * c + 1] for c in range(chips)]
    ring = [[2 * c + k for c in range(chips)] for k in range(2)]
    packed = call(pack_body, [shape(2, PACKED, LANES, dtype=BF16)], [FAR] * 4)(x, bc, g, step)[0]
    got = lax.all_to_all(packed, "seq", 0, 0, axis_index_groups=cores)
    tail = call(tail_body, [kept(PAIRS + 2, HALO, LANES, dtype=BF16)], [VMEM])(got)[0]
    halo = lax.ppermute(tail, "seq", [(i, i + 2) for i in range(n_seq - 2)])
    by_row, by_col, taps, side = call(
        steps_body,
        [kept(7 * n, ROWS), kept(ROWS, 4 * n), kept(5, HALF + 2 * LANES), kept(8, LANES)],
        [VMEM, FAR, FAR, SMEM, SMEM, SMEM],
    )(got, conv_weight, conv_bias, step_bias, log_rate, skip_gain)
    ext = [pltpu.VMEM((2, SEG + HALO, LANES), F32), pltpu.VMEM((SEG + HALO, 2 * LANES), F32)]
    bc_act, near, send = call(
        first_body,
        [
            kept(SEG, 2 * LANES, dtype=BF16),
            far(PAIRS, 2 * ROWS, LANES, dtype=BF16),
            shape(PAIRS, SENT, LANES, dtype=BF16),
        ],
        [VMEM] * 4,
        ext,
    )(got, halo, taps, by_col)
    sent = lax.all_to_all(send, "seq", 0, 0, axis_index_groups=ring)
    dx, slope, xw, gw, dbc, slope2, row = call(
        inner_body,
        [
            far(PAIRS, SEG, LANES),
            far(PAIRS, SEG, LANES),
            far(PAIRS, SEG, LANES, dtype=BF16),
            far(PAIRS, SEG, LANES, dtype=BF16),
            far(SEG, 2 * LANES),
            far(SEG, 2 * LANES),
            far(3 * n, ROWS),
        ],
        [VMEM] * 6,
        ext,
    )(got, halo, taps, by_row, by_col, bc_act)
    scanned = call(scan_body, [far(chips, 2 * ROWS, LANES, dtype=BF16)], [VMEM])(sent)[0]
    states = lax.all_to_all(scanned, "seq", 0, 0, axis_index_groups=ring)
    dpre, gstep, part = call(
        last_body,
        [kept(SEG + 2 * HALO, HALF + 2 * LANES), far(n, ROWS), far(PAIRS, 8, LANES)],
        [VMEM] * 7 + [FAR] * 8,
        ext + [pltpu.VMEM((3 * n, ROWS), F32)],
    )(got, halo, by_row, by_col, bc_act, side, states, near, dx, slope, xw, gw, dbc, slope2, row)
    part = lax.all_to_all(part, "seq", 0, 0, axis_index_groups=ring)
    part = spread(part, n_dp, 1.0)
    part = lax.all_to_all(part, "dp", 0, 0)
    part = spread(part, n_seq, 1.0 / n_dp)
    part = lax.all_to_all(part, "seq", 0, 0)
    gx, gbc, rim = call(
        input_body,
        [kept(SEG, HALF, dtype=BF16), kept(SEG, 2 * LANES), kept(PAIRS + 2, HALO, LANES, dtype=BF16)],
        [VMEM] * 2,
    )(dpre, taps)
    back = lax.ppermute(rim, "seq", [(i, i - 2) for i in range(2, n_seq)])
    keepx, keepbc, keepstep, give = call(
        swap_body,
        [
            kept(ROWS, HALF, dtype=BF16),
            kept(ROWS, 2 * LANES),
            kept(HEADS, ROWS),
            kept(PAIRS + 3, ROWS, LANES, dtype=BF16),
        ],
        [VMEM, VMEM, VMEM, FAR, VMEM],
    )(gx, gbc, back, gstep, side)
    came = lax.ppermute(give, "seq", [(i, i ^ 1) for i in range(n_seq)])
    gx, gbc, gstep = call(
        merge_body, [shape(ROWS, inner, dtype=BF16), shape(ROWS, 2 * LANES, dtype=BF16), shape(n, ROWS)], [VMEM] * 5
    )(keepx, keepbc, keepstep, came, side)
    weight, offset, bias, rate, skip = call(
        unpack_body,
        [shape(4, inner + 2 * LANES), shape(inner + 2 * LANES), shape(n), shape(n), shape(n)],
        [VMEM],
    )(part)
    return gx[None], gbc[None], gstep[None], weight, offset, bias, rate, skip


def solution(mesh):
    return jax.shard_map(
        compute,
        mesh=mesh,
        in_specs=(
            P("dp", "seq", None),
            P("dp", "seq", None),
            P("dp", None, "seq"),
            P(),
            P(),
            P(),
            P(),
            P(),
            P("dp", "seq", None),
        ),
        out_specs=(
            P("dp", "seq", None),
            P("dp", "seq", None),
            P("dp", None, "seq"),
            P(),
            P(),
            P(),
            P(),
            P(),
        ),
        check_vma=False,
    )
```

time: 125 us -> 116 us (0.928)
  local copies, waits for them, and re-layouts: 12.3 us -> 0 us
  Pallas kernels: 14 us -> 21.9 us
  starting transfers between devices: 29.7 us -> 36.8 us
  waiting for transfers between devices: 27.7 us -> 21.9 us
  blocking collectives: 37.1 us -> 34.2 us
  other arithmetic: 2.18 us -> 0 us
    pallas_call x7 -> x13, Pallas kernels: 14 us -> 21.9 us  [call(): kernel(*(pltpu.with_memory_space_constraint(a, pltpu.VMEM if spec is VMEM...]
    unnamed x37 -> x0, local copies, waits for them, and re-layouts: 5.54 us -> none
    all_to_all x4, starting transfers between devices: 22.2 us -> 26.7 us  [the longest x1 10 us: compute(): part = lax.all_to_all(part, 'seq', 0, 0)]
    all_to_all x4, waiting for transfers between devices: 25.5 us -> 21.9 us  [the longest x1 9.75 us: compute(): states = lax.all_to_all(scanned, 'seq', 0, 0, axis_index_groups=ring)]
    all_to_all x3 -> x2, blocking collectives: 37.1 us -> 34.2 us  [the longest x1 23.1 us: compute(): sent = lax.all_to_all(send, 'seq', 0, 0, axis_index_groups=ring)]
    scatter-add x2 -> x0, local copies, waits for them, and re-layouts: 2.71 us -> none  [the longest x1 1.41 us: on_device(): gx = gx.at[rows - 3:].add(back[:3, :inner])]
    slice x5 -> x0, local copies, waits for them, and re-layouts: 2.67 us -> none  [the longest x2 1.45 us: on_device(): tail = jnp.concatenate([x[rows - HALO:], bc[rows - HALO:]], 1)]
    ppermute x2 -> x3, starting transfers between devices: 7.49 us -> 10.1 us  [the longest x1 7.52 us: compute(): came = lax.ppermute(give, 'seq', [(i, i ^ 1) for i in range(n_seq)])]
  transfers between devices with their start and end apart: 6 -> 7, of which waited for: 5 -> 4; matrix products, arithmetic and copies ran while one was open for 4% -> 0% of each run, Pallas kernels for 4% -> 8%
where the time goes in v3:
time: 116 us
  starting transfers between devices  36.8 us (32%)
  blocking collectives  34.2 us (29%)
  Pallas kernels  21.9 us (19%)
  waiting for transfers between devices  21.9 us (19%)
    all_to_all x1, blocking collectives, compute(): sent = lax.all_to_all(send, 'seq', 0, 0, axis_index_groups=ring)  23.1 us
    pallas_call x13, Pallas kernels, call(): kernel(*(pltpu.with_memory_space_constraint(a, pltpu.VMEM if spec is VMEM...  21.9 us
    all_to_all x1, blocking collectives, compute(): got = lax.all_to_all(packed, 'seq', 0, 0, axis_index_groups=cores)  11.2 us
    all_to_all x1, starting transfers between devices, compute(): part = lax.all_to_all(part, 'seq', 0, 0)  10 us
    all_to_all x1, waiting for transfers between devices, compute(): states = lax.all_to_all(scanned, 'seq', 0, 0, axis_index_groups=ring)  9.75 us
    all_to_all x1, starting transfers between devices, compute(): part = lax.all_to_all(part, 'dp', 0, 0)  9.67 us
    ppermute x1, starting transfers between devices, compute(): came = lax.ppermute(give, 'seq', [(i, i ^ 1) for i in range(n_seq)])  7.52 us
    all_to_all x1, waiting for transfers between devices, compute(): part = lax.all_to_all(part, 'seq', 0, 0)  6.85 us
  transfers between devices with their start and end apart: 7, of which 4 were waited for; matrix products, arithmetic and copies ran while one was open for 0% of the time, Pallas kernels for 8%

profile of v3, /device:TPU:1, one launch (start us, length us, event | category | flops | bytes accessed | tf_op | source)
XLA Modules:
  0.0 115.6 jit_solution(16267118807314843844)
XLA Ops:
  0.6 1.4 %shard_map.152 = bf16[2,2368,128]{2,1,0:T(8,128)(2,1)S(1)} custom-call(bf16[128,2048]{1,0:T(8,128)(2,1)} %bitcast.7, bf16[128,256]{1,0:T(8,128)(2,1)} %bitcast.9, bf16[128,2048]{1,0:T(8,128)(2,1)} %bitcast.8, f32[32,128]{1,0:T(8,128)} %bitcast.10), custom_call_target="tpu_custom_call" | custom-call | tf_op jit(solution)/shard_map/pallas_call | solution.py:43
  2.1 11.2 %all_to_all.30.got_ref = bf16[2,2368,128]{2,1,0:T(8,128)(2,1)S(1)} all-to-all(bf16[2,2368,128]{2,1,0:T(8,128)(2,1)S(1)} %shard_map.152), channel_id=1, replica_groups={{0,1},{2,3},{4,5},{6,7},{8,9},{10,11},{12,13},{14,15},{16,17},{18,19},{..., dimensions={0} | all-to-all | bytes 2424832 | tf_op jit(solution)/shard_map/all_to_all | solution.py:465
  13.2 1.3 %collective-permute-start = (bf16[10,8,128]{2,1,0:T(8,128)(2,1)S(1)}, bf16[10,8,128]{2,1,0:T(8,128)(2,1)S(1)}, u32[]{:S(2)}, u32[]{:S(2)}) collective-permute-start(bf16[10,8,128]{2,1,0:T(8,128)(2,1)S(1)} %shard_map.153), channel_id=1, source_target_pairs={{0,2},{1,3},{2,4},{3,5},{4,6},{5,7},{6,8},{7,9},{8,10},{9,11},{10,... | collective-permute-start | bytes 61448 | tf_op jit(solution)/shard_map/ppermute | solution.py:467
  14.5 1.2 %shard_map.154 = (f32[224,128]{1,0:T(8,128)S(1)}, f32[128,128]{1,0:T(8,128)S(1)}, f32[5,1280]{1,0:T(8,128)S(1)}, f32[8,128]{1,0:T(8,128)S(1)}) custom-call(bf16[2,2368,128]{2,1,0:T(8,128)(2,1)S(1)} %all_to_all.30.got_ref, f32[4,2304]{1,0:T(4,128)} %weight_ref.1, f32[2304]{0:T(1024)} %offset_ref.1, f32[32]{0:T(128)} %bias_ref.1, f32[32]{0:T(128)} %rate_ref.1, ...), custom_call_target="tpu_custom_call" | custom-call | tf_op jit(solution)/shard_map/pallas_call | solution.py:43
  15.7 0.0 collective-permute-done.halo_ref
  15.7 2.7 %shard_map.155 = (bf16[256,256]{1,0:T(8,128)(2,1)S(1)}, bf16[8,256,128]{2,1,0:T(8,128)(2,1)}, bf16[8,272,128]{2,1,0:T(8,128)(2,1)S(1)}) custom-call(bf16[2,2368,128]{2,1,0:T(8,128)(2,1)S(1)} %all_to_all.30.got_ref, bf16[10,8,128]{2,1,0:T(8,128)(2,1)S(1)} %collective-permute-done.halo_ref, f32[5,1280]{1,0:T(8,128)S(1)} %get-tuple-element.42.taps_ref, ...), custom_call_target="tpu_custom_call" | custom-call | tf_op jit(solution)/shard_map/pallas_call | solution.py:43
  18.5 23.1 %all_to_all.31.got_ref = bf16[8,272,128]{2,1,0:T(8,128)(2,1)S(1)} all-to-all(bf16[8,272,128]{2,1,0:T(8,128)(2,1)S(1)} %get-tuple-element.45), channel_id=1, replica_groups={{0,2,4,6,8,10,12,14},{1,3,5,7,9,11,13,15},{16,18,20,22,24,26,28,30},{17..., dimensions={0} | all-to-all | bytes 1114112 | tf_op jit(solution)/shard_map/all_to_all | solution.py:484
  41.5 0.9 shard_map.156
  42.4 3.7 %all-to-all-start.2 = ((bf16[8,256,128]{2,1,0:T(8,128)(2,1)}), bf16[8,256,128]{2,1,0:T(8,128)(2,1)S(1)}, u32[]{:S(2)}, u32[]{:S(2)}) async-start(bf16[8,256,128]{2,1,0:T(8,128)(2,1)} %shard_map.156), calls=%async_computation.2 | async-start | bytes 1048576 | tf_op jit(solution)/shard_map/all_to_all | solution.py:500
  46.1 4.5 %shard_map.157 = (f32[8,256,128]{2,1,0:T(8,128)}, f32[8,256,128]{2,1,0:T(8,128)}, bf16[8,256,128]{2,1,0:T(8,128)(2,1)}, bf16[8,256,128]{2,1,0:T(8,128)(2,1)}, f3...) custom-call(bf16[2,2368,128]{2,1,0:T(8,128)(2,1)S(1)} %all_to_all.30.got_ref, ...), custom_call_target="tpu_custom_call" | custom-call | tf_op jit(solution)/shard_map/pallas_call | solution.py:43
  50.6 9.7 %all-to-all-done.2.states_ref = bf16[8,256,128]{2,1,0:T(8,128)(2,1)S(1)} async-done(((bf16[8,256,128]{2,1,0:T(8,128)(2,1)}), bf16[8,256,128]{2,1,0:T(8,128)(2,1)S(1)}, u32[]{:S(2)}, u32[]{:S(2)}) %all-to-all-start.2) | async-done | bytes 524320 | tf_op jit(solution)/shard_map/all_to_all | solution.py:500
  60.4 6.4 %shard_map.158 = (f32[272,1280]{1,0:T(8,128)S(1)}, f32[32,128]{1,0:T(8,128)}, f32[8,8,128]{2,1,0:T(8,128)}) custom-call(bf16[2,2368,128]{2,1,0:T(8,128)(2,1)S(1)} %all_to_all.30.got_ref, bf16[10,8,128]{2,1,0:T(8,128)(2,1)S(1)} %collective-permute-done.halo_ref, f32[224,128]{1,0:T(8,128)S(1)} %get-tuple-element.40.rows_ref, ...), custom_call_target="tpu_custom_call" | custom-call | tf_op jit(solution)/shard_map/pallas_call | solution.py:43
  66.8 3.3 %all-to-all-start.3 = ((f32[8,8,128]{2,1,0:T(8,128)}), f32[8,8,128]{2,1,0:T(8,128)S(1)}, u32[]{:S(2)}, u32[]{:S(2)}) async-start(f32[8,8,128]{2,1,0:T(8,128)} %get-tuple-element.66), calls=%async_computation.3 | async-start | bytes 65536 | tf_op jit(solution)/shard_map/all_to_all | solution.py:507
  70.1 0.9 shard_map.159
  71.0 1.3 %collective-permute-start.1 = (bf16[10,8,128]{2,1,0:T(8,128)(2,1)S(1)}, bf16[10,8,128]{2,1,0:T(8,128)(2,1)S(1)}, u32[]{:S(2)}, u32[]{:S(2)}) collective-permute-start(bf16[10,8,128]{2,1,0:T(8,128)(2,1)S(1)} %get-tuple-element.57), channel_id=1, source_target_pairs={{2,0},{3,1},{4,2},{5,3},{6,4},{7,5},{8,6},{9,7},{10,8},{11,9},{12,... | collective-permute-start | bytes 61448 | tf_op jit(solution)/shard_map/ppermute | solution.py:517
  72.3 4.6 %all-to-all-done.3.in_ref = f32[8,8,128]{2,1,0:T(8,128)S(1)} async-done(((f32[8,8,128]{2,1,0:T(8,128)}), f32[8,8,128]{2,1,0:T(8,128)S(1)}, u32[]{:S(2)}, u32[]{:S(2)}) %all-to-all-start.3) | async-done | bytes 32800 | tf_op jit(solution)/shard_map/all_to_all | solution.py:507
  76.9 0.7 shard_map.162
  77.6 9.7 %all-to-all-start.4 = ((f32[32,8,128]{2,1,0:T(8,128)}), f32[32,8,128]{2,1,0:T(8,128)S(1)}, u32[]{:S(2)}, u32[]{:S(2)}) async-start(f32[32,8,128]{2,1,0:T(8,128)} %shard_map.162), calls=%async_computation.4 | async-start | bytes 262144 | tf_op jit(solution)/shard_map/all_to_all | solution.py:509
  87.3 0.0 collective-permute-done.1.back_ref
  87.3 0.9 shard_map.160
  88.1 7.5 %collective-permute-start.2 = (bf16[11,128,128]{2,1,0:T(8,128)(2,1)S(1)}, bf16[11,128,128]{2,1,0:T(8,128)(2,1)S(1)}, u32[]{:S(2)}, u32[]{:S(2)}) collective-permute-start(bf16[11,128,128]{2,1,0:T(8,128)(2,1)S(1)} %get-tuple-element.62), channel_id=1, source_target_pairs={{0,1},{1,0},{2,3},{3,2},{4,5},{5,4},{6,7},{7,6},{8,9},{9,8},{10,11... | collective-permute-start | bytes 1081352 | tf_op jit(solution)/shard_map/ppermute | solution.py:528
  95.7 0.7 all-to-all-done.4.in_ref
  96.4 0.7 shard_map.163
  97.1 10.0 %all-to-all-start.5 = ((f32[16,8,128]{2,1,0:T(8,128)}), f32[16,8,128]{2,1,0:T(8,128)S(1)}, u32[]{:S(2)}, u32[]{:S(2)}) async-start(f32[16,8,128]{2,1,0:T(8,128)} %shard_map.163), calls=%async_computation.5 | async-start | bytes 131072 | tf_op jit(solution)/shard_map/all_to_all | solution.py:511
  107.1 0.0 collective-permute-done.2.came_ref
  107.1 1.0 shard_map.161
  108.1 6.9 %all-to-all-done.5.in_ref = f32[16,8,128]{2,1,0:T(8,128)S(1)} async-done(((f32[16,8,128]{2,1,0:T(8,128)}), f32[16,8,128]{2,1,0:T(8,128)S(1)}, u32[]{:S(2)}, u32[]{:S(2)}) %all-to-all-start.5) | async-done | bytes 65568 | tf_op jit(solution)/shard_map/all_to_all | solution.py:511
  114.9 0.6 shard_map.164
  (1 shorter events, 0.0 us)
Async XLA Ops:
  13.2 2.5 %collective-permute-start = (bf16[10,8,128]{2,1,0:T(8,128)(2,1)S(1)}, bf16[10,8,128]{2,1,0:T(8,128)(2,1)S(1)}, u32[]{:S(2)}, u32[]{:S(2)}) collective-permute-start(bf16[10,8,128]{2,1,0:T(8,128)(2,1)S(1)} %shard_map.153), channel_id=1, source_target_pairs={{0,2},{1,3},{2,4},{3,5},{4,6},{5,7},{6,8},{7,9},{8,10},{9,11},{10,... | collective-permute-start | bytes 61448 | tf_op jit(solution)/shard_map/ppermute | solution.py:467
  42.4 17.9 %all-to-all-start.2 = ((bf16[8,256,128]{2,1,0:T(8,128)(2,1)}), bf16[8,256,128]{2,1,0:T(8,128)(2,1)S(1)}, u32[]{:S(2)}, u32[]{:S(2)}) async-start(bf16[8,256,128]{2,1,0:T(8,128)(2,1)} %shard_map.156), calls=%async_computation.2 | async-start | bytes 1048576 | tf_op jit(solution)/shard_map/all_to_all | solution.py:500
  66.8 10.1 %all-to-all-start.3 = ((f32[8,8,128]{2,1,0:T(8,128)}), f32[8,8,128]{2,1,0:T(8,128)S(1)}, u32[]{:S(2)}, u32[]{:S(2)}) async-start(f32[8,8,128]{2,1,0:T(8,128)} %get-tuple-element.66), calls=%async_computation.3 | async-start | bytes 65536 | tf_op jit(solution)/shard_map/all_to_all | solution.py:507
  71.0 16.2 %collective-permute-start.1 = (bf16[10,8,128]{2,1,0:T(8,128)(2,1)S(1)}, bf16[10,8,128]{2,1,0:T(8,128)(2,1)S(1)}, u32[]{:S(2)}, u32[]{:S(2)}) collective-permute-start(bf16[10,8,128]{2,1,0:T(8,128)(2,1)S(1)} %get-tuple-element.57), channel_id=1, source_target_pairs={{2,0},{3,1},{4,2},{5,3},{6,4},{7,5},{8,6},{9,7},{10,8},{11,9},{12,... | collective-permute-start | bytes 61448 | tf_op jit(solution)/shard_map/ppermute | solution.py:517
  77.6 18.8 %all-to-all-start.4 = ((f32[32,8,128]{2,1,0:T(8,128)}), f32[32,8,128]{2,1,0:T(8,128)S(1)}, u32[]{:S(2)}, u32[]{:S(2)}) async-start(f32[32,8,128]{2,1,0:T(8,128)} %shard_map.162), calls=%async_computation.4 | async-start | bytes 262144 | tf_op jit(solution)/shard_map/all_to_all | solution.py:509
  88.1 19.0 %collective-permute-start.2 = (bf16[11,128,128]{2,1,0:T(8,128)(2,1)S(1)}, bf16[11,128,128]{2,1,0:T(8,128)(2,1)S(1)}, u32[]{:S(2)}, u32[]{:S(2)}) collective-permute-start(bf16[11,128,128]{2,1,0:T(8,128)(2,1)S(1)} %get-tuple-element.62), channel_id=1, source_target_pairs={{0,1},{1,0},{2,3},{3,2},{4,5},{5,4},{6,7},{7,6},{8,9},{9,8},{10,11... | collective-permute-start | bytes 1081352 | tf_op jit(solution)/shard_map/ppermute | solution.py:528
  97.1 17.9 %all-to-all-start.5 = ((f32[16,8,128]{2,1,0:T(8,128)}), f32[16,8,128]{2,1,0:T(8,128)S(1)}, u32[]{:S(2)}, u32[]{:S(2)}) async-start(f32[16,8,128]{2,1,0:T(8,128)} %shard_map.163), calls=%async_computation.5 | async-start | bytes 131072 | tf_op jit(solution)/shard_map/all_to_all | solution.py:511

commit v4 on v3

--- a/solution.py
+++ b/solution.py
@@ -15,11 +15,12 @@
 PAIRS = 8
 HEADS = 16
 HALF = PAIRS * LANES
+WIDE = 2 * LANES
 SEG = 2 * ROWS
 G_AT, B_AT, C_AT, STEP_AT = HALF, 2 * HALF, 2 * HALF + ROWS, 2 * HALF + 2 * ROWS
 SIDE_AT = STEP_AT + 3 * HEADS
 PACKED = SIDE_AT + 16
-SENT = 2 * ROWS + 16
+SENT = 2 * ROWS + 8
 VMEM = pl.BlockSpec(memory_space=pltpu.VMEM)
 FAR = pl.BlockSpec(memory_space=pltpu.VMEM)
 SMEM = pl.BlockSpec(memory_space=pltpu.SMEM)
@@ -100,7 +101,7 @@
     return out
 
 
-def steps_body(got_ref, weight_ref, offset_ref, bias_ref, rate_ref, skip_ref, rows_ref, cols_ref, taps_ref, side_ref):
+def steps_body(got_ref, weight_ref, offset_ref, bias_ref, rate_ref, skip_ref, rows_ref, cols_ref, taps_ref, side_ref, parts_ref):
     side = got_ref[0, SIDE_AT:, :].astype(F32)[:8]
     side_ref[...] = side
     second = side[:1] > 0.5
@@ -132,33 +133,43 @@
     rows_ref[5 * n : 6 * n, :] = rate
     rows_ref[6 * n :, :] = head_rows(skip_ref, second)
     cols_ref[...] = stack.T
+    for k, value in enumerate((weight, fade)):
+        split = [value]
+        for _ in range(2):
+            split.append(split[-1] - split[-1].astype(BF16).astype(F32))
+        for r in range(2):
+            for c in range(HALF // WIDE):
+                at = r * HEADS + 4 * c
+                rows = [piece[at : at + 4] for piece in split] + [jnp.zeros((4, ROWS), F32)]
+                parts_ref[k, r, c] = jnp.concatenate(rows, 0).astype(BF16)
+
+
+def spreader():
+    part, head = iota((16, WIDE), 0), iota((16, WIDE), 1) // 64
+    return jnp.where((part % 4 == head) & (part < 12), 1.0, 0.0).astype(BF16)
+
+
+def beside(first, second):
+    return jnp.concatenate([first, second], 1)
 
 
 def head_of(r, o):
     return r * HEADS + 2 * o
 
 
-def fill(ext_ref, halo, first, second):
-    ext_ref[:HALO, :] = halo.astype(F32)
-    ext_ref[HALO : HALO + ROWS, :] = first.astype(F32)
-    ext_ref[HALO + ROWS :, :] = second.astype(F32)
-
-
-def fill_pair(ext_ref, got_ref, halo_ref, o):
-    rows = slice(o * ROWS, (o + 1) * ROWS)
-    fill(ext_ref, halo_ref[o], got_ref[0, rows, :], got_ref[1, rows, :])
-
-
-def fill_bc(ext2_ref, got_ref, halo_ref):
-    for k, at in enumerate((B_AT, C_AT)):
-        lanes = slice(k * LANES, (k + 1) * LANES)
-        fill(ext2_ref.at[:, lanes], halo_ref[PAIRS + k], got_ref[0, at : at + ROWS, :], got_ref[1, at : at + ROWS, :])
-
-
-def preact(ext_ref, taps_ref, at, lanes):
-    acc = taps_ref[4:5, at : at + lanes]
+def fill(ext_ref, got_ref, halo_ref):
+    for o in range(PAIRS + 2):
+        at = o * ROWS if o < PAIRS else B_AT + (o - PAIRS) * ROWS
+        ext_ref[o, :HALO, :] = halo_ref[o].astype(F32)
+        for r in range(2):
+            ext_ref[o, HALO + r * ROWS : HALO + (r + 1) * ROWS, :] = got_ref[r, at : at + ROWS, :].astype(F32)
+
+
+def preact(ext_ref, taps_ref, o, first=0, count=SEG):
+    lanes = slice(o * LANES, (o + 1) * LANES)
+    acc = taps_ref[4:5, lanes]
     for k in range(4):
-        acc = acc + taps_ref[k : k + 1, at : at + lanes] * ext_ref[pl.ds(HALO - 3 + k, SEG), :]
+        acc = acc + taps_ref[k : k + 1, lanes] * ext_ref[o, pl.ds(HALO - 3 + k + first, count), :]
     return acc
 
 
@@ -176,37 +187,42 @@
 
 def decay_rows(total):
     high = total.astype(BF16).astype(F32)
-    row = iota((16, LANES), 0)
+    row = iota((8, LANES), 0)
     return jnp.where(row == 0, high, jnp.where(row == 1, total - high, 0.0)).astype(BF16)
 
 
-def first_body(got_ref, halo_ref, taps_ref, cols_ref, bcact_ref, near_ref, send_ref, ext_ref, ext2_ref):
-    fill_bc(ext2_ref, got_ref, halo_ref)
-    pre = preact(ext2_ref, taps_ref, HALF, 2 * LANES)
+def first_body(got_ref, halo_ref, taps_ref, parts_ref, bcact_ref, near_ref, send_ref, ext_ref):
+    fill(ext_ref, got_ref, halo_ref)
+    pre = beside(preact(ext_ref, taps_ref, PAIRS), preact(ext_ref, taps_ref, PAIRS + 1))
     bc = pre * jax.nn.sigmoid(pre)
     bcact_ref[...] = bc.astype(BF16)
     bc = bc.astype(BF16).astype(F32)
     b_t = [bc[r * ROWS : (r + 1) * ROWS, :LANES].T.astype(BF16) for r in range(2)]
     c_t = [bc[r * ROWS : (r + 1) * ROWS, LANES:].T.astype(BF16) for r in range(2)]
-    left = iota((ROWS, LANES), 1) < 64
-    for o in range(PAIRS):
-        ext = ext_ref.at[o % 2]
-        fill_pair(ext, got_ref, halo_ref, o)
-        pre = preact(ext, taps_ref, o * LANES, LANES)
-        act = (pre * jax.nn.sigmoid(pre)).astype(BF16).astype(F32)
+    over = spreader()
+    for c in range(HALF // WIDE):
         ends, backs, totals = [], [], []
+        g_at = G_AT + 2 * c * ROWS
         for r in range(2):
-            fade = pair_column(cols_ref, 3, r, o, left)
-            xw = (act[r * ROWS : (r + 1) * ROWS] * pair_column(cols_ref, 2, r, o, left)).astype(BF16)
-            gw = (got_ref[r, G_AT + o * ROWS : G_AT + (o + 1) * ROWS, :].astype(F32) * fade).astype(BF16)
+            pre = beside(*(preact(ext_ref, taps_ref, 2 * c + k, r * ROWS, ROWS) for k in range(2)))
+            act = (pre * jax.nn.sigmoid(pre)).astype(BF16).astype(F32)
+            fade = dot(parts_ref[1, r, c], over, TN)
+            xw = (act * dot(parts_ref[0, r, c], over, TN)).astype(BF16)
+            g = beside(got_ref[r, g_at : g_at + ROWS, :], got_ref[r, g_at + ROWS : g_at + 2 * ROWS, :])
+            gw = (g.astype(F32) * fade).astype(BF16)
             ends.append(dot(b_t[r], xw))
             backs.append(dot(c_t[r], gw))
             totals.append(fade[ROWS - 1 :, :])
-        near_ref[o, :ROWS, :] = ends[0].astype(BF16)
-        near_ref[o, ROWS:, :] = backs[1].astype(BF16)
-        send_ref[o, :ROWS, :] = (totals[1] * ends[0] + ends[1]).astype(BF16)
-        send_ref[o, ROWS : 2 * ROWS, :] = (backs[0] + totals[0] * backs[1]).astype(BF16)
-        send_ref[o, 2 * ROWS :, :] = decay_rows(totals[0] * totals[1])
+        end = totals[1] * ends[0] + ends[1]
+        back = backs[0] + totals[0] * backs[1]
+        total = totals[0] * totals[1]
+        for k in range(2):
+            o, lanes = 2 * c + k, slice(k * LANES, (k + 1) * LANES)
+            near_ref[o, :ROWS, :] = ends[0][:, lanes].astype(BF16)
+            near_ref[o, ROWS:, :] = backs[1][:, lanes].astype(BF16)
+            send_ref[o, :ROWS, :] = end[:, lanes].astype(BF16)
+            send_ref[o, ROWS : 2 * ROWS, :] = back[:, lanes].astype(BF16)
+            send_ref[o, 2 * ROWS :, :] = decay_rows(total[:, lanes])
 
 
 def scan_body(got_ref, out_ref):
@@ -223,11 +239,11 @@
 
 def inner_body(
     got_ref, halo_ref, taps_ref, rows_ref, cols_ref, bcact_ref,
-    dx_ref, slope_ref, xw_ref, gw_ref, dbc_ref, slope2_ref, row_ref, ext_ref, ext2_ref,
+    dx_ref, slope_ref, xw_ref, gw_ref, dbc_ref, slope2_ref, row_ref, ext_ref,
 ):
     n = 2 * HEADS
-    fill_bc(ext2_ref, got_ref, halo_ref)
-    pre = preact(ext2_ref, taps_ref, HALF, 2 * LANES)
+    fill(ext_ref, got_ref, halo_ref)
+    pre = beside(preact(ext_ref, taps_ref, PAIRS), preact(ext_ref, taps_ref, PAIRS + 1))
     gate = jax.nn.sigmoid(pre)
     slope2_ref[...] = gate * (1.0 + pre * (1.0 - gate))
     causal = iota((ROWS, ROWS), 0) <= iota((ROWS, ROWS), 1)
@@ -238,19 +254,18 @@
     scores = [dot(b[r], c[r], NT) for r in range(2)]
     dscores = [jnp.zeros((ROWS, ROWS), F32) for _ in range(2)]
     for o in range(PAIRS):
-        ext = ext_ref.at[o % 2]
-        fill_pair(ext, got_ref, halo_ref, o)
-        pre = preact(ext, taps_ref, o * LANES, LANES)
+        lanes = slice(o * LANES, (o + 1) * LANES)
+        pre = preact(ext_ref, taps_ref, o)
         gate = jax.nn.sigmoid(pre)
-        slope_ref[o] = gate * (1.0 + pre * (1.0 - gate))
+        slope_ref[:, lanes] = (gate * (1.0 + pre * (1.0 - gate))).astype(BF16)
         whole = (pre * gate).astype(BF16)
         for r in range(2):
             h = head_of(r, o)
             rows = slice(r * ROWS, (r + 1) * ROWS)
             act = whole[rows]
             wide = got_ref[r, G_AT + o * ROWS : G_AT + (o + 1) * ROWS, :].astype(F32)
-            xw_ref[o, rows] = (act.astype(F32) * pair_column(cols_ref, 2, r, o, left)).astype(BF16)
-            gw_ref[o, rows] = (wide * pair_column(cols_ref, 3, r, o, left)).astype(BF16)
+            xw_ref[rows, lanes] = (act.astype(F32) * pair_column(cols_ref, 2, r, o, left)).astype(BF16)
+            gw_ref[rows, lanes] = (wide * pair_column(cols_ref, 3, r, o, left)).astype(BF16)
             skip = jnp.where(left[:1], rows_ref[6 * n + h : 6 * n + h + 1, :], rows_ref[6 * n + h + 1 : 6 * n + h + 2, :])
             dx = skip * wide
             both = jnp.sum(act.astype(F32) * wide, 0, keepdims=True)
@@ -267,82 +282,99 @@
                 row_ref[h + k : h + k + 1, :] = dot(ones, both)[:1]
                 row_ref[n + h + k : n + h + k + 1, :] = dot(ones, both, NT)[:1]
                 dx = dx + dot(mixing.astype(BF16), own)
-            dx_ref[o, rows] = dx
+            dx_ref[rows, lanes] = dx.astype(BF16)
     for r in range(2):
         ds = dscores[r].astype(BF16)
         dbc_ref[r * ROWS : (r + 1) * ROWS, :LANES] = dot(ds, c[r])
         dbc_ref[r * ROWS : (r + 1) * ROWS, LANES:] = dot(ds, b[r], TN)
 
 
-def tap_sums(dpre, ext_ref):
-    sums = [jnp.sum(dpre * ext_ref[pl.ds(HALO - 3 + k, SEG), :], 0, keepdims=True) for k in range(4)]
+def tap_sums(dpre_ref, ext_ref, o):
+    dpre = dpre_ref[o, HALO : HALO + SEG, :]
+    sums = [jnp.sum(dpre * ext_ref[o, pl.ds(HALO - 3 + k, SEG), :], 0, keepdims=True) for k in range(4)]
     return sums + [jnp.sum(dpre, 0, keepdims=True)]
 
 
 def last_body(
-    got_ref, halo_ref, rows_ref, cols_ref, bcact_ref, side_ref, states_ref,
+    got_ref, halo_ref, rows_ref, cols_ref, parts_ref, bcact_ref, side_ref, states_ref,
     near_ref, dx_ref, slope_ref, xw_ref, gw_ref, dbc_ref, slope2_ref, row_ref,
-    dpre_ref, gstep_ref, part_ref, ext_ref, ext2_ref, acc_ref,
+    dpre_ref, gstep_ref, part_ref, ext_ref, acc_ref, state_ref, later_ref, sums_ref,
 ):
     n = 2 * HEADS
-    left = iota((ROWS, LANES), 1) < 64
-    half = jnp.where((iota((8, LANES), 1) < 64) == (iota((8, LANES), 0) == 0), 1.0, 0.0).astype(BF16)
+    left = iota((1, LANES), 1) < 64
+    quarter = iota((1, WIDE), 1) // 64
     b = [bcact_ref[r * ROWS : (r + 1) * ROWS, :LANES] for r in range(2)]
     c = [bcact_ref[r * ROWS : (r + 1) * ROWS, LANES:] for r in range(2)]
-    db = [jnp.zeros((ROWS, LANES), F32) for _ in range(2)]
-    dc = [jnp.zeros((ROWS, LANES), F32) for _ in range(2)]
+    fill(ext_ref, got_ref, halo_ref)
     part_ref[...] = jnp.zeros(part_ref.shape, F32)
-    pad = jnp.zeros((HALO, HALF + 2 * LANES), F32)
-    dpre_ref[:HALO, :] = pad
-    dpre_ref[HALO + SEG :, :] = pad
-    for o in range(PAIRS):
-        lanes = slice(o * LANES, (o + 1) * LANES)
-        state, later = states_ref[o, :ROWS, :], states_ref[o, ROWS:, :]
+    pad = jnp.zeros((PAIRS + 2, HALO, LANES), F32)
+    dpre_ref[:, :HALO, :] = pad
+    dpre_ref[:, HALO + SEG :, :] = pad
+    over = spreader()
+    for m in range(HALF // WIDE):
+        lanes = slice(m * WIDE, (m + 1) * WIDE)
         total = []
         for r in range(2):
-            h = 3 * n + head_of(r, o)
-            total.append(jnp.where(left[:1], cols_ref[ROWS - 1 :, h : h + 1], cols_ref[ROWS - 1 :, h + 1 : h + 2]))
-        states = [state, (total[0] * state.astype(F32) + near_ref[o, :ROWS, :].astype(F32)).astype(BF16)]
-        laters = [(total[1] * later.astype(F32) + near_ref[o, ROWS:, :].astype(F32)).astype(BF16), later]
-        ext = ext_ref.at[o % 2]
-        fill_pair(ext, got_ref, halo_ref, o)
+            h = 3 * n + r * HEADS + 4 * m
+            row = cols_ref[ROWS - 1 :, h : h + 1]
+            for k in range(1, 4):
+                row = jnp.where(quarter >= k, cols_ref[ROWS - 1 :, h + k : h + k + 1], row)
+            total.append(row)
+        state, later, near, near_later = (
+            beside(ref[2 * m, rows, :], ref[2 * m + 1, rows, :])
+            for ref in (states_ref, near_ref)
+            for rows in (slice(0, ROWS), slice(ROWS, 2 * ROWS))
+        )
+        states = [state, (total[0] * state.astype(F32) + near.astype(F32)).astype(BF16)]
+        laters = [(total[1] * later.astype(F32) + near_later.astype(F32)).astype(BF16), later]
         for r in range(2):
             rows = slice(r * ROWS, (r + 1) * ROWS)
-            h = head_of(r, o)
-            xw = xw_ref[o, rows]
-            gw = gw_ref[o, rows]
-            carried = dot(c[r], states[r]) * gw.astype(F32)
-            dxw = dot(b[r], laters[r]).astype(BF16).astype(F32)
-            dc[r] = dc[r] + dot(gw, states[r], NT)
-            db[r] = db[r] + dot(xw, laters[r], NT)
-            acc_ref[h : h + 2, :] = dot(half, carried.astype(BF16), NT)[:2]
-            acc_ref[n + h : n + h + 2, :] = dot(half, (dxw * xw.astype(F32)).astype(BF16), NT)[:2]
+            state_ref[r, :, lanes] = states[r]
+            later_ref[r, :, lanes] = laters[r]
+            xw = xw_ref[rows, lanes].astype(F32)
+            sums_ref[rows, lanes] = (dot(c[r], states[r]) * gw_ref[rows, lanes].astype(F32)).astype(BF16)
+            dxw = dot(b[r], laters[r])
+            sums_ref[rows, HALF + m * WIDE : HALF + (m + 1) * WIDE] = (dxw * xw).astype(BF16)
             both = jnp.sum(states[r].astype(F32) * laters[r].astype(F32), 0, keepdims=True)
-            acc_ref[2 * n + h : 2 * n + h + 1, :] = jnp.where(left[:1], both, 0.0)
-            acc_ref[2 * n + h + 1 : 2 * n + h + 2, :] = jnp.where(left[:1], 0.0, both)
-            dact = dx_ref[o, rows] + pair_column(cols_ref, 2, r, o, left) * dxw
-            dpre_ref[HALO + r * ROWS : HALO + (r + 1) * ROWS, lanes] = dact.astype(BF16).astype(F32) * slope_ref[o, rows]
-        sums = tap_sums(dpre_ref[HALO : HALO + SEG, lanes], ext)
+            for k in range(2):
+                h = head_of(r, 2 * m + k)
+                mine = both[:, k * LANES : (k + 1) * LANES]
+                acc_ref[h : h + 1, :] = jnp.where(left, mine, 0.0)
+                acc_ref[h + 1 : h + 2, :] = jnp.where(left, 0.0, mine)
+            dact = dx_ref[rows, lanes].astype(F32) + dot(parts_ref[0, r, m], over, TN) * dxw
+            dact = dact * slope_ref[rows, lanes].astype(F32)
+            for k in range(2):
+                dpre_ref[2 * m + k, HALO + r * ROWS : HALO + (r + 1) * ROWS, :] = dact[:, k * LANES : (k + 1) * LANES]
+    dpre2 = []
+    for r in range(2):
+        rows = slice(r * ROWS, (r + 1) * ROWS)
+        dpre2.append(beside(dot(xw_ref[rows, :], later_ref[r], NT), dot(gw_ref[rows, :], state_ref[r], NT)))
+    dpre2 = (dbc_ref[...] + jnp.concatenate(dpre2, 0)) * slope2_ref[...]
+    for k in range(2):
+        dpre_ref[PAIRS + k, HALO : HALO + SEG, :] = dpre2[:, k * LANES : (k + 1) * LANES]
+    for o in range(PAIRS + 2):
+        sums = tap_sums(dpre_ref, ext_ref, o)
         for k in range(5):
-            part_ref[o, k : k + 1, :] = sums[k]
-    fill_bc(ext2_ref, got_ref, halo_ref)
-    dpre2 = jnp.concatenate([jnp.concatenate(db, 0), jnp.concatenate(dc, 0)], 1)
-    dpre2 = (dbc_ref[...] + dpre2) * slope2_ref[...]
-    dpre_ref[HALO : HALO + SEG, HALF:] = dpre2
-    sums = tap_sums(dpre2, ext2_ref)
-    for k in range(5):
-        part_ref[k, 5:6, :] = sums[k][:, :LANES]
-        part_ref[k, 6:7, :] = sums[k][:, LANES:]
+            if o < PAIRS:
+                part_ref[o, k : k + 1, :] = sums[k]
+            else:
+                part_ref[k, 5 + o - PAIRS : 6 + o - PAIRS, :] = sums[k]
+    lane = iota((16, LANES), 1)
+    pick = [jnp.where(lane == h, 1.0, 0.0).astype(BF16) for h in range(n)]
+    pick = jnp.concatenate([p for p in pick for _ in range(4)], 0)
+    by_head = dot(sums_ref[...], pick)
+    by_head = [by_head[r * ROWS : (r + 1) * ROWS].T for r in range(2)]
+    entered = jnp.concatenate([t[:HEADS] for t in by_head], 0)
+    ended = jnp.concatenate([t[HEADS:n] for t in by_head], 0)
     step = rows_ref[n : 2 * n, :]
     gate = rows_ref[4 * n : 5 * n, :]
     rate = rows_ref[5 * n : 6 * n, :]
     total = rows_ref[3 * n : 4 * n, ROWS - 1 :]
     at_t = row_ref[:n, :]
     at_s = row_ref[n : 2 * n, :]
-    ended = acc_ref[n : 2 * n, :]
-    at_end = jnp.sum(ended, 1, keepdims=True) + total * jnp.sum(acc_ref[2 * n :, :], 1, keepdims=True)
+    at_end = jnp.sum(ended, 1, keepdims=True) + total * jnp.sum(acc_ref[...], 1, keepdims=True)
     final = iota((n, ROWS), 1) == ROWS - 1
-    dcumul = at_t - at_s + acc_ref[:n, :] - ended + jnp.where(final, at_end, 0.0)
+    dcumul = at_t - at_s + entered - ended + jnp.where(final, at_end, 0.0)
     onward = (iota((ROWS, ROWS), 0) >= iota((ROWS, ROWS), 1)).astype(F32)
     ddecay = dot(dcumul, onward, precision=HIGH)
     dstep = ((at_s + ended) / step + ddecay * rate) * gate
@@ -363,8 +395,8 @@
         rim = jnp.zeros((HALO, LANES), F32)
         for k in range(4):
             tap = taps_ref[k : k + 1, lanes]
-            own = own + tap * dpre_ref[pl.ds(HALO + 3 - k, SEG), lanes]
-            rim = rim + tap * dpre_ref[pl.ds(HALO - k, HALO), lanes]
+            own = own + tap * dpre_ref[o, pl.ds(HALO + 3 - k, SEG), :]
+            rim = rim + tap * dpre_ref[o, pl.ds(HALO - k, HALO), :]
         rim_ref[o, :, :] = rim.astype(BF16)
         if o < PAIRS:
             gx_ref[:, lanes] = own.astype(BF16)
@@ -465,30 +497,36 @@
     got = lax.all_to_all(packed, "seq", 0, 0, axis_index_groups=cores)
     tail = call(tail_body, [kept(PAIRS + 2, HALO, LANES, dtype=BF16)], [VMEM])(got)[0]
     halo = lax.ppermute(tail, "seq", [(i, i + 2) for i in range(n_seq - 2)])
-    by_row, by_col, taps, side = call(
+    by_row, by_col, taps, side, parts = call(
         steps_body,
-        [kept(7 * n, ROWS), kept(ROWS, 4 * n), kept(5, HALF + 2 * LANES), kept(8, LANES)],
+        [
+            kept(7 * n, ROWS),
+            kept(ROWS, 4 * n),
+            kept(5, HALF + 2 * LANES),
+            kept(8, LANES),
+            kept(2, 2, HALF // WIDE, 16, ROWS, dtype=BF16),
+        ],
         [VMEM, FAR, FAR, SMEM, SMEM, SMEM],
     )(got, conv_weight, conv_bias, step_bias, log_rate, skip_gain)
-    ext = [pltpu.VMEM((2, SEG + HALO, LANES), F32), pltpu.VMEM((SEG + HALO, 2 * LANES), F32)]
+    ext = [pltpu.VMEM((PAIRS + 2, SEG + HALO, LANES), F32)]
     bc_act, near, send = call(
         first_body,
         [
             kept(SEG, 2 * LANES, dtype=BF16),
-            far(PAIRS, 2 * ROWS, LANES, dtype=BF16),
-            shape(PAIRS, SENT, LANES, dtype=BF16),
+            kept(PAIRS, 2 * ROWS, LANES, dtype=BF16),
+            far(PAIRS, SENT, LANES, dtype=BF16),
         ],
         [VMEM] * 4,
         ext,
-    )(got, halo, taps, by_col)
+    )(got, halo, taps, parts)
     sent = lax.all_to_all(send, "seq", 0, 0, axis_index_groups=ring)
     dx, slope, xw, gw, dbc, slope2, row = call(
         inner_body,
         [
-            far(PAIRS, SEG, LANES),
-            far(PAIRS, SEG, LANES),
-            far(PAIRS, SEG, LANES, dtype=BF16),
-            far(PAIRS, SEG, LANES, dtype=BF16),
+            far(SEG, HALF, dtype=BF16),
+            far(SEG, HALF, dtype=BF16),
+            far(SEG, HALF, dtype=BF16),
+            far(SEG, HALF, dtype=BF16),
             far(SEG, 2 * LANES),
             far(SEG, 2 * LANES),
             far(3 * n, ROWS),
@@ -496,14 +534,20 @@
         [VMEM] * 6,
         ext,
     )(got, halo, taps, by_row, by_col, bc_act)
-    scanned = call(scan_body, [far(chips, 2 * ROWS, LANES, dtype=BF16)], [VMEM])(sent)[0]
+    scanned = call(scan_body, [shape(chips, 2 * ROWS, LANES, dtype=BF16)], [VMEM])(sent)[0]
     states = lax.all_to_all(scanned, "seq", 0, 0, axis_index_groups=ring)
     dpre, gstep, part = call(
         last_body,
-        [kept(SEG + 2 * HALO, HALF + 2 * LANES), far(n, ROWS), far(PAIRS, 8, LANES)],
-        [VMEM] * 7 + [FAR] * 8,
-        ext + [pltpu.VMEM((3 * n, ROWS), F32)],
-    )(got, halo, by_row, by_col, bc_act, side, states, near, dx, slope, xw, gw, dbc, slope2, row)
+        [kept(PAIRS + 2, SEG + 2 * HALO, LANES), far(n, ROWS), far(PAIRS, 8, LANES)],
+        [VMEM] * 13 + [FAR] * 3,
+        ext
+        + [
+            pltpu.VMEM((n, ROWS), F32),
+            pltpu.VMEM((2, ROWS, HALF), BF16),
+            pltpu.VMEM((2, ROWS, HALF), BF16),
+            pltpu.VMEM((SEG, 2 * HALF), BF16),
+        ],
+    )(got, halo, by_row, by_col, parts, bc_act, side, states, near, dx, slope, xw, gw, dbc, slope2, row)
     part = lax.all_to_all(part, "seq", 0, 0, axis_index_groups=ring)
     part = spread(part, n_dp, 1.0)
     part = lax.all_to_all(part, "dp", 0, 0)

time: 116 us -> 121 us (1.043)
  local copies, waits for them, and re-layouts: 0 us -> 6.74 us
  Pallas kernels: 21.9 us -> 19.3 us
    unnamed x0 -> x16, local copies, waits for them, and re-layouts: none -> 6.74 us
    pallas_call x13, Pallas kernels: 21.9 us -> 19.3 us  [call(): kernel(*(pltpu.with_memory_space_constraint(a, pltpu.VMEM if spec is VMEM...]
where the time goes in v4:
time: 121 us; the launch traced here: 120 us
  starting transfers between devices  36.8 us (30%)
  blocking collectives  34.2 us (28%)
  waiting for transfers between devices  22.4 us (19%)
  Pallas kernels  19.3 us (16%)
  local copies, waits for them, and re-layouts  6.74 us (6%)
    all_to_all x1, blocking collectives, compute(): sent = lax.all_to_all(send, 'seq', 0, 0, axis_index_groups=ring)  23.1 us
    pallas_call x13, Pallas kernels, call(): kernel(*(pltpu.with_memory_space_constraint(a, pltpu.VMEM if spec is VMEM...  19.3 us
    all_to_all x1, blocking collectives, compute(): got = lax.all_to_all(packed, 'seq', 0, 0, axis_index_groups=cores)  11.2 us
    all_to_all x1, starting transfers between devices, compute(): part = lax.all_to_all(part, 'seq', 0, 0)  10.1 us
    all_to_all x1, starting transfers between devices, compute(): part = lax.all_to_all(part, 'dp', 0, 0)  9.67 us
    all_to_all x1, waiting for transfers between devices, compute(): states = lax.all_to_all(scanned, 'seq', 0, 0, axis_index_groups=ring)  9.65 us
    ppermute x1, starting transfers between devices, compute(): came = lax.ppermute(give, 'seq', [(i, i ^ 1) for i in range(n_seq)])  7.52 us
    all_to_all x1, waiting for transfers between devices, compute(): part = lax.all_to_all(part, 'seq', 0, 0)  6.85 us
  transfers between devices with their start and end apart: 7, of which 4 were waited for; matrix products, arithmetic and copies ran while one was open for 0% of the time, Pallas kernels for 8%

profile of v4, /device:TPU:1, one launch (start us, length us, event | category | flops | bytes accessed | tf_op | source)
XLA Modules:
  0.0 120.2 jit_solution(11450264593808524116)
XLA Ops:
  0.6 1.4 %shard_map.152 = bf16[2,2368,128]{2,1,0:T(8,128)(2,1)S(1)} custom-call(bf16[128,2048]{1,0:T(8,128)(2,1)} %bitcast.7, bf16[128,256]{1,0:T(8,128)(2,1)} %bitcast.9, bf16[128,2048]{1,0:T(8,128)(2,1)} %bitcast.8, f32[32,128]{1,0:T(8,128)} %bitcast.10), custom_call_target="tpu_custom_call" | custom-call | tf_op jit(solution)/shard_map/pallas_call | solution.py:44
  2.1 11.2 %all_to_all.30.got_ref = bf16[2,2368,128]{2,1,0:T(8,128)(2,1)S(1)} all-to-all(bf16[2,2368,128]{2,1,0:T(8,128)(2,1)S(1)} %shard_map.152), channel_id=1, replica_groups={{0,1},{2,3},{4,5},{6,7},{8,9},{10,11},{12,13},{14,15},{16,17},{18,19},{..., dimensions={0} | all-to-all | bytes 2424832 | tf_op jit(solution)/shard_map/all_to_all | solution.py:497
  13.2 1.3 %collective-permute-start = (bf16[10,8,128]{2,1,0:T(8,128)(2,1)S(1)}, bf16[10,8,128]{2,1,0:T(8,128)(2,1)S(1)}, u32[]{:S(2)}, u32[]{:S(2)}) collective-permute-start(bf16[10,8,128]{2,1,0:T(8,128)(2,1)S(1)} %shard_map.153), channel_id=1, source_target_pairs={{0,2},{1,3},{2,4},{3,5},{4,6},{5,7},{6,8},{7,9},{8,10},{9,11},{10,... | collective-permute-start | bytes 61448 | tf_op jit(solution)/shard_map/ppermute | solution.py:499
  14.5 1.2 %shard_map.154 = (f32[224,128]{1,0:T(8,128)S(1)}, f32[128,128]{1,0:T(8,128)S(1)}, f32[5,1280]{1,0:T(8,128)S(1)}, f32[8,128]{1,0:T(8,128)S(1)}, bf16[2,2,4,16,128]{4,3,2,1,0:T(8,128)(2,1)S(1)}) custom-call(bf16[2,2368,128]{2,1,0:T(8,128)(2,1)S(1)} %all_to_all.30.got_ref, f32[4,2304]{1,0:T(4,128)} %weight_ref.1, f32[2304]{0:T(1024)} %offset_ref.1, ...), custom_call_target="tpu_custom_call" | custom-call | tf_op jit(solution)/shard_map/pallas_call | solution.py:44
  15.7 0.0 collective-permute-done.halo_ref
  15.8 0.0 copy-start.6
  15.8 2.7 %shard_map.155 = (bf16[256,256]{1,0:T(8,128)(2,1)S(1)}, bf16[8,256,128]{2,1,0:T(8,128)(2,1)S(1)}, bf16[8,264,128]{2,1,0:T(8,128)(2,1)}) custom-call(bf16[2,2368,128]{2,1,0:T(8,128)(2,1)S(1)} %all_to_all.30.got_ref, bf16[10,8,128]{2,1,0:T(8,128)(2,1)S(1)} %collective-permute-done.halo_ref, f32[5,1280]{1,0:T(8,128)S(1)} %get-tuple-element.44.taps_ref, ...), custom_call_target="tpu_custom_call" | custom-call | tf_op jit(solution)/shard_map/pallas_call | solution.py:44
  18.5 0.0 copy-start
  18.5 0.8 copy-done
  19.3 23.1 %all_to_all.31.got_ref = bf16[8,264,128]{2,1,0:T(8,128)(2,1)S(1)} all-to-all(bf16[8,264,128]{2,1,0:T(8,128)(2,1)} %get-tuple-element.47), channel_id=1, replica_groups={{0,2,4,6,8,10,12,14},{1,3,5,7,9,11,13,15},{16,18,20,22,24,26,28,30},{17..., dimensions={0} | all-to-all | bytes 1081344 | tf_op jit(solution)/shard_map/all_to_all | solution.py:522
  42.4 0.9 shard_map.156
  43.3 3.7 %all-to-all-start.2 = ((bf16[8,256,128]{2,1,0:T(8,128)(2,1)}), bf16[8,256,128]{2,1,0:T(8,128)(2,1)S(1)}, u32[]{:S(2)}, u32[]{:S(2)}) async-start(bf16[8,256,128]{2,1,0:T(8,128)(2,1)} %shard_map.156), calls=%async_computation.2 | async-start | bytes 1048576 | tf_op jit(solution)/shard_map/all_to_all | solution.py:538
  46.9 0.0 copy-done.6
  46.9 4.6 %shard_map.157 = (bf16[256,1024]{1,0:T(8,128)(2,1)}, bf16[256,1024]{1,0:T(8,128)(2,1)}, bf16[256,1024]{1,0:T(8,128)(2,1)}, bf16[256,1024]{1,0:T(8,128)(2,1)}, f3...) custom-call(bf16[2,2368,128]{2,1,0:T(8,128)(2,1)S(1)} %all_to_all.30.got_ref, ...), custom_call_target="tpu_custom_call" | custom-call | tf_op jit(solution)/shard_map/pallas_call | solution.py:44
  51.5 9.7 %all-to-all-done.2.states_ref = bf16[8,256,128]{2,1,0:T(8,128)(2,1)S(1)} async-done(((bf16[8,256,128]{2,1,0:T(8,128)(2,1)}), bf16[8,256,128]{2,1,0:T(8,128)(2,1)S(1)}, u32[]{:S(2)}, u32[]{:S(2)}) %all-to-all-start.2) | async-done | bytes 524320 | tf_op jit(solution)/shard_map/all_to_all | solution.py:538
  61.2 0.0 copy-start.1
  61.2 1.0 copy-done.1
  62.2 0.0 copy-start.2
  62.2 1.0 copy-done.2
  63.3 0.0 copy-start.3
  63.3 1.0 copy-done.3
  64.3 0.0 copy-start.4
  64.3 1.0 copy-done.4
  65.4 0.0 copy-start.5
  65.4 1.0 copy-done.5
  66.4 0.0 copy-start.7
  66.4 0.7 copy-done.7
  67.1 4.3 %shard_map.158 = (f32[10,272,128]{2,1,0:T(8,128)S(1)}, f32[32,128]{1,0:T(8,128)}, f32[8,8,128]{2,1,0:T(8,128)}) custom-call(bf16[2,2368,128]{2,1,0:T(8,128)(2,1)S(1)} %all_to_all.30.got_ref, bf16[10,8,128]{2,1,0:T(8,128)(2,1)S(1)} %copy-done.7, f32[224,128]{1,0:T(8,128)S(1)} %get-tuple-element.41.rows_ref, f32[128,128]{1,0:T(8,128)S(1)} %get-tuple-element.42.cols_ref, ...), custom_call_target="tpu_custom_call" | custom-call | tf_op jit(solution)/shard_map/pallas_call | solution.py:44
  71.4 3.3 %all-to-all-start.3 = ((f32[8,8,128]{2,1,0:T(8,128)}), f32[8,8,128]{2,1,0:T(8,128)S(1)}, u32[]{:S(2)}, u32[]{:S(2)}) async-start(f32[8,8,128]{2,1,0:T(8,128)} %get-tuple-element.68), calls=%async_computation.3 | async-start | bytes 65536 | tf_op jit(solution)/shard_map/all_to_all | solution.py:551
  74.8 0.4 shard_map.159
  75.1 1.3 %collective-permute-start.1 = (bf16[10,8,128]{2,1,0:T(8,128)(2,1)S(1)}, bf16[10,8,128]{2,1,0:T(8,128)(2,1)S(1)}, u32[]{:S(2)}, u32[]{:S(2)}) collective-permute-start(bf16[10,8,128]{2,1,0:T(8,128)(2,1)S(1)} %get-tuple-element.59), channel_id=1, source_target_pairs={{2,0},{3,1},{4,2},{5,3},{6,4},{7,5},{8,6},{9,7},{10,8},{11,9},{12,... | collective-permute-start | bytes 61448 | tf_op jit(solution)/shard_map/ppermute | solution.py:561
  76.4 5.1 %all-to-all-done.3.in_ref = f32[8,8,128]{2,1,0:T(8,128)S(1)} async-done(((f32[8,8,128]{2,1,0:T(8,128)}), f32[8,8,128]{2,1,0:T(8,128)S(1)}, u32[]{:S(2)}, u32[]{:S(2)}) %all-to-all-start.3) | async-done | bytes 32800 | tf_op jit(solution)/shard_map/all_to_all | solution.py:551
  81.6 0.7 shard_map.162
  82.2 9.7 %all-to-all-start.4 = ((f32[32,8,128]{2,1,0:T(8,128)}), f32[32,8,128]{2,1,0:T(8,128)S(1)}, u32[]{:S(2)}, u32[]{:S(2)}) async-start(f32[32,8,128]{2,1,0:T(8,128)} %shard_map.162), calls=%async_computation.4 | async-start | bytes 262144 | tf_op jit(solution)/shard_map/all_to_all | solution.py:553
  91.9 0.0 collective-permute-done.1.back_ref
  91.9 0.9 shard_map.160
  92.8 7.5 %collective-permute-start.2 = (bf16[11,128,128]{2,1,0:T(8,128)(2,1)S(1)}, bf16[11,128,128]{2,1,0:T(8,128)(2,1)S(1)}, u32[]{:S(2)}, u32[]{:S(2)}) collective-permute-start(bf16[11,128,128]{2,1,0:T(8,128)(2,1)S(1)} %get-tuple-element.64), channel_id=1, source_target_pairs={{0,1},{1,0},{2,3},{3,2},{4,5},{5,4},{6,7},{7,6},{8,9},{9,8},{10,11... | collective-permute-start | bytes 1081352 | tf_op jit(solution)/shard_map/ppermute | solution.py:572
  100.3 0.7 all-to-all-done.4.in_ref
  101.1 0.7 shard_map.163
  101.7 10.1 %all-to-all-start.5 = ((f32[16,8,128]{2,1,0:T(8,128)}), f32[16,8,128]{2,1,0:T(8,128)S(1)}, u32[]{:S(2)}, u32[]{:S(2)}) async-start(f32[16,8,128]{2,1,0:T(8,128)} %shard_map.163), calls=%async_computation.5 | async-start | bytes 131072 | tf_op jit(solution)/shard_map/all_to_all | solution.py:555
  111.8 0.0 collective-permute-done.2.came_ref
  111.8 1.0 shard_map.161
  112.7 6.9 %all-to-all-done.5.in_ref = f32[16,8,128]{2,1,0:T(8,128)S(1)} async-done(((f32[16,8,128]{2,1,0:T(8,128)}), f32[16,8,128]{2,1,0:T(8,128)S(1)}, u32[]{:S(2)}, u32[]{:S(2)}) %all-to-all-start.5) | async-done | bytes 65568 | tf_op jit(solution)/shard_map/all_to_all | solution.py:555
  119.6 0.6 shard_map.164
  (1 shorter events, 0.0 us)
Async XLA Ops:
  13.2 2.5 %collective-permute-start = (bf16[10,8,128]{2,1,0:T(8,128)(2,1)S(1)}, bf16[10,8,128]{2,1,0:T(8,128)(2,1)S(1)}, u32[]{:S(2)}, u32[]{:S(2)}) collective-permute-start(bf16[10,8,128]{2,1,0:T(8,128)(2,1)S(1)} %shard_map.153), channel_id=1, source_target_pairs={{0,2},{1,3},{2,4},{3,5},{4,6},{5,7},{6,8},{7,9},{8,10},{9,11},{10,... | collective-permute-start | bytes 61448 | tf_op jit(solution)/shard_map/ppermute | solution.py:499
  15.8 31.2 %copy-start.6 = (bf16[10,8,128]{2,1,0:T(8,128)(2,1)}, bf16[10,8,128]{2,1,0:T(8,128)(2,1)S(1)}, u32[]{:S(2)}) copy-start(bf16[10,8,128]{2,1,0:T(8,128)(2,1)S(1)} %collective-permute-done.halo_ref) | copy-start | bytes 61444
  18.5 0.8 copy-start
  43.3 17.9 %all-to-all-start.2 = ((bf16[8,256,128]{2,1,0:T(8,128)(2,1)}), bf16[8,256,128]{2,1,0:T(8,128)(2,1)S(1)}, u32[]{:S(2)}, u32[]{:S(2)}) async-start(bf16[8,256,128]{2,1,0:T(8,128)(2,1)} %shard_map.156), calls=%async_computation.2 | async-start | bytes 1048576 | tf_op jit(solution)/shard_map/all_to_all | solution.py:538
  61.2 1.0 copy-start.1
  62.2 1.0 copy-start.2
  63.3 1.0 copy-start.3
  64.3 1.0 copy-start.4
  65.4 1.0 copy-start.5
  66.4 0.7 copy-start.7
  71.4 10.1 %all-to-all-start.3 = ((f32[8,8,128]{2,1,0:T(8,128)}), f32[8,8,128]{2,1,0:T(8,128)S(1)}, u32[]{:S(2)}, u32[]{:S(2)}) async-start(f32[8,8,128]{2,1,0:T(8,128)} %get-tuple-element.68), calls=%async_computation.3 | async-start | bytes 65536 | tf_op jit(solution)/shard_map/all_to_all | solution.py:551
  75.1 16.8 %collective-permute-start.1 = (bf16[10,8,128]{2,1,0:T(8,128)(2,1)S(1)}, bf16[10,8,128]{2,1,0:T(8,128)(2,1)S(1)}, u32[]{:S(2)}, u32[]{:S(2)}) collective-permute-start(bf16[10,8,128]{2,1,0:T(8,128)(2,1)S(1)} %get-tuple-element.59), channel_id=1, source_target_pairs={{2,0},{3,1},{4,2},{5,3},{6,4},{7,5},{8,6},{9,7},{10,8},{11,9},{12,... | collective-permute-start | bytes 61448 | tf_op jit(solution)/shard_map/ppermute | solution.py:561
  82.2 18.8 %all-to-all-start.4 = ((f32[32,8,128]{2,1,0:T(8,128)}), f32[32,8,128]{2,1,0:T(8,128)S(1)}, u32[]{:S(2)}, u32[]{:S(2)}) async-start(f32[32,8,128]{2,1,0:T(8,128)} %shard_map.162), calls=%async_computation.4 | async-start | bytes 262144 | tf_op jit(solution)/shard_map/all_to_all | solution.py:553
  92.8 19.0 %collective-permute-start.2 = (bf16[11,128,128]{2,1,0:T(8,128)(2,1)S(1)}, bf16[11,128,128]{2,1,0:T(8,128)(2,1)S(1)}, u32[]{:S(2)}, u32[]{:S(2)}) collective-permute-start(bf16[11,128,128]{2,1,0:T(8,128)(2,1)S(1)} %get-tuple-element.64), channel_id=1, source_target_pairs={{0,1},{1,0},{2,3},{3,2},{4,5},{5,4},{6,7},{7,6},{8,9},{9,8},{10,11... | collective-permute-start | bytes 1081352 | tf_op jit(solution)/shard_map/ppermute | solution.py:572
  101.7 17.9 %all-to-all-start.5 = ((f32[16,8,128]{2,1,0:T(8,128)}), f32[16,8,128]{2,1,0:T(8,128)S(1)}, u32[]{:S(2)}, u32[]{:S(2)}) async-start(f32[16,8,128]{2,1,0:T(8,128)} %shard_map.163), calls=%async_computation.5 | async-start | bytes 131072 | tf_op jit(solution)/shard_map/all_to_all | solution.py:555

commit v5 on v4

--- a/solution.py
+++ b/solution.py
@@ -298,7 +298,7 @@
 def last_body(
     got_ref, halo_ref, rows_ref, cols_ref, parts_ref, bcact_ref, side_ref, states_ref,
     near_ref, dx_ref, slope_ref, xw_ref, gw_ref, dbc_ref, slope2_ref, row_ref,
-    dpre_ref, gstep_ref, part_ref, ext_ref, acc_ref, state_ref, later_ref, sums_ref,
+    dpre_ref, gstep_ref, sent_ref, ext_ref, acc_ref, state_ref, later_ref, sums_ref, part_ref,
 ):
     n = 2 * HEADS
     left = iota((1, LANES), 1) < 64
@@ -386,6 +386,8 @@
     at = iota((n, LANES), 1) - iota((n, LANES), 0) % HEADS - jnp.where(second, HEADS, 0)
     placed = jnp.where(at == 0, dbias, jnp.where(at == n, drate, jnp.where(at == 2 * n, dskip, 0.0)))
     part_ref[0, 7:8, :] = jnp.sum(placed, 0, keepdims=True)
+    for o in range(PAIRS):
+        sent_ref[o] = part_ref[o].astype(BF16)
 
 
 def input_body(dpre_ref, taps_ref, gx_ref, gbc_ref, rim_ref):
@@ -448,10 +450,10 @@
 
 
 def spread_body(in_ref, out_ref, *, scale):
-    total = in_ref[0]
+    total = in_ref[0].astype(F32)
     for j in range(1, in_ref.shape[0]):
-        total = total + in_ref[j]
-    total = total * scale
+        total = total + in_ref[j].astype(F32)
+    total = (total * scale).astype(BF16)
     for j in range(out_ref.shape[0]):
         out_ref[j] = total
 
@@ -460,20 +462,21 @@
     def body(in_ref, out_ref):
         spread_body(in_ref, out_ref, scale=scale)
 
-    return call(body, [far(count, 8, LANES)], [VMEM])(x)[0]
+    return call(body, [far(count, 8, LANES, dtype=BF16)], [VMEM])(x)[0]
 
 
 def unpack_body(in_ref, weight_ref, offset_ref, bias_ref, rate_ref, skip_ref):
-    heads = in_ref[0, 7:8, :] + in_ref[1, 7:8, :]
+    pieces = [in_ref[j].astype(F32) for j in range(2 * PAIRS)]
+    heads = pieces[0][7:8, :] + pieces[1][7:8, :]
     for k, ref in enumerate((bias_ref, rate_ref, skip_ref)):
         ref[...] = heads[:, k * 2 * HEADS : (k + 1) * 2 * HEADS].reshape(2 * HEADS)
     for k in range(2):
         for o in range(PAIRS):
             lanes = slice(k * HALF + o * LANES, k * HALF + (o + 1) * LANES)
-            weight_ref[:, lanes] = in_ref[2 * o + k, :4, :]
-            offset_ref[lanes] = in_ref[2 * o + k, 4, :]
+            weight_ref[:, lanes] = pieces[2 * o + k][:4]
+            offset_ref[lanes] = pieces[2 * o + k][4]
     for k in range(5):
-        both = in_ref[2 * k, 5:7, :] + in_ref[2 * k + 1, 5:7, :]
+        both = pieces[2 * k][5:7] + pieces[2 * k + 1][5:7]
         for m in range(2):
             lanes = slice(2 * HALF + m * LANES, 2 * HALF + (m + 1) * LANES)
             if k < 4:
@@ -538,7 +541,7 @@
     states = lax.all_to_all(scanned, "seq", 0, 0, axis_index_groups=ring)
     dpre, gstep, part = call(
         last_body,
-        [kept(PAIRS + 2, SEG + 2 * HALO, LANES), far(n, ROWS), far(PAIRS, 8, LANES)],
+        [kept(PAIRS + 2, SEG + 2 * HALO, LANES), far(n, ROWS), far(PAIRS, 8, LANES, dtype=BF16)],
         [VMEM] * 13 + [FAR] * 3,
         ext
         + [
@@ -546,6 +549,7 @@
             pltpu.VMEM((2, ROWS, HALF), BF16),
             pltpu.VMEM((2, ROWS, HALF), BF16),
             pltpu.VMEM((SEG, 2 * HALF), BF16),
+            pltpu.VMEM((PAIRS, 8, LANES), F32),
         ],
     )(got, halo, by_row, by_col, parts, bc_act, side, states, near, dx, slope, xw, gw, dbc, slope2, row)
     part = lax.all_to_all(part, "seq", 0, 0, axis_index_groups=ring)

time: 121 us -> 126 us (1.041)
  blocking collectives: 34.2 us -> 75.2 us
  starting transfers between devices: 36.8 us -> 13.5 us
  waiting for transfers between devices: 22.4 us -> 13 us
  local copies, waits for them, and re-layouts: 6.74 us -> 4.17 us
    all_to_all x0 -> x3, blocking collectives: none -> 40.9 us  [the longest x1 18.6 us: compute(): part = lax.all_to_all(part, 'dp', 0, 0)]
    all_to_all x3 -> x0, starting transfers between devices: 23.1 us -> none  [the longest x1 10.1 us: compute(): part = lax.all_to_all(part, 'seq', 0, 0)]
    all_to_all x3 -> x0, waiting for transfers between devices: 12.7 us -> none  [the longest x1 6.85 us: compute(): part = lax.all_to_all(part, 'seq', 0, 0)]
    ppermute x1, waiting for transfers between devices: 0.01 us -> 3.23 us  [compute(): back = lax.ppermute(rim, 'seq', [(i, i - 2) for i in range(2, n_seq)])]
    unnamed x16 -> x10, local copies, waits for them, and re-layouts: 6.74 us -> 4.17 us
  transfers between devices with their start and end apart: 7 -> 4, of which waited for: 4 -> 2; matrix products, arithmetic and copies ran while one was open for 0% -> 0% of each run, Pallas kernels for 8% -> 6%
where the time goes in v5:
time: 126 us
  blocking collectives  75.2 us (60%)
  Pallas kernels  19 us (15%)
  starting transfers between devices  13.5 us (11%)
  waiting for transfers between devices  13 us (10%)
  local copies, waits for them, and re-layouts  4.17 us (3%)
    all_to_all x1, blocking collectives, compute(): sent = lax.all_to_all(send, 'seq', 0, 0, axis_index_groups=ring)  23.1 us
    pallas_call x13, Pallas kernels, call(): kernel(*(pltpu.with_memory_space_constraint(a, pltpu.VMEM if spec is VMEM...  19 us
    all_to_all x1, blocking collectives, compute(): part = lax.all_to_all(part, 'dp', 0, 0)  18.6 us
    all_to_all x1, blocking collectives, compute(): part = lax.all_to_all(part, 'seq', 0, 0)  13.3 us
    all_to_all x1, blocking collectives, compute(): got = lax.all_to_all(packed, 'seq', 0, 0, axis_index_groups=cores)  11.2 us
    all_to_all x1, waiting for transfers between devices, compute(): states = lax.all_to_all(scanned, 'seq', 0, 0, axis_index_groups=ring)  9.78 us
    all_to_all x1, blocking collectives, compute(): part = lax.all_to_all(part, 'seq', 0, 0, axis_index_groups=ring)  8.98 us
    ppermute x1, starting transfers between devices, compute(): came = lax.ppermute(give, 'seq', [(i, i ^ 1) for i in range(n_seq)])  7.25 us
  transfers between devices with their start and end apart: 4, of which 2 were waited for; matrix products, arithmetic and copies ran while one was open for 0% of the time, Pallas kernels for 6%

profile of v5, /device:TPU:1, one launch (start us, length us, event | category | flops | bytes accessed | tf_op | source)
XLA Modules:
  0.0 125.6 jit_solution(5206833598359115297)
XLA Ops:
  0.6 1.4 %shard_map.152 = bf16[2,2368,128]{2,1,0:T(8,128)(2,1)S(1)} custom-call(bf16[128,2048]{1,0:T(8,128)(2,1)} %bitcast.7, bf16[128,256]{1,0:T(8,128)(2,1)} %bitcast.9, bf16[128,2048]{1,0:T(8,128)(2,1)} %bitcast.8, f32[32,128]{1,0:T(8,128)} %bitcast.10), custom_call_target="tpu_custom_call" | custom-call | tf_op jit(solution)/shard_map/pallas_call | solution.py:44
  2.1 11.2 %all_to_all.30.got_ref = bf16[2,2368,128]{2,1,0:T(8,128)(2,1)S(1)} all-to-all(bf16[2,2368,128]{2,1,0:T(8,128)(2,1)S(1)} %shard_map.152), channel_id=1, replica_groups={{0,1},{2,3},{4,5},{6,7},{8,9},{10,11},{12,13},{14,15},{16,17},{18,19},{..., dimensions={0} | all-to-all | bytes 2424832 | tf_op jit(solution)/shard_map/all_to_all | solution.py:500
  13.2 1.3 %collective-permute-start = (bf16[10,8,128]{2,1,0:T(8,128)(2,1)S(1)}, bf16[10,8,128]{2,1,0:T(8,128)(2,1)S(1)}, u32[]{:S(2)}, u32[]{:S(2)}) collective-permute-start(bf16[10,8,128]{2,1,0:T(8,128)(2,1)S(1)} %shard_map.153), channel_id=1, source_target_pairs={{0,2},{1,3},{2,4},{3,5},{4,6},{5,7},{6,8},{7,9},{8,10},{9,11},{10,... | collective-permute-start | bytes 61448 | tf_op jit(solution)/shard_map/ppermute | solution.py:502
  14.5 1.2 shard_map.154
  15.7 0.0 collective-permute-done.halo_ref
  15.7 2.7 %shard_map.155 = (bf16[256,256]{1,0:T(8,128)(2,1)S(1)}, bf16[8,256,128]{2,1,0:T(8,128)(2,1)S(1)}, bf16[8,264,128]{2,1,0:T(8,128)(2,1)}) custom-call(bf16[2,2368,128]{2,1,0:T(8,128)(2,1)S(1)} %all_to_all.30.got_ref, bf16[10,8,128]{2,1,0:T(8,128)(2,1)S(1)} %collective-permute-done.halo_ref, f32[5,1280]{1,0:T(8,128)S(1)} %get-tuple-element.44.taps_ref, ...), custom_call_target="tpu_custom_call" | custom-call | tf_op jit(solution)/shard_map/pallas_call | solution.py:44
  18.5 23.1 %all_to_all.31.got_ref = bf16[8,264,128]{2,1,0:T(8,128)(2,1)S(1)} all-to-all(bf16[8,264,128]{2,1,0:T(8,128)(2,1)} %get-tuple-element.47), channel_id=1, replica_groups={{0,2,4,6,8,10,12,14},{1,3,5,7,9,11,13,15},{16,18,20,22,24,26,28,30},{17..., dimensions={0} | all-to-all | bytes 1081344 | tf_op jit(solution)/shard_map/all_to_all | solution.py:525
  41.6 0.9 shard_map.156
  42.5 3.7 %all-to-all-start.2 = ((bf16[8,256,128]{2,1,0:T(8,128)(2,1)}), bf16[8,256,128]{2,1,0:T(8,128)(2,1)S(1)}, u32[]{:S(2)}, u32[]{:S(2)}) async-start(bf16[8,256,128]{2,1,0:T(8,128)(2,1)} %shard_map.156), calls=%async_computation.2 | async-start | bytes 1048576 | tf_op jit(solution)/shard_map/all_to_all | solution.py:541
  46.1 4.5 %shard_map.157 = (bf16[256,1024]{1,0:T(8,128)(2,1)}, bf16[256,1024]{1,0:T(8,128)(2,1)}, bf16[256,1024]{1,0:T(8,128)(2,1)}, bf16[256,1024]{1,0:T(8,128)(2,1)}, f3...) custom-call(bf16[2,2368,128]{2,1,0:T(8,128)(2,1)S(1)} %all_to_all.30.got_ref, ...), custom_call_target="tpu_custom_call" | custom-call | tf_op jit(solution)/shard_map/pallas_call | solution.py:44
  50.6 9.8 %all-to-all-done.2.states_ref = bf16[8,256,128]{2,1,0:T(8,128)(2,1)S(1)} async-done(((bf16[8,256,128]{2,1,0:T(8,128)(2,1)}), bf16[8,256,128]{2,1,0:T(8,128)(2,1)S(1)}, u32[]{:S(2)}, u32[]{:S(2)}) %all-to-all-start.2) | async-done | bytes 524320 | tf_op jit(solution)/shard_map/all_to_all | solution.py:541
  60.4 0.0 copy-start
  60.4 1.0 copy-done
  61.4 0.0 copy-start.1
  61.4 1.0 copy-done.1
  62.5 0.0 copy-start.2
  62.5 1.0 copy-done.2
  63.5 0.0 copy-start.3
  63.5 1.0 copy-done.3
  64.6 4.1 %shard_map.158 = (f32[10,272,128]{2,1,0:T(8,128)S(1)}, f32[32,128]{1,0:T(8,128)}, bf16[8,8,128]{2,1,0:T(8,128)(2,1)}) custom-call(bf16[2,2368,128]{2,1,0:T(8,128)(2,1)S(1)} %all_to_all.30.got_ref, bf16[10,8,128]{2,1,0:T(8,128)(2,1)S(1)} %collective-permute-done.halo_ref, f32[224,128]{1,0:T(8,128)S(1)} %get-tuple-element.41.rows_ref, ...), custom_call_target="tpu_custom_call" | custom-call | tf_op jit(solution)/shard_map/pallas_call | solution.py:44
  68.7 0.0 copy-start.4
  68.7 0.4 shard_map.159
  69.1 1.3 %collective-permute-start.1 = (bf16[10,8,128]{2,1,0:T(8,128)(2,1)S(1)}, bf16[10,8,128]{2,1,0:T(8,128)(2,1)S(1)}, u32[]{:S(2)}, u32[]{:S(2)}) collective-permute-start(bf16[10,8,128]{2,1,0:T(8,128)(2,1)S(1)} %get-tuple-element.59), channel_id=1, source_target_pairs={{2,0},{3,1},{4,2},{5,3},{6,4},{7,5},{8,6},{9,7},{10,8},{11,9},{12,... | collective-permute-start | bytes 61448 | tf_op jit(solution)/shard_map/ppermute | solution.py:565
  70.4 3.2 %collective-permute-done.1.back_ref = bf16[10,8,128]{2,1,0:T(8,128)(2,1)S(1)} collective-permute-done((bf16[10,8,128]{2,1,0:T(8,128)(2,1)S(1)}, bf16[10,8,128]{2,1,0:T(8,128)(2,1)S(1)}, u32[]{:S(2)}, u32[]{:S(2)}) %collective-permute-start.1) | collective-permute-done | bytes 20512 | tf_op jit(solution)/shard_map/ppermute | solution.py:565
  73.6 0.9 shard_map.160
  74.5 7.3 %collective-permute-start.2 = (bf16[11,128,128]{2,1,0:T(8,128)(2,1)S(1)}, bf16[11,128,128]{2,1,0:T(8,128)(2,1)S(1)}, u32[]{:S(2)}, u32[]{:S(2)}) collective-permute-start(bf16[11,128,128]{2,1,0:T(8,128)(2,1)S(1)} %get-tuple-element.64), channel_id=1, source_target_pairs={{0,1},{1,0},{2,3},{3,2},{4,5},{5,4},{6,7},{7,6},{8,9},{9,8},{10,11... | collective-permute-start | bytes 1081352 | tf_op jit(solution)/shard_map/ppermute | solution.py:576
  81.7 0.0 copy-done.4
  81.7 9.0 %all_to_all.32.in_ref = bf16[8,8,128]{2,1,0:T(8,128)(2,1)S(1)} all-to-all(bf16[8,8,128]{2,1,0:T(8,128)(2,1)S(1)} %copy-done.4), channel_id=1, replica_groups={{0,2,4,6,8,10,12,14},{1,3,5,7,9,11,13,15},{16,18,20,22,24,26,28,30},{17..., dimensions={0} | all-to-all | bytes 32768 | tf_op jit(solution)/shard_map/all_to_all | solution.py:555
  90.7 0.6 shard_map.162
  91.3 18.6 %all_to_all.33.in_ref = bf16[32,8,128]{2,1,0:T(8,128)(2,1)S(1)} all-to-all(bf16[32,8,128]{2,1,0:T(8,128)(2,1)} %shard_map.162), channel_id=1, replica_groups=mesh['dp'=32,'seq'=16] {'dp'}, dimensions={0} | all-to-all | bytes 131072 | tf_op jit(solution)/shard_map/all_to_all | solution.py:557
  110.0 0.7 shard_map.163
  110.6 13.3 %all_to_all.34.in_ref = bf16[16,8,128]{2,1,0:T(8,128)(2,1)S(1)} all-to-all(bf16[16,8,128]{2,1,0:T(8,128)(2,1)} %shard_map.163), channel_id=1, replica_groups=mesh['dp'=32,'seq'=16] {'seq'}, dimensions={0} | all-to-all | bytes 65536 | tf_op jit(solution)/shard_map/all_to_all | solution.py:559
  123.9 0.6 shard_map.164
  124.6 0.0 collective-permute-done.2.came_ref
  124.6 1.0 shard_map.161
  (1 shorter events, 0.0 us)
Async XLA Ops:
  13.2 2.5 %collective-permute-start = (bf16[10,8,128]{2,1,0:T(8,128)(2,1)S(1)}, bf16[10,8,128]{2,1,0:T(8,128)(2,1)S(1)}, u32[]{:S(2)}, u32[]{:S(2)}) collective-permute-start(bf16[10,8,128]{2,1,0:T(8,128)(2,1)S(1)} %shard_map.153), channel_id=1, source_target_pairs={{0,2},{1,3},{2,4},{3,5},{4,6},{5,7},{6,8},{7,9},{8,10},{9,11},{10,... | collective-permute-start | bytes 61448 | tf_op jit(solution)/shard_map/ppermute | solution.py:502
  42.5 17.9 %all-to-all-start.2 = ((bf16[8,256,128]{2,1,0:T(8,128)(2,1)}), bf16[8,256,128]{2,1,0:T(8,128)(2,1)S(1)}, u32[]{:S(2)}, u32[]{:S(2)}) async-start(bf16[8,256,128]{2,1,0:T(8,128)(2,1)} %shard_map.156), calls=%async_computation.2 | async-start | bytes 1048576 | tf_op jit(solution)/shard_map/all_to_all | solution.py:541
  60.4 1.0 copy-start
  61.4 1.0 copy-start.1
  62.5 1.0 copy-start.2
  63.5 1.0 copy-start.3
  68.7 13.0 %copy-start.4 = (bf16[8,8,128]{2,1,0:T(8,128)(2,1)S(1)}, bf16[8,8,128]{2,1,0:T(8,128)(2,1)}, u32[]{:S(2)}) copy-start(bf16[8,8,128]{2,1,0:T(8,128)(2,1)} %get-tuple-element.68) | copy-start | bytes 49156
  69.1 4.5 %collective-permute-start.1 = (bf16[10,8,128]{2,1,0:T(8,128)(2,1)S(1)}, bf16[10,8,128]{2,1,0:T(8,128)(2,1)S(1)}, u32[]{:S(2)}, u32[]{:S(2)}) collective-permute-start(bf16[10,8,128]{2,1,0:T(8,128)(2,1)S(1)} %get-tuple-element.59), channel_id=1, source_target_pairs={{2,0},{3,1},{4,2},{5,3},{6,4},{7,5},{8,6},{9,7},{10,8},{11,9},{12,... | collective-permute-start | bytes 61448 | tf_op jit(solution)/shard_map/ppermute | solution.py:565
  74.5 50.1 %collective-permute-start.2 = (bf16[11,128,128]{2,1,0:T(8,128)(2,1)S(1)}, bf16[11,128,128]{2,1,0:T(8,128)(2,1)S(1)}, u32[]{:S(2)}, u32[]{:S(2)}) collective-permute-start(bf16[11,128,128]{2,1,0:T(8,128)(2,1)S(1)} %get-tuple-element.64), channel_id=1, source_target_pairs={{0,1},{1,0},{2,3},{3,2},{4,5},{5,4},{6,7},{7,6},{8,9},{9,8},{10,11... | collective-permute-start | bytes 1081352 | tf_op jit(solution)/shard_map/ppermute | solution.py:576

commit v6 on v5

--- a/solution.py
+++ b/solution.py
@@ -245,7 +245,7 @@
     fill(ext_ref, got_ref, halo_ref)
     pre = beside(preact(ext_ref, taps_ref, PAIRS), preact(ext_ref, taps_ref, PAIRS + 1))
     gate = jax.nn.sigmoid(pre)
-    slope2_ref[...] = gate * (1.0 + pre * (1.0 - gate))
+    slope2_ref[...] = (gate * (1.0 + pre * (1.0 - gate))).astype(BF16)
     causal = iota((ROWS, ROWS), 0) <= iota((ROWS, ROWS), 1)
     left = iota((ROWS, LANES), 1) < 64
     ones = jnp.ones((8, ROWS), BF16)
@@ -285,8 +285,8 @@
             dx_ref[rows, lanes] = dx.astype(BF16)
     for r in range(2):
         ds = dscores[r].astype(BF16)
-        dbc_ref[r * ROWS : (r + 1) * ROWS, :LANES] = dot(ds, c[r])
-        dbc_ref[r * ROWS : (r + 1) * ROWS, LANES:] = dot(ds, b[r], TN)
+        dbc_ref[r * ROWS : (r + 1) * ROWS, :LANES] = dot(ds, c[r]).astype(BF16)
+        dbc_ref[r * ROWS : (r + 1) * ROWS, LANES:] = dot(ds, b[r], TN).astype(BF16)
 
 
 def tap_sums(dpre_ref, ext_ref, o):
@@ -349,7 +349,7 @@
     for r in range(2):
         rows = slice(r * ROWS, (r + 1) * ROWS)
         dpre2.append(beside(dot(xw_ref[rows, :], later_ref[r], NT), dot(gw_ref[rows, :], state_ref[r], NT)))
-    dpre2 = (dbc_ref[...] + jnp.concatenate(dpre2, 0)) * slope2_ref[...]
+    dpre2 = (dbc_ref[...].astype(F32) + jnp.concatenate(dpre2, 0)) * slope2_ref[...].astype(F32)
     for k in range(2):
         dpre_ref[PAIRS + k, HALO : HALO + SEG, :] = dpre2[:, k * LANES : (k + 1) * LANES]
     for o in range(PAIRS + 2):
@@ -530,8 +530,8 @@
             far(SEG, HALF, dtype=BF16),
             far(SEG, HALF, dtype=BF16),
             far(SEG, HALF, dtype=BF16),
-            far(SEG, 2 * LANES),
-            far(SEG, 2 * LANES),
+            far(SEG, 2 * LANES, dtype=BF16),
+            far(SEG, 2 * LANES, dtype=BF16),
             far(3 * n, ROWS),
         ],
         [VMEM] * 6,

time: 126 us -> 126 us (level)
  no operation moved by 1% of the time
where the time goes in v6:
time: 126 us; the launch traced here: 125 us
  blocking collectives  75.2 us (60%)
  Pallas kernels  18.8 us (15%)
  starting transfers between devices  13.5 us (11%)
  waiting for transfers between devices  13.2 us (10%)
  local copies, waits for them, and re-layouts  4.17 us (3%)
    all_to_all x1, blocking collectives, compute(): sent = lax.all_to_all(send, 'seq', 0, 0, axis_index_groups=ring)  23.1 us
    pallas_call x13, Pallas kernels, call(): kernel(*(pltpu.with_memory_space_constraint(a, pltpu.VMEM if spec is VMEM...  18.8 us
    all_to_all x1, blocking collectives, compute(): part = lax.all_to_all(part, 'dp', 0, 0)  18.6 us
    all_to_all x1, blocking collectives, compute(): part = lax.all_to_all(part, 'seq', 0, 0)  13.3 us
    all_to_all x1, blocking collectives, compute(): got = lax.all_to_all(packed, 'seq', 0, 0, axis_index_groups=cores)  11.2 us
    all_to_all x1, waiting for transfers between devices, compute(): states = lax.all_to_all(scanned, 'seq', 0, 0, axis_index_groups=ring)  9.96 us
    all_to_all x1, blocking collectives, compute(): part = lax.all_to_all(part, 'seq', 0, 0, axis_index_groups=ring)  8.98 us
    ppermute x1, starting transfers between devices, compute(): came = lax.ppermute(give, 'seq', [(i, i ^ 1) for i in range(n_seq)])  7.24 us
  transfers between devices with their start and end apart: 4, of which 2 were waited for; matrix products, arithmetic and copies ran while one was open for 0% of the time, Pallas kernels for 6%

profile of v6, /device:TPU:1, one launch (start us, length us, event | category | flops | bytes accessed | tf_op | source)
XLA Modules:
  0.0 125.5 jit_solution(6006133437852945280)
XLA Ops:
  0.6 1.4 %shard_map.152 = bf16[2,2368,128]{2,1,0:T(8,128)(2,1)S(1)} custom-call(bf16[128,2048]{1,0:T(8,128)(2,1)} %bitcast.7, bf16[128,256]{1,0:T(8,128)(2,1)} %bitcast.9, bf16[128,2048]{1,0:T(8,128)(2,1)} %bitcast.8, f32[32,128]{1,0:T(8,128)} %bitcast.10), custom_call_target="tpu_custom_call" | custom-call | tf_op jit(solution)/shard_map/pallas_call | solution.py:44
  2.1 11.2 %all_to_all.30.got_ref = bf16[2,2368,128]{2,1,0:T(8,128)(2,1)S(1)} all-to-all(bf16[2,2368,128]{2,1,0:T(8,128)(2,1)S(1)} %shard_map.152), channel_id=1, replica_groups={{0,1},{2,3},{4,5},{6,7},{8,9},{10,11},{12,13},{14,15},{16,17},{18,19},{..., dimensions={0} | all-to-all | bytes 2424832 | tf_op jit(solution)/shard_map/all_to_all | solution.py:500
  13.2 1.3 %collective-permute-start = (bf16[10,8,128]{2,1,0:T(8,128)(2,1)S(1)}, bf16[10,8,128]{2,1,0:T(8,128)(2,1)S(1)}, u32[]{:S(2)}, u32[]{:S(2)}) collective-permute-start(bf16[10,8,128]{2,1,0:T(8,128)(2,1)S(1)} %shard_map.153), channel_id=1, source_target_pairs={{0,2},{1,3},{2,4},{3,5},{4,6},{5,7},{6,8},{7,9},{8,10},{9,11},{10,... | collective-permute-start | bytes 61448 | tf_op jit(solution)/shard_map/ppermute | solution.py:502
  14.5 1.2 shard_map.154
  15.7 0.0 collective-permute-done.halo_ref
  15.7 2.7 %shard_map.155 = (bf16[256,256]{1,0:T(8,128)(2,1)S(1)}, bf16[8,256,128]{2,1,0:T(8,128)(2,1)S(1)}, bf16[8,264,128]{2,1,0:T(8,128)(2,1)}) custom-call(bf16[2,2368,128]{2,1,0:T(8,128)(2,1)S(1)} %all_to_all.30.got_ref, bf16[10,8,128]{2,1,0:T(8,128)(2,1)S(1)} %collective-permute-done.halo_ref, f32[5,1280]{1,0:T(8,128)S(1)} %get-tuple-element.44.taps_ref, ...), custom_call_target="tpu_custom_call" | custom-call | tf_op jit(solution)/shard_map/pallas_call | solution.py:44
  18.5 23.1 %all_to_all.31.got_ref = bf16[8,264,128]{2,1,0:T(8,128)(2,1)S(1)} all-to-all(bf16[8,264,128]{2,1,0:T(8,128)(2,1)} %get-tuple-element.47), channel_id=1, replica_groups={{0,2,4,6,8,10,12,14},{1,3,5,7,9,11,13,15},{16,18,20,22,24,26,28,30},{17..., dimensions={0} | all-to-all | bytes 1081344 | tf_op jit(solution)/shard_map/all_to_all | solution.py:525
  41.6 0.9 shard_map.156
  42.5 3.7 %all-to-all-start.2 = ((bf16[8,256,128]{2,1,0:T(8,128)(2,1)}), bf16[8,256,128]{2,1,0:T(8,128)(2,1)S(1)}, u32[]{:S(2)}, u32[]{:S(2)}) async-start(bf16[8,256,128]{2,1,0:T(8,128)(2,1)} %shard_map.156), calls=%async_computation.2 | async-start | bytes 1048576 | tf_op jit(solution)/shard_map/all_to_all | solution.py:541
  46.1 4.3 %shard_map.157 = (bf16[256,1024]{1,0:T(8,128)(2,1)}, bf16[256,1024]{1,0:T(8,128)(2,1)}, bf16[256,1024]{1,0:T(8,128)(2,1)}, bf16[256,1024]{1,0:T(8,128)(2,1)}, bf...) custom-call(bf16[2,2368,128]{2,1,0:T(8,128)(2,1)S(1)} %all_to_all.30.got_ref, ...), custom_call_target="tpu_custom_call" | custom-call | tf_op jit(solution)/shard_map/pallas_call | solution.py:44
  50.4 10.0 %all-to-all-done.2.states_ref = bf16[8,256,128]{2,1,0:T(8,128)(2,1)S(1)} async-done(((bf16[8,256,128]{2,1,0:T(8,128)(2,1)}), bf16[8,256,128]{2,1,0:T(8,128)(2,1)S(1)}, u32[]{:S(2)}, u32[]{:S(2)}) %all-to-all-start.2) | async-done | bytes 524320 | tf_op jit(solution)/shard_map/all_to_all | solution.py:541
  60.4 0.0 copy-start
  60.4 1.0 copy-done
  61.4 0.0 copy-start.1
  61.4 1.0 copy-done.1
  62.5 0.0 copy-start.2
  62.5 1.0 copy-done.2
  63.5 0.0 copy-start.3
  63.5 1.0 copy-done.3
  64.6 4.1 %shard_map.158 = (f32[10,272,128]{2,1,0:T(8,128)S(1)}, f32[32,128]{1,0:T(8,128)}, bf16[8,8,128]{2,1,0:T(8,128)(2,1)}) custom-call(bf16[2,2368,128]{2,1,0:T(8,128)(2,1)S(1)} %all_to_all.30.got_ref, bf16[10,8,128]{2,1,0:T(8,128)(2,1)S(1)} %collective-permute-done.halo_ref, f32[224,128]{1,0:T(8,128)S(1)} %get-tuple-element.41.rows_ref, ...), custom_call_target="tpu_custom_call" | custom-call | tf_op jit(solution)/shard_map/pallas_call | solution.py:44
  68.6 0.0 copy-start.4
  68.6 0.4 shard_map.159
  69.0 1.3 %collective-permute-start.1 = (bf16[10,8,128]{2,1,0:T(8,128)(2,1)S(1)}, bf16[10,8,128]{2,1,0:T(8,128)(2,1)S(1)}, u32[]{:S(2)}, u32[]{:S(2)}) collective-permute-start(bf16[10,8,128]{2,1,0:T(8,128)(2,1)S(1)} %get-tuple-element.59), channel_id=1, source_target_pairs={{2,0},{3,1},{4,2},{5,3},{6,4},{7,5},{8,6},{9,7},{10,8},{11,9},{12,... | collective-permute-start | bytes 61448 | tf_op jit(solution)/shard_map/ppermute | solution.py:565
  70.3 3.2 %collective-permute-done.1.back_ref = bf16[10,8,128]{2,1,0:T(8,128)(2,1)S(1)} collective-permute-done((bf16[10,8,128]{2,1,0:T(8,128)(2,1)S(1)}, bf16[10,8,128]{2,1,0:T(8,128)(2,1)S(1)}, u32[]{:S(2)}, u32[]{:S(2)}) %collective-permute-start.1) | collective-permute-done | bytes 20512 | tf_op jit(solution)/shard_map/ppermute | solution.py:565
  73.5 0.9 shard_map.160
  74.4 7.2 %collective-permute-start.2 = (bf16[11,128,128]{2,1,0:T(8,128)(2,1)S(1)}, bf16[11,128,128]{2,1,0:T(8,128)(2,1)S(1)}, u32[]{:S(2)}, u32[]{:S(2)}) collective-permute-start(bf16[11,128,128]{2,1,0:T(8,128)(2,1)S(1)} %get-tuple-element.64), channel_id=1, source_target_pairs={{0,1},{1,0},{2,3},{3,2},{4,5},{5,4},{6,7},{7,6},{8,9},{9,8},{10,11... | collective-permute-start | bytes 1081352 | tf_op jit(solution)/shard_map/ppermute | solution.py:576
  81.6 0.0 copy-done.4
  81.7 9.0 %all_to_all.32.in_ref = bf16[8,8,128]{2,1,0:T(8,128)(2,1)S(1)} all-to-all(bf16[8,8,128]{2,1,0:T(8,128)(2,1)S(1)} %copy-done.4), channel_id=1, replica_groups={{0,2,4,6,8,10,12,14},{1,3,5,7,9,11,13,15},{16,18,20,22,24,26,28,30},{17..., dimensions={0} | all-to-all | bytes 32768 | tf_op jit(solution)/shard_map/all_to_all | solution.py:555
  90.6 0.6 shard_map.162
  91.3 18.6 %all_to_all.33.in_ref = bf16[32,8,128]{2,1,0:T(8,128)(2,1)S(1)} all-to-all(bf16[32,8,128]{2,1,0:T(8,128)(2,1)} %shard_map.162), channel_id=1, replica_groups=mesh['dp'=32,'seq'=16] {'dp'}, dimensions={0} | all-to-all | bytes 131072 | tf_op jit(solution)/shard_map/all_to_all | solution.py:557
  109.9 0.7 shard_map.163
  110.6 13.3 %all_to_all.34.in_ref = bf16[16,8,128]{2,1,0:T(8,128)(2,1)S(1)} all-to-all(bf16[16,8,128]{2,1,0:T(8,128)(2,1)} %shard_map.163), channel_id=1, replica_groups=mesh['dp'=32,'seq'=16] {'seq'}, dimensions={0} | all-to-all | bytes 65536 | tf_op jit(solution)/shard_map/all_to_all | solution.py:559
  123.9 0.6 shard_map.164
  124.5 0.0 collective-permute-done.2.came_ref
  124.5 1.0 shard_map.161
  (1 shorter events, 0.0 us)
Async XLA Ops:
  13.2 2.5 %collective-permute-start = (bf16[10,8,128]{2,1,0:T(8,128)(2,1)S(1)}, bf16[10,8,128]{2,1,0:T(8,128)(2,1)S(1)}, u32[]{:S(2)}, u32[]{:S(2)}) collective-permute-start(bf16[10,8,128]{2,1,0:T(8,128)(2,1)S(1)} %shard_map.153), channel_id=1, source_target_pairs={{0,2},{1,3},{2,4},{3,5},{4,6},{5,7},{6,8},{7,9},{8,10},{9,11},{10,... | collective-permute-start | bytes 61448 | tf_op jit(solution)/shard_map/ppermute | solution.py:502
  42.5 17.9 %all-to-all-start.2 = ((bf16[8,256,128]{2,1,0:T(8,128)(2,1)}), bf16[8,256,128]{2,1,0:T(8,128)(2,1)S(1)}, u32[]{:S(2)}, u32[]{:S(2)}) async-start(bf16[8,256,128]{2,1,0:T(8,128)(2,1)} %shard_map.156), calls=%async_computation.2 | async-start | bytes 1048576 | tf_op jit(solution)/shard_map/all_to_all | solution.py:541
  60.4 1.0 copy-start
  61.4 1.0 copy-start.1
  62.5 1.0 copy-start.2
  63.5 1.0 copy-start.3
  68.6 13.0 %copy-start.4 = (bf16[8,8,128]{2,1,0:T(8,128)(2,1)S(1)}, bf16[8,8,128]{2,1,0:T(8,128)(2,1)}, u32[]{:S(2)}) copy-start(bf16[8,8,128]{2,1,0:T(8,128)(2,1)} %get-tuple-element.68) | copy-start | bytes 49156
  69.0 4.5 %collective-permute-start.1 = (bf16[10,8,128]{2,1,0:T(8,128)(2,1)S(1)}, bf16[10,8,128]{2,1,0:T(8,128)(2,1)S(1)}, u32[]{:S(2)}, u32[]{:S(2)}) collective-permute-start(bf16[10,8,128]{2,1,0:T(8,128)(2,1)S(1)} %get-tuple-element.59), channel_id=1, source_target_pairs={{2,0},{3,1},{4,2},{5,3},{6,4},{7,5},{8,6},{9,7},{10,8},{11,9},{12,... | collective-permute-start | bytes 61448 | tf_op jit(solution)/shard_map/ppermute | solution.py:565
  74.4 50.1 %collective-permute-start.2 = (bf16[11,128,128]{2,1,0:T(8,128)(2,1)S(1)}, bf16[11,128,128]{2,1,0:T(8,128)(2,1)S(1)}, u32[]{:S(2)}, u32[]{:S(2)}) collective-permute-start(bf16[11,128,128]{2,1,0:T(8,128)(2,1)S(1)} %get-tuple-element.64), channel_id=1, source_target_pairs={{0,1},{1,0},{2,3},{3,2},{4,5},{5,4},{6,7},{7,6},{8,9},{9,8},{10,11... | collective-permute-start | bytes 1081352 | tf_op jit(solution)/shard_map/ppermute | solution.py:576
